TPU v7x, 32 devices: a whole 2x2x4 slice. The times are simulated.
32 devices in a mesh: grp: 4 (over z), blk: 4 (over x, core), sub: 2 (over y).
Axes of the slice: x: 2, y: 2, z: 4, core: 2. Of those that a mesh axis runs over, the one named last changes fastest.
Arguments:
- mass_per_volume: float32 [16, 64, 512], P('blk', 'sub', 'grp'), may hold values from 0.8 to 1.2
- flow_speed_vector: float32 [3, 16, 64, 512], P(None, 'blk', 'sub', 'grp'), may hold values from -1 to 1
- normal_stress: float32 [16, 64, 512], P('blk', 'sub', 'grp'), may hold values from 0.8 to 1.2
- facing_strip_index: int32 [4, 4, 64], P('grp', 'blk', 'sub'), may hold values from 0 to 63, as said below
- solid_kelvin: float32 [32, 16, 512], P('blk', 'sub', 'grp'), may hold values from 0.5 to 1.5
- face_coupling: float32 [6, 32, 16, 512], P(None, 'blk', 'sub', 'grp'), may hold values from 0 to 2, as said below
- substance_index: int32 [32, 16, 512], P('blk', 'sub', 'grp'), may hold values from 0 to 7
- substance_storage: float32 [8], replicated, may hold values from 0.5 to 4
Outputs:
- fluid_next: float32 [5, 16, 64, 512], P(None, 'blk', 'sub', 'grp')
- metal_next: float32 [32, 16, 512], P('blk', 'sub', 'grp')
Inputs may be any that keep to these rules, and one draw needn't show every extreme that they name: `facing_strip_index`: A value v names metal device v // 8 of the blade (devices numbered over blk then sub) and strip v % 8 on it. The strips of each fluid device name exactly 4 distinct metal devices, each exactly 8 times; strips within a metal device are named with any multiplicity. `face_coupling`: channels 0 to 2 are the conductances across the lower x, y and z face of each cell, channels 3 to 5 across the upper ones; a cell's upper conductance equals the lower one of the next cell along that dimension. Conductances across the grid's ends in x and y and across multiples of 128 along z are zero, all others lie in 0.2 to 2.
All inputs are finite; a program needn't handle non-finite values.
Results may differ from a plain program's by a relative error of at most 0.0001.
Values sent between devices are 32-bit elements; how exact they have to be, the bound alone decides.
No kernel may reach another device: no remote copies, remote signals or barrier semaphores. Data moves between devices by JAX's collectives and lax.ppermute only.
A program may use at most 64 MiB of HBM per device.

v0:
```python
import jax
import jax.numpy as jnp
from jax import lax
from jax.sharding import PartitionSpec as P

ITERS = 4


gamma_gas = 1.4
time_step = 0.1
viscosity = 0.05
film_coeff = 1.0
third_part = 1.0 / 3.0
two_thirds = 2.0 / 3.0


def extended(block, sides, width, periodic):
    for axis, dim in sides:
        count = lax.axis_size(axis)
        forward = [(i, i + 1) for i in range(count - 1)]
        if periodic:
            forward.append((count - 1, 0))
        backward = [(target, source) for source, target in forward]
        low = lax.ppermute(
            lax.slice_in_dim(block, block.shape[dim] - width, None, axis=dim), axis, forward
        )
        high = lax.ppermute(lax.slice_in_dim(block, 0, width, axis=dim), axis, backward)
        block = jnp.concatenate([low, block, high], axis=dim)
    return block


def cut_faces(values, axis_id, start_at, stop_at):
    first_space = values.ndim - 3
    indexer = [slice(None)] * values.ndim
    for member in range(3):
        if member == axis_id:
            indexer[first_space + member] = slice(start_at, stop_at)
        else:
            indexer[first_space + member] = slice(1, -1)
    return values[tuple(indexer)]


def cut_along(values, axis_id, start_at, stop_at):
    indexer = [slice(None)] * values.ndim
    indexer[values.ndim - 3 + axis_id] = slice(start_at, stop_at)
    return values[tuple(indexer)]


def crop_cells(values, margin):
    return values[..., margin:-margin, margin:-margin, margin:-margin]


def advance_rate(padded, source):
    mass_per_volume = padded[0]
    flow_speed_vector = padded[1:4] / mass_per_volume
    kinetic = 0.5 * jnp.sum(padded[1:4] * flow_speed_vector, axis=0)
    normal_stress = (gamma_gas - 1.0) * (padded[4] - kinetic)
    sound_speed = jnp.sqrt(gamma_gas * normal_stress / mass_per_volume)
    interior = crop_cells(padded, 1)
    rate_sum = jnp.zeros_like(interior)
    smooth_sum = jnp.zeros_like(interior)
    for axis_id in range(3):
        along_vel = flow_speed_vector[axis_id]
        flux_dir = padded * along_vel
        flux_dir = flux_dir.at[1 + axis_id].add(normal_stress)
        flux_dir = flux_dir.at[4].add(normal_stress * along_vel)
        wave_speed = jnp.abs(along_vel) + sound_speed
        left_flux = cut_faces(flux_dir, axis_id, 0, -1)
        right_flux = cut_faces(flux_dir, axis_id, 1, None)
        left_state = cut_faces(padded, axis_id, 0, -1)
        right_state = cut_faces(padded, axis_id, 1, None)
        face_speed = jnp.maximum(
            cut_faces(wave_speed, axis_id, 0, -1), cut_faces(wave_speed, axis_id, 1, None)
        )
        face_flux = 0.5 * (left_flux + right_flux) - 0.5 * face_speed * (right_state - left_state)
        rate_sum = rate_sum - (
            cut_along(face_flux, axis_id, 1, None) - cut_along(face_flux, axis_id, 0, -1)
        )
        line_cut = cut_faces(padded, axis_id, None, None)
        smooth_sum = smooth_sum + (
            cut_along(line_cut, axis_id, 2, None)
            - 2.0 * cut_along(line_cut, axis_id, 1, -1)
            + cut_along(line_cut, axis_id, 0, -2)
        )
    weights = jnp.array([0.0, 1.0, 1.0, 1.0, 1.0], jnp.float32).reshape(5, 1, 1, 1)
    rate_sum = rate_sum + viscosity * weights * smooth_sum
    return rate_sum.at[4].add(-source)


def fluid_state(mass_per_volume, flow_speed_vector, normal_stress):
    momentum = mass_per_volume[None] * flow_speed_vector
    energy = normal_stress / (gamma_gas - 1.0) + 0.5 * jnp.sum(momentum * flow_speed_vector, axis=0)
    return jnp.concatenate([mass_per_volume[None], momentum, energy[None]], axis=0)


def section_update(section_no, base, present_iterate, source):
    fresh = crop_cells(present_iterate, 1) + time_step * advance_rate(present_iterate, source)
    if section_no == 0:
        return fresh
    if section_no == 1:
        return 0.75 * base + 0.25 * fresh
    return third_part * base + two_thirds * fresh


def metal_apply(padded, face_coupling, storage_coefficient):
    center = padded[1:-1, 1:-1, 1:-1]
    result = storage_coefficient * center
    result = (
        result
        + face_coupling[0] * (center - padded[:-2, 1:-1, 1:-1])
        + face_coupling[3] * (center - padded[2:, 1:-1, 1:-1])
    )
    result = (
        result
        + face_coupling[1] * (center - padded[1:-1, :-2, 1:-1])
        + face_coupling[4] * (center - padded[1:-1, 2:, 1:-1])
    )
    result = (
        result
        + face_coupling[2] * (center - padded[1:-1, 1:-1, :-2])
        + face_coupling[5] * (center - padded[1:-1, 1:-1, 2:])
    )
    return result


def solid_conduction_apply(field_in, face_coupling, storage_coefficient):
    padded = extended(field_in, (("blk", 0), ("sub", 1)), 1, False)
    padded = jnp.pad(padded, ((0, 0), (0, 0), (1, 1)))
    return metal_apply(padded, face_coupling, storage_coefficient)


def paired_sums(equation_misfit, image_dir):
    return lax.psum(
        (jnp.sum(equation_misfit * equation_misfit), jnp.sum(equation_misfit * image_dir)),
        ("blk", "sub"),
    )


def shards(
    mass_per_volume,
    flow_speed_vector,
    normal_stress,
    facing_strip_index,
    solid_kelvin,
    face_coupling,
    substance_index,
    substance_storage,
):
    highest = lax.Precision.HIGHEST
    fy_cells = mass_per_volume.shape[1]
    solid_across_count = solid_kelvin.shape[1]
    conserved = fluid_state(mass_per_volume, flow_speed_vector, normal_stress)
    face_temp = normal_stress[0] / mass_per_volume[0]
    surface_kelvin = solid_kelvin[0]
    routes = facing_strip_index.reshape(fy_cells)
    every_surface = lax.all_gather(surface_kelvin, ("blk", "sub"), axis=0, tiled=True)
    wall_seen = jnp.take(every_surface, routes, axis=0)
    heat_flux = film_coeff * (face_temp - wall_seen)
    columns = lax.iota(jnp.int32, solid_across_count * lax.axis_size(("blk", "sub")))
    matches = (routes[:, None] == columns[None, :]).astype(jnp.float32)
    arriving_energy = lax.psum_scatter(
        jnp.dot(matches.T, heat_flux, precision=highest),
        ("blk", "sub"),
        scatter_dimension=0,
        tiled=True,
    )
    sink = jnp.zeros_like(mass_per_volume).at[0].set(heat_flux)
    present_iterate = conserved
    for section_no in range(3):
        padded = extended(present_iterate, (("grp", 3), ("blk", 1), ("sub", 2)), 1, True)
        present_iterate = section_update(section_no, conserved, padded, sink)
    mats_count = substance_storage.shape[0]
    storage_coefficient = jnp.sum(
        jnp.where(
            substance_index[None] == lax.iota(jnp.int32, mats_count)[:, None, None, None],
            substance_storage[:, None, None, None],
            0.0,
        ),
        axis=0,
    )
    kelvin_distribution = jnp.zeros_like(solid_kelvin).at[0].set(arriving_energy)
    forcing_vector = storage_coefficient * solid_kelvin + kelvin_distribution
    converged_kelvin = solid_kelvin
    equation_misfit = forcing_vector - solid_conduction_apply(
        converged_kelvin, face_coupling, storage_coefficient
    )
    image_dir = solid_conduction_apply(equation_misfit, face_coupling, storage_coefficient)
    norm_now, product = paired_sums(equation_misfit, image_dir)
    search_factor = norm_now / product
    search_vector = equation_misfit
    along_dir = image_dir
    for step_no in range(ITERS):
        converged_kelvin = converged_kelvin + search_factor * search_vector
        equation_misfit = equation_misfit - search_factor * along_dir
        if step_no + 1 < ITERS:
            image_dir = solid_conduction_apply(equation_misfit, face_coupling, storage_coefficient)
            norm_next, product = paired_sums(equation_misfit, image_dir)
            beta_ratio = norm_next / norm_now
            search_factor = norm_next / (product - beta_ratio * norm_next / search_factor)
            search_vector = equation_misfit + beta_ratio * search_vector
            along_dir = image_dir + beta_ratio * along_dir
            norm_now = norm_next
    return (present_iterate, converged_kelvin)


def solution(mesh):
    in_specs = (
        P("blk", "sub", "grp"),
        P(None, "blk", "sub", "grp"),
        P("blk", "sub", "grp"),
        P("grp", "blk", "sub"),
        P("blk", "sub", "grp"),
        P(None, "blk", "sub", "grp"),
        P("blk", "sub", "grp"),
        P(),
    )
    out_specs = (P(None, "blk", "sub", "grp"), P("blk", "sub", "grp"))
    return jax.shard_map(shards, mesh=mesh, in_specs=in_specs, out_specs=out_specs, check_vma=False)
```

profile of v0, /device:TPU:0, one launch (start us, length us, event | category | flops | bytes accessed | tf_op | source)
XLA Modules:
  0.0 248.2 jit_solution(12696086499956093475)
XLA Ops:
  1.5 2.4 collective-permute-start.18
  3.9 1.3 collective-permute-start.19
  5.2 16.1 %all-gather = f32[1,64,128]{2,1,0:T(8,128)S(1)} all-gather(f32[1,8,128]{2,1,0:T(8,128)S(1)} %get-tuple-element.406), channel_id=2, replica_groups=mesh['grp'=4,'blk'=4,'sub'=2] {'blk','sub'}, dimensions={1}, use_global_device_ids=true | all-gather | bytes 36864 | tf_op jit(solution)/shard_map/all_gather | solution.py:156
  25.0 24.7 %all-reduce.6 = f32[64,128]{1,0:T(8,128)S(1)} all-reduce(f32[64,128]{1,0:T(8,128)S(1)} %fusion.189), channel_id=3, replica_groups=mesh['grp'=4,'blk'=4,'sub'=2] {'blk','sub'}, use_global_device_ids=true, to_apply=%region_5.6.clone | all-reduce | flops 8192 | bytes 65536
  52.4 1.3 collective-permute-start.21
  53.7 4.5 %collective-permute-start.20 = (f32[10,1,128]{2,1,0:T(1,128)S(1)}, f32[10,1,128]{2,1,0:T(1,128)S(1)}, u32[]{:S(2)}, u32[]{:S(2)}) collective-permute-start(f32[10,1,128]{2,1,0:T(1,128)S(1)} %get-tuple-element.393), channel_id=1, source_target_pairs={{0,1},{2,3},{4,5},{6,7},{8,9},{10,11},{12,13},{14,15},{16,17},{18,... | collective-permute-start | bytes 15368 | tf_op jit(solution)/shard_map/ppermute | solution.py:24
  60.8 1.3 collective-permute-start.23
  62.1 3.0 %collective-permute-start.22 = (f32[1,8,128]{2,1,0:T(8,128)S(1)}, f32[1,8,128]{2,1,0:T(8,128)S(1)}, u32[]{:S(2)}, u32[]{:S(2)}) collective-permute-start(f32[1,8,128]{2,1,0:T(8,128)S(1)} %get-tuple-element.401), channel_id=1, source_target_pairs={{0,2},{2,4},{4,6},{1,3},{3,5},{5,7},{8,10},{10,12},{12,14},{9,11},... | collective-permute-start | bytes 12296 | tf_op jit(solution)/shard_map/ppermute | solution.py:24
  67.2 4.5 %collective-permute-start.24 = (f32[10,1,128]{2,1,0:T(1,128)S(1)}, f32[10,1,128]{2,1,0:T(1,128)S(1)}, u32[]{:S(2)}, u32[]{:S(2)}) collective-permute-start(f32[10,1,128]{2,1,0:T(1,128)S(1)} %get-tuple-element.391), channel_id=1, source_target_pairs={{0,1},{2,3},{4,5},{6,7},{8,9},{10,11},{12,13},{14,15},{16,17},{18,... | collective-permute-start | bytes 15368 | tf_op jit(solution)/shard_map/ppermute | solution.py:24
  73.9 16.1 %all-reduce.10 = (f32[]{:T(128)}, f32[]{:T(128)}) all-reduce(f32[]{:T(128)} %get-tuple-element.283, f32[]{:T(128)} %get-tuple-element.282), channel_id=1, replica_groups=mesh['grp'=4,'blk'=4,'sub'=2] {'blk','sub'}, use_global_device_ids=true, to_apply=%region_7.8 | all-reduce | flops 2 | bytes 16 | tf_op jit(solution)/shard_map/psum | solution.py:133
  91.4 1.3 collective-permute-start.27
  92.7 3.0 %collective-permute-start.26 = (f32[1,8,128]{2,1,0:T(8,128)S(1)}, f32[1,8,128]{2,1,0:T(8,128)S(1)}, u32[]{:S(2)}, u32[]{:S(2)}) collective-permute-start(f32[1,8,128]{2,1,0:T(8,128)S(1)} %get-tuple-element.399), channel_id=1, source_target_pairs={{0,2},{2,4},{4,6},{1,3},{3,5},{5,7},{8,10},{10,12},{12,14},{9,11},... | collective-permute-start | bytes 12296 | tf_op jit(solution)/shard_map/ppermute | solution.py:24
  97.8 4.5 %collective-permute-start.28 = (f32[10,1,128]{2,1,0:T(1,128)S(1)}, f32[10,1,128]{2,1,0:T(1,128)S(1)}, u32[]{:S(2)}, u32[]{:S(2)}) collective-permute-start(f32[10,1,128]{2,1,0:T(1,128)S(1)} %get-tuple-element.389), channel_id=1, source_target_pairs={{0,1},{2,3},{4,5},{6,7},{8,9},{10,11},{12,13},{14,15},{16,17},{18,... | collective-permute-start | bytes 15368 | tf_op jit(solution)/shard_map/ppermute | solution.py:24
  102.5 3.7 %collective-permute-start.1 = (f32[5,4,32,1]{3,2,1,0:T(8,128)S(1)}, f32[5,4,32,1]{3,2,1,0:T(8,128)S(1)}, u32[]{:S(2)}, u32[]{:S(2)}) collective-permute-start(f32[5,4,32,1]{3,2,1,0:T(8,128)S(1)} %get-tuple-element.375), channel_id=1, source_target_pairs={{8,0},{16,8},{24,16},{0,24},{9,1},{17,9},{25,17},{1,25},{10,2},{18... | collective-permute-start | bytes 7688 | tf_op jit(solution)/shard_map/ppermute | solution.py:27
  107.1 14.5 %all-reduce.9 = (f32[]{:T(128)}, f32[]{:T(128)}) all-reduce(f32[]{:T(128)} %get-tuple-element.281, f32[]{:T(128)} %get-tuple-element.280), channel_id=1, replica_groups=mesh['grp'=4,'blk'=4,'sub'=2] {'blk','sub'}, use_global_device_ids=true, to_apply=%region_11.12 | all-reduce | flops 2 | bytes 16 | tf_op jit(solution)/shard_map/psum | solution.py:133
  126.1 1.3 collective-permute-start.31
  127.4 3.0 %collective-permute-start.30 = (f32[1,8,128]{2,1,0:T(8,128)S(1)}, f32[1,8,128]{2,1,0:T(8,128)S(1)}, u32[]{:S(2)}, u32[]{:S(2)}) collective-permute-start(f32[1,8,128]{2,1,0:T(8,128)S(1)} %get-tuple-element.397), channel_id=1, source_target_pairs={{0,2},{2,4},{4,6},{1,3},{3,5},{5,7},{8,10},{10,12},{12,14},{9,11},... | collective-permute-start | bytes 12296 | tf_op jit(solution)/shard_map/ppermute | solution.py:24
  132.6 4.5 %collective-permute-start.32 = (f32[10,1,128]{2,1,0:T(1,128)S(1)}, f32[10,1,128]{2,1,0:T(1,128)S(1)}, u32[]{:S(2)}, u32[]{:S(2)}) collective-permute-start(f32[10,1,128]{2,1,0:T(1,128)S(1)} %get-tuple-element.387), channel_id=1, source_target_pairs={{0,1},{2,3},{4,5},{6,7},{8,9},{10,11},{12,13},{14,15},{16,17},{18,... | collective-permute-start | bytes 15368 | tf_op jit(solution)/shard_map/ppermute | solution.py:24
  137.3 1.8 collective-permute-start.3
  140.0 16.1 %all-reduce.8 = (f32[]{:T(128)}, f32[]{:T(128)}) all-reduce(f32[]{:T(128)} %get-tuple-element.279, f32[]{:T(128)} %get-tuple-element.278), channel_id=1, replica_groups=mesh['grp'=4,'blk'=4,'sub'=2] {'blk','sub'}, use_global_device_ids=true, to_apply=%region_15.16 | all-reduce | flops 2 | bytes 16 | tf_op jit(solution)/shard_map/psum | solution.py:133
  161.9 3.0 %collective-permute-start.34 = (f32[1,8,128]{2,1,0:T(8,128)S(1)}, f32[1,8,128]{2,1,0:T(8,128)S(1)}, u32[]{:S(2)}, u32[]{:S(2)}) collective-permute-start(f32[1,8,128]{2,1,0:T(8,128)S(1)} %get-tuple-element.395), channel_id=1, source_target_pairs={{0,2},{2,4},{4,6},{1,3},{3,5},{5,7},{8,10},{10,12},{12,14},{9,11},... | collective-permute-start | bytes 12296 | tf_op jit(solution)/shard_map/ppermute | solution.py:24
  165.8 1.5 collective-permute-start.4
  176.2 3.0 %collective-permute-start.7 = (f32[5,4,32,1]{3,2,1,0:T(8,128)S(1)}, f32[5,4,32,1]{3,2,1,0:T(8,128)S(1)}, u32[]{:S(2)}, u32[]{:S(2)}) collective-permute-start(f32[5,4,32,1]{3,2,1,0:T(8,128)S(1)} %get-tuple-element.373), channel_id=1, source_target_pairs={{8,0},{16,8},{24,16},{0,24},{9,1},{17,9},{25,17},{1,25},{10,2},{18... | collective-permute-start | bytes 7688 | tf_op jit(solution)/shard_map/ppermute | solution.py:27
  180.5 4.5 %collective-permute-start.36 = (f32[10,1,128]{2,1,0:T(1,128)S(1)}, f32[10,1,128]{2,1,0:T(1,128)S(1)}, u32[]{:S(2)}, u32[]{:S(2)}) collective-permute-start(f32[10,1,128]{2,1,0:T(1,128)S(1)} %get-tuple-element.385), channel_id=1, source_target_pairs={{0,1},{2,3},{4,5},{6,7},{8,9},{10,11},{12,13},{14,15},{16,17},{18,... | collective-permute-start | bytes 15368 | tf_op jit(solution)/shard_map/ppermute | solution.py:24
  185.0 2.7 %collective-permute-done.6 = f32[5,4,32,1]{3,2,1,0:T(8,128)S(1)} collective-permute-done((f32[5,4,32,1]{3,2,1,0:T(8,128)S(1)}, f32[5,4,32,1]{3,2,1,0:T(8,128)S(1)}, u32[]{:S(2)}, u32[]{:S(2)}) %collective-permute-start.6) | collective-permute-done | bytes 2592 | tf_op jit(solution)/shard_map/ppermute | solution.py:24
  187.8 5.1 %collective-permute-done.7 = f32[5,4,32,1]{3,2,1,0:T(8,128)S(1)} collective-permute-done((f32[5,4,32,1]{3,2,1,0:T(8,128)S(1)}, f32[5,4,32,1]{3,2,1,0:T(8,128)S(1)}, u32[]{:S(2)}, u32[]{:S(2)}) %collective-permute-start.7) | collective-permute-done | bytes 2592 | tf_op jit(solution)/shard_map/ppermute | solution.py:27
  193.8 3.7 %collective-permute-done.9 = f32[5,1,32,130]{3,2,1,0:T(8,128)S(1)} collective-permute-done((f32[5,1,32,130]{3,2,1,0:T(8,128)S(1)}, f32[5,1,32,130]{3,2,1,0:T(8,128)S(1)}, u32[]{:S(2)}, u32[]{:S(2)}) %collective-permute-start.9) | collective-permute-done | bytes 83232 | tf_op jit(solution)/shard_map/ppermute | solution.py:27
  197.4 1.5 collective-permute-done.8
  209.0 2.8 %collective-permute-start.12 = (f32[5,4,32,1]{3,2,1,0:T(8,128)S(1)}, f32[5,4,32,1]{3,2,1,0:T(8,128)S(1)}, u32[]{:S(2)}, u32[]{:S(2)}) collective-permute-start(f32[5,4,32,1]{3,2,1,0:T(8,128)S(1)} %get-tuple-element.372), channel_id=1, source_target_pairs={{0,8},{8,16},{16,24},{24,0},{1,9},{9,17},{17,25},{25,1},{2,10},{10... | collective-permute-start | bytes 7688 | tf_op jit(solution)/shard_map/ppermute | solution.py:24
  213.5 13.6 %all-reduce.7 = (f32[]{:T(128)}, f32[]{:T(128)}) all-reduce(f32[]{:T(128)} %get-tuple-element.292, f32[]{:T(128)} %fusion.109), channel_id=1, replica_groups=mesh['grp'=4,'blk'=4,'sub'=2] {'blk','sub'}, use_global_device_ids=true, to_apply=%region_19.20 | all-reduce | flops 2 | bytes 16 | tf_op jit(solution)/shard_map/psum | solution.py:133
  232.8 3.7 %collective-permute-done.15 = f32[5,1,32,130]{3,2,1,0:T(8,128)S(1)} collective-permute-done((f32[5,1,32,130]{3,2,1,0:T(8,128)S(1)}, f32[5,1,32,130]{3,2,1,0:T(8,128)S(1)}, u32[]{:S(2)}, u32[]{:S(2)}) %collective-permute-start.15) | collective-permute-done | bytes 83232 | tf_op jit(solution)/shard_map/ppermute | solution.py:27
  236.5 1.5 collective-permute-done.14
  (172 shorter events, 56.8 us)
Async XLA Ops:
  1.5 50.1 %collective-permute-start.18 = (f32[1,8,128]{2,1,0:T(8,128)S(1)}, f32[1,8,128]{2,1,0:T(8,128)S(1)}, u32[]{:S(2)}, u32[]{:S(2)}) collective-permute-start(f32[1,8,128]{2,1,0:T(8,128)S(1)} %get-tuple-element.405), channel_id=1, source_target_pairs={{0,2},{2,4},{4,6},{1,3},{3,5},{5,7},{8,10},{10,12},{12,14},{9,11},... | collective-permute-start | bytes 12296 | tf_op jit(solution)/shard_map/ppermute | solution.py:24
  3.9 48.5 %collective-permute-start.19 = (f32[1,8,128]{2,1,0:T(8,128)S(1)}, f32[1,8,128]{2,1,0:T(8,128)S(1)}, u32[]{:S(2)}, u32[]{:S(2)}) collective-permute-start(f32[1,8,128]{2,1,0:T(8,128)S(1)} %get-tuple-element.406), channel_id=1, source_target_pairs={{2,0},{4,2},{6,4},{3,1},{5,3},{7,5},{10,8},{12,10},{14,12},{11,9},... | collective-permute-start | bytes 12296 | tf_op jit(solution)/shard_map/ppermute | solution.py:27
  52.4 5.9 %collective-permute-start.21 = (f32[10,1,128]{2,1,0:T(1,128)S(1)}, f32[10,1,128]{2,1,0:T(1,128)S(1)}, u32[]{:S(2)}, u32[]{:S(2)}) collective-permute-start(f32[10,1,128]{2,1,0:T(1,128)S(1)} %get-tuple-element.394), channel_id=1, source_target_pairs={{1,0},{3,2},{5,4},{7,6},{9,8},{11,10},{13,12},{15,14},{17,16},{19,... | collective-permute-start | bytes 15368 | tf_op jit(solution)/shard_map/ppermute | solution.py:27
  53.7 5.9 %collective-permute-start.20 = (f32[10,1,128]{2,1,0:T(1,128)S(1)}, f32[10,1,128]{2,1,0:T(1,128)S(1)}, u32[]{:S(2)}, u32[]{:S(2)}) collective-permute-start(f32[10,1,128]{2,1,0:T(1,128)S(1)} %get-tuple-element.393), channel_id=1, source_target_pairs={{0,1},{2,3},{4,5},{6,7},{8,9},{10,11},{12,13},{14,15},{16,17},{18,... | collective-permute-start | bytes 15368 | tf_op jit(solution)/shard_map/ppermute | solution.py:24
  60.8 4.4 %collective-permute-start.23 = (f32[1,8,128]{2,1,0:T(8,128)S(1)}, f32[1,8,128]{2,1,0:T(8,128)S(1)}, u32[]{:S(2)}, u32[]{:S(2)}) collective-permute-start(f32[1,8,128]{2,1,0:T(8,128)S(1)} %get-tuple-element.402), channel_id=1, source_target_pairs={{2,0},{4,2},{6,4},{3,1},{5,3},{7,5},{10,8},{12,10},{14,12},{11,9},... | collective-permute-start | bytes 12296 | tf_op jit(solution)/shard_map/ppermute | solution.py:27
  65.9 5.9 %collective-permute-start.25 = (f32[10,1,128]{2,1,0:T(1,128)S(1)}, f32[10,1,128]{2,1,0:T(1,128)S(1)}, u32[]{:S(2)}, u32[]{:S(2)}) collective-permute-start(f32[10,1,128]{2,1,0:T(1,128)S(1)} %get-tuple-element.392), channel_id=1, source_target_pairs={{1,0},{3,2},{5,4},{7,6},{9,8},{11,10},{13,12},{15,14},{17,16},{19,... | collective-permute-start | bytes 15368 | tf_op jit(solution)/shard_map/ppermute | solution.py:27
  67.2 5.9 %collective-permute-start.24 = (f32[10,1,128]{2,1,0:T(1,128)S(1)}, f32[10,1,128]{2,1,0:T(1,128)S(1)}, u32[]{:S(2)}, u32[]{:S(2)}) collective-permute-start(f32[10,1,128]{2,1,0:T(1,128)S(1)} %get-tuple-element.391), channel_id=1, source_target_pairs={{0,1},{2,3},{4,5},{6,7},{8,9},{10,11},{12,13},{14,15},{16,17},{18,... | collective-permute-start | bytes 15368 | tf_op jit(solution)/shard_map/ppermute | solution.py:24
  91.4 4.4 %collective-permute-start.27 = (f32[1,8,128]{2,1,0:T(8,128)S(1)}, f32[1,8,128]{2,1,0:T(8,128)S(1)}, u32[]{:S(2)}, u32[]{:S(2)}) collective-permute-start(f32[1,8,128]{2,1,0:T(8,128)S(1)} %get-tuple-element.400), channel_id=1, source_target_pairs={{2,0},{4,2},{6,4},{3,1},{5,3},{7,5},{10,8},{12,10},{14,12},{11,9},... | collective-permute-start | bytes 12296 | tf_op jit(solution)/shard_map/ppermute | solution.py:27
  96.5 9.7 %collective-permute-start.29 = (f32[10,1,128]{2,1,0:T(1,128)S(1)}, f32[10,1,128]{2,1,0:T(1,128)S(1)}, u32[]{:S(2)}, u32[]{:S(2)}) collective-permute-start(f32[10,1,128]{2,1,0:T(1,128)S(1)} %get-tuple-element.390), channel_id=1, source_target_pairs={{1,0},{3,2},{5,4},{7,6},{9,8},{11,10},{13,12},{15,14},{17,16},{19,... | collective-permute-start | bytes 15368 | tf_op jit(solution)/shard_map/ppermute | solution.py:27
  97.8 8.4 %collective-permute-start.28 = (f32[10,1,128]{2,1,0:T(1,128)S(1)}, f32[10,1,128]{2,1,0:T(1,128)S(1)}, u32[]{:S(2)}, u32[]{:S(2)}) collective-permute-start(f32[10,1,128]{2,1,0:T(1,128)S(1)} %get-tuple-element.389), channel_id=1, source_target_pairs={{0,1},{2,3},{4,5},{6,7},{8,9},{10,11},{12,13},{14,15},{16,17},{18,... | collective-permute-start | bytes 15368 | tf_op jit(solution)/shard_map/ppermute | solution.py:24
  102.5 34.6 %collective-permute-start.1 = (f32[5,4,32,1]{3,2,1,0:T(8,128)S(1)}, f32[5,4,32,1]{3,2,1,0:T(8,128)S(1)}, u32[]{:S(2)}, u32[]{:S(2)}) collective-permute-start(f32[5,4,32,1]{3,2,1,0:T(8,128)S(1)} %get-tuple-element.375), channel_id=1, source_target_pairs={{8,0},{16,8},{24,16},{0,24},{9,1},{17,9},{25,17},{1,25},{10,2},{18... | collective-permute-start | bytes 7688 | tf_op jit(solution)/shard_map/ppermute | solution.py:27
  106.2 30.9 %collective-permute-start = (f32[5,4,32,1]{3,2,1,0:T(8,128)S(1)}, f32[5,4,32,1]{3,2,1,0:T(8,128)S(1)}, u32[]{:S(2)}, u32[]{:S(2)}) collective-permute-start(f32[5,4,32,1]{3,2,1,0:T(8,128)S(1)} %get-tuple-element.376), channel_id=1, source_target_pairs={{0,8},{8,16},{16,24},{24,0},{1,9},{9,17},{17,25},{25,1},{2,10},{10... | collective-permute-start | bytes 7688 | tf_op jit(solution)/shard_map/ppermute | solution.py:24
  126.1 4.4 %collective-permute-start.31 = (f32[1,8,128]{2,1,0:T(8,128)S(1)}, f32[1,8,128]{2,1,0:T(8,128)S(1)}, u32[]{:S(2)}, u32[]{:S(2)}) collective-permute-start(f32[1,8,128]{2,1,0:T(8,128)S(1)} %get-tuple-element.398), channel_id=1, source_target_pairs={{2,0},{4,2},{6,4},{3,1},{5,3},{7,5},{10,8},{12,10},{14,12},{11,9},... | collective-permute-start | bytes 12296 | tf_op jit(solution)/shard_map/ppermute | solution.py:27
  131.3 7.9 %collective-permute-start.33 = (f32[10,1,128]{2,1,0:T(1,128)S(1)}, f32[10,1,128]{2,1,0:T(1,128)S(1)}, u32[]{:S(2)}, u32[]{:S(2)}) collective-permute-start(f32[10,1,128]{2,1,0:T(1,128)S(1)} %get-tuple-element.388), channel_id=1, source_target_pairs={{1,0},{3,2},{5,4},{7,6},{9,8},{11,10},{13,12},{15,14},{17,16},{19,... | collective-permute-start | bytes 15368 | tf_op jit(solution)/shard_map/ppermute | solution.py:27
  132.6 6.6 %collective-permute-start.32 = (f32[10,1,128]{2,1,0:T(1,128)S(1)}, f32[10,1,128]{2,1,0:T(1,128)S(1)}, u32[]{:S(2)}, u32[]{:S(2)}) collective-permute-start(f32[10,1,128]{2,1,0:T(1,128)S(1)} %get-tuple-element.387), channel_id=1, source_target_pairs={{0,1},{2,3},{4,5},{6,7},{8,9},{10,11},{12,13},{14,15},{16,17},{18,... | collective-permute-start | bytes 15368 | tf_op jit(solution)/shard_map/ppermute | solution.py:24
  137.3 27.6 %collective-permute-start.3 = (f32[5,1,32,130]{3,2,1,0:T(8,128)S(1)}, f32[5,1,32,130]{3,2,1,0:T(8,128)S(1)}, u32[]{:S(2)}, u32[]{:S(2)}) collective-permute-start(f32[5,1,32,130]{3,2,1,0:T(8,128)S(1)} %get-tuple-element.358), channel_id=1, source_target_pairs={{2,0},{4,2},{6,4},{0,6},{3,1},{5,3},{7,5},{1,7},{10,8},{12,10},{14... | collective-permute-start | bytes 249608 | tf_op jit(solution)/shard_map/ppermute | solution.py:27
  139.1 25.8 %collective-permute-start.2 = (f32[5,1,32,130]{3,2,1,0:T(8,128)S(1)}, f32[5,1,32,130]{3,2,1,0:T(8,128)S(1)}, u32[]{:S(2)}, u32[]{:S(2)}) collective-permute-start(f32[5,1,32,130]{3,2,1,0:T(8,128)S(1)} %get-tuple-element.357), channel_id=1, source_target_pairs={{0,2},{2,4},{4,6},{6,0},{1,3},{3,5},{5,7},{7,1},{8,10},{10,12},{12... | collective-permute-start | bytes 249608 | tf_op jit(solution)/shard_map/ppermute | solution.py:24
  160.6 18.5 %collective-permute-start.35 = (f32[1,8,128]{2,1,0:T(8,128)S(1)}, f32[1,8,128]{2,1,0:T(8,128)S(1)}, u32[]{:S(2)}, u32[]{:S(2)}) collective-permute-start(f32[1,8,128]{2,1,0:T(8,128)S(1)} %get-tuple-element.396), channel_id=1, source_target_pairs={{2,0},{4,2},{6,4},{3,1},{5,3},{7,5},{10,8},{12,10},{14,12},{11,9},... | collective-permute-start | bytes 12296 | tf_op jit(solution)/shard_map/ppermute | solution.py:27
  161.9 17.3 %collective-permute-start.34 = (f32[1,8,128]{2,1,0:T(8,128)S(1)}, f32[1,8,128]{2,1,0:T(8,128)S(1)}, u32[]{:S(2)}, u32[]{:S(2)}) collective-permute-start(f32[1,8,128]{2,1,0:T(8,128)S(1)} %get-tuple-element.395), channel_id=1, source_target_pairs={{0,2},{2,4},{4,6},{1,3},{3,5},{5,7},{8,10},{10,12},{12,14},{9,11},... | collective-permute-start | bytes 12296 | tf_op jit(solution)/shard_map/ppermute | solution.py:24
  165.8 4.1 %collective-permute-start.4 = (f32[5,6,1,130]{3,2,1,0:T(1,128)S(1)}, f32[5,6,1,130]{3,2,1,0:T(1,128)S(1)}, u32[]{:S(2)}, u32[]{:S(2)}) collective-permute-start(f32[5,6,1,130]{3,2,1,0:T(1,128)S(1)} %get-tuple-element.322), channel_id=1, source_target_pairs={{0,1},{1,0},{2,3},{3,2},{4,5},{5,4},{6,7},{7,6},{8,9},{9,8},{10,11... | collective-permute-start | bytes 46808 | tf_op jit(solution)/shard_map/ppermute | solution.py:24
  175.3 12.5 %collective-permute-start.6 = (f32[5,4,32,1]{3,2,1,0:T(8,128)S(1)}, f32[5,4,32,1]{3,2,1,0:T(8,128)S(1)}, u32[]{:S(2)}, u32[]{:S(2)}) collective-permute-start(f32[5,4,32,1]{3,2,1,0:T(8,128)S(1)} %get-tuple-element.374), channel_id=1, source_target_pairs={{0,8},{8,16},{16,24},{24,0},{1,9},{9,17},{17,25},{25,1},{2,10},{10... | collective-permute-start | bytes 7688 | tf_op jit(solution)/shard_map/ppermute | solution.py:24
  176.2 16.7 %collective-permute-start.7 = (f32[5,4,32,1]{3,2,1,0:T(8,128)S(1)}, f32[5,4,32,1]{3,2,1,0:T(8,128)S(1)}, u32[]{:S(2)}, u32[]{:S(2)}) collective-permute-start(f32[5,4,32,1]{3,2,1,0:T(8,128)S(1)} %get-tuple-element.373), channel_id=1, source_target_pairs={{8,0},{16,8},{24,16},{0,24},{9,1},{17,9},{25,17},{1,25},{10,2},{18... | collective-permute-start | bytes 7688 | tf_op jit(solution)/shard_map/ppermute | solution.py:27
  179.2 14.4 %collective-permute-start.37 = (f32[10,1,128]{2,1,0:T(1,128)S(1)}, f32[10,1,128]{2,1,0:T(1,128)S(1)}, u32[]{:S(2)}, u32[]{:S(2)}) collective-permute-start(f32[10,1,128]{2,1,0:T(1,128)S(1)} %get-tuple-element.386), channel_id=1, source_target_pairs={{1,0},{3,2},{5,4},{7,6},{9,8},{11,10},{13,12},{15,14},{17,16},{19,... | collective-permute-start | bytes 15368 | tf_op jit(solution)/shard_map/ppermute | solution.py:27
  180.5 13.1 %collective-permute-start.36 = (f32[10,1,128]{2,1,0:T(1,128)S(1)}, f32[10,1,128]{2,1,0:T(1,128)S(1)}, u32[]{:S(2)}, u32[]{:S(2)}) collective-permute-start(f32[10,1,128]{2,1,0:T(1,128)S(1)} %get-tuple-element.385), channel_id=1, source_target_pairs={{0,1},{2,3},{4,5},{6,7},{8,9},{10,11},{12,13},{14,15},{16,17},{18,... | collective-permute-start | bytes 15368 | tf_op jit(solution)/shard_map/ppermute | solution.py:24
  193.0 4.4 %collective-permute-start.9 = (f32[5,1,32,130]{3,2,1,0:T(8,128)S(1)}, f32[5,1,32,130]{3,2,1,0:T(8,128)S(1)}, u32[]{:S(2)}, u32[]{:S(2)}) collective-permute-start(f32[5,1,32,130]{3,2,1,0:T(8,128)S(1)} %get-tuple-element.349), channel_id=1, source_target_pairs={{2,0},{4,2},{6,4},{0,6},{3,1},{5,3},{7,5},{1,7},{10,8},{12,10},{14... | collective-permute-start | bytes 249608 | tf_op jit(solution)/shard_map/ppermute | solution.py:27
  193.1 5.8 %collective-permute-start.8 = (f32[5,1,32,130]{3,2,1,0:T(8,128)S(1)}, f32[5,1,32,130]{3,2,1,0:T(8,128)S(1)}, u32[]{:S(2)}, u32[]{:S(2)}) collective-permute-start(f32[5,1,32,130]{3,2,1,0:T(8,128)S(1)} %get-tuple-element.348), channel_id=1, source_target_pairs={{0,2},{2,4},{4,6},{6,0},{1,3},{3,5},{5,7},{7,1},{8,10},{10,12},{12... | collective-permute-start | bytes 249608 | tf_op jit(solution)/shard_map/ppermute | solution.py:24
  199.1 4.0 %collective-permute-start.10 = (f32[5,6,1,130]{3,2,1,0:T(1,128)S(1)}, f32[5,6,1,130]{3,2,1,0:T(1,128)S(1)}, u32[]{:S(2)}, u32[]{:S(2)}) collective-permute-start(f32[5,6,1,130]{3,2,1,0:T(1,128)S(1)} %get-tuple-element.318), channel_id=1, source_target_pairs={{0,1},{1,0},{2,3},{3,2},{4,5},{5,4},{6,7},{7,6},{8,9},{9,8},{10,11... | collective-permute-start | bytes 46808 | tf_op jit(solution)/shard_map/ppermute | solution.py:24
  209.0 22.0 %collective-permute-start.12 = (f32[5,4,32,1]{3,2,1,0:T(8,128)S(1)}, f32[5,4,32,1]{3,2,1,0:T(8,128)S(1)}, u32[]{:S(2)}, u32[]{:S(2)}) collective-permute-start(f32[5,4,32,1]{3,2,1,0:T(8,128)S(1)} %get-tuple-element.372), channel_id=1, source_target_pairs={{0,8},{8,16},{16,24},{24,0},{1,9},{9,17},{17,25},{25,1},{2,10},{10... | collective-permute-start | bytes 7688 | tf_op jit(solution)/shard_map/ppermute | solution.py:24
  211.8 19.2 %collective-permute-start.13 = (f32[5,4,32,1]{3,2,1,0:T(8,128)S(1)}, f32[5,4,32,1]{3,2,1,0:T(8,128)S(1)}, u32[]{:S(2)}, u32[]{:S(2)}) collective-permute-start(f32[5,4,32,1]{3,2,1,0:T(8,128)S(1)} %get-tuple-element.371), channel_id=1, source_target_pairs={{8,0},{16,8},{24,16},{0,24},{9,1},{17,9},{25,17},{1,25},{10,2},{18... | collective-permute-start | bytes 7688 | tf_op jit(solution)/shard_map/ppermute | solution.py:27
  231.2 5.3 %collective-permute-start.15 = (f32[5,1,32,130]{3,2,1,0:T(8,128)S(1)}, f32[5,1,32,130]{3,2,1,0:T(8,128)S(1)}, u32[]{:S(2)}, u32[]{:S(2)}) collective-permute-start(f32[5,1,32,130]{3,2,1,0:T(8,128)S(1)} %get-tuple-element.340), channel_id=1, source_target_pairs={{2,0},{4,2},{6,4},{0,6},{3,1},{5,3},{7,5},{1,7},{10,8},{12,10},{14... | collective-permute-start | bytes 249608 | tf_op jit(solution)/shard_map/ppermute | solution.py:27
  232.2 5.8 %collective-permute-start.14 = (f32[5,1,32,130]{3,2,1,0:T(8,128)S(1)}, f32[5,1,32,130]{3,2,1,0:T(8,128)S(1)}, u32[]{:S(2)}, u32[]{:S(2)}) collective-permute-start(f32[5,1,32,130]{3,2,1,0:T(8,128)S(1)} %get-tuple-element.339), channel_id=1, source_target_pairs={{0,2},{2,4},{4,6},{6,0},{1,3},{3,5},{5,7},{7,1},{8,10},{10,12},{12... | collective-permute-start | bytes 249608 | tf_op jit(solution)/shard_map/ppermute | solution.py:24
  238.2 4.0 %collective-permute-start.16 = (f32[5,6,1,130]{3,2,1,0:T(1,128)S(1)}, f32[5,6,1,130]{3,2,1,0:T(1,128)S(1)}, u32[]{:S(2)}, u32[]{:S(2)}) collective-permute-start(f32[5,6,1,130]{3,2,1,0:T(1,128)S(1)} %get-tuple-element.316), channel_id=1, source_target_pairs={{0,1},{1,0},{2,3},{3,2},{4,5},{5,4},{6,7},{7,6},{8,9},{9,8},{10,11... | collective-permute-start | bytes 46808 | tf_op jit(solution)/shard_map/ppermute | solution.py:24
  (12 other events, 319.9 us)
where the time goes:
time: 249 us; the launch traced here: 248 us
  blocking collectives  101 us (41%)
  starting transfers between devices  71.1 us (29%)
  waiting for transfers between devices  29.6 us (12%)
  other arithmetic  26.2 us (11%)
  between operations  15.9 us (6%)
  local copies, waits for them, and re-layouts  3.51 us (1%)
    psum x4, blocking collectives, paired_sums(): lax.psum((jnp.sum(equation_misfit * equation_misfit), jnp.sum(equation_mi...  60.2 us
    ppermute x19, starting transfers between devices, extended(): lax.ppermute(lax.slice_in_dim(block, block.shape[dim] - width, None, axis...  45 us
    ppermute x19, starting transfers between devices, extended(): lax.ppermute(lax.slice_in_dim(block, 0, width, axis=dim), axis, backward)  26.1 us
    unnamed x1, blocking collectives  24.7 us
    all_gather x1, blocking collectives, shards(): lax.all_gather(surface_kelvin, ('blk', 'sub'), axis=0, tiled=True)  16.1 us
    ppermute x19, waiting for transfers between devices, extended(): lax.ppermute(lax.slice_in_dim(block, 0, width, axis=dim), axis, backward)  15.8 us
    ppermute x19, waiting for transfers between devices, extended(): lax.ppermute(lax.slice_in_dim(block, block.shape[dim] - width, None, axis...  13.8 us
  transfers between devices with their start and end apart: 38, of which 17 were waited for; matrix products, arithmetic and copies ran while one was open for 7% of the time, Pallas kernels for 0%

commit v1 on v0

v1 whole, which is shorter than its diff:
```python
import functools

import jax
import jax.numpy as jnp
from jax import lax
from jax.experimental import pallas as pl
from jax.experimental.pallas import tpu as pltpu
from jax.sharding import PartitionSpec as P

ITERS = 4
HALO = 3
TILE = 8
FIELDS = 5

gamma_gas = 1.4
time_step = 0.1
viscosity = 0.05
film_coeff = 1.0
third_part = 1.0 / 3.0
two_thirds = 2.0 / 3.0

HIGHEST = lax.Precision.HIGHEST
VMEM_BYTES = 56 * 1024 * 1024


def call(body, out, inputs, smem=(), cost=100_000, scratch=(), name=None):
    in_specs = [
        pl.BlockSpec(memory_space=pltpu.SMEM if i in smem else pltpu.VMEM)
        for i in range(len(inputs))
    ]
    return pl.pallas_call(
        body,
        out_shape=out,
        in_specs=in_specs,
        out_specs=jax.tree.map(lambda _: pl.BlockSpec(memory_space=pltpu.VMEM), out),
        scratch_shapes=list(scratch),
        name=name,
        cost_estimate=pl.CostEstimate(flops=cost, bytes_accessed=cost, transcendentals=0),
        compiler_params=pltpu.CompilerParams(vmem_limit_bytes=VMEM_BYTES),
    )(*inputs)


def f32(*shape):
    return jax.ShapeDtypeStruct(shape, jnp.float32)


def up_to_tile(count):
    return -(-count // TILE) * TILE


def iota(shape, dim):
    return lax.broadcasted_iota(jnp.int32, shape, dim)


def dot(a, b, a_dim, b_dim):
    return lax.dot_general(
        a, b, (((a_dim,), (b_dim,)), ((), ())), precision=HIGHEST,
        preferred_element_type=jnp.float32,
    )


def below(ref, r, count, *at):
    start = pl.multiple_of(r - TILE, TILE)
    return ref[(*at, pl.ds(start, count + TILE))][TILE - 1:TILE - 1 + count]


def above(ref, r, count, *at):
    start = pl.multiple_of(r, TILE)
    return ref[(*at, pl.ds(start, count + TILE))][1:1 + count]


def parity():
    return lax.rem(lax.axis_index("blk"), 2)


def pack_kernel(
    rho_ref, vel_ref, pre_ref, route_ref, kelvin_ref, couple_ref, kind_ref, store_ref,
    state_ref, yedge_ref, aface_ref, bface_ref, metal_ref, wall_ref,
):
    planes, rows, lanes = rho_ref.shape
    along, across, _ = kelvin_ref.shape
    cells = along * across
    wall_ref[0:across] = kelvin_ref[0]
    wall_ref[across:across + TILE] = jnp.zeros((TILE, lanes), jnp.float32)
    wall_ref[across:across + 1, 0:rows] = route_ref[...].astype(jnp.float32)
    for x in range(planes):
        rho = rho_ref[x]
        vel = [vel_ref[d, x] for d in range(3)]
        mom = [rho * v for v in vel]
        kinetic = mom[0] * vel[0] + mom[1] * vel[1] + mom[2] * vel[2]
        energy = pre_ref[x] / (gamma_gas - 1.0) + 0.5 * kinetic
        for f, value in enumerate([rho, *mom, energy]):
            state_ref[f, x] = value
    used = FIELDS * planes * HALO
    for f in range(FIELDS):
        for x in range(planes):
            at = (f * planes + x) * HALO
            yedge_ref[0, at:at + HALO] = state_ref[f, x, 0:HALO]
            yedge_ref[1, at:at + HALO] = state_ref[f, x, rows - HALO:rows]
    if yedge_ref.shape[1] > used:
        for side in range(2):
            yedge_ref[side, used:] = jnp.zeros(
                (yedge_ref.shape[1] - used, lanes), jnp.float32
            )
    for odd in range(2):

        @pl.when(parity() == odd)
        def _():
            for f in range(FIELDS):
                for j in range(HALO):
                    aface_ref[f, j] = state_ref[f, j + (planes - HALO) * (1 - odd)]
                    bface_ref[f, j] = state_ref[f, j + (planes - HALO) * odd]

    for x in range(along):
        at = x * across
        metal_ref[at:at + across] = kelvin_ref[x]
        kind = kind_ref[x]
        capacity = jnp.zeros((across, lanes), jnp.float32)
        for m in range(store_ref.shape[0]):
            capacity = jnp.where(kind == m, store_ref[m], capacity)
        metal_ref[cells + at:cells + at + across] = capacity
        for d in range(3):
            base = (2 + d) * cells + at
            metal_ref[base:base + across] = couple_ref[d, x]
    metal_ref[5 * cells:5 * cells + rows] = pre_ref[0] / rho_ref[0]
    metal_ref[5 * cells + rows:5 * cells + rows + TILE] = wall_ref[across:across + TILE]


def edge_kernel(planes, lo_at, hi_at, starts, *refs):
    ylo_ref, yhi_ref = refs[0], refs[1]
    parts, (aedge_ref, bedge_ref) = refs[2:-2], refs[-2:]
    used = FIELDS * HALO * HALO
    span = up_to_tile(used)
    for odd in range(2):

        @pl.when(parity() == odd)
        def _():
            for out, first in (
                (aedge_ref, (planes - HALO) * (1 - odd)),
                (bedge_ref, (planes - HALO) * odd),
            ):
                for f in range(FIELDS):
                    for side, (ref, base) in enumerate(((ylo_ref, lo_at), (yhi_ref, hi_at))):
                        at = side * span + f * HALO * HALO
                        src = base + (f * planes + first) * HALO
                        out[at:at + HALO * HALO] = ref[src:src + HALO * HALO]

    for out in (aedge_ref, bedge_ref):
        for side in range(2):
            if span > used:
                out[side * span + used:(side + 1) * span] = jnp.zeros(
                    (span - used, ylo_ref.shape[1]), jnp.float32
                )
    at = 2 * span
    for ref, (start, count) in zip(parts, starts):
        bedge_ref[at:at + count] = ref[start:start + count]
        at += count


def assemble_kernel(dims, lo_at, hi_at, wall_at, *refs):
    axes, across = dims
    count_blk, count_sub = axes
    state_ref, aface_ref, bface_ref, ylo_ref, yhi_ref, aedge_ref, bedge_ref = refs[:7]
    wall_refs = refs[7:-5]
    block_ref, zlo_ref, zhi_ref, table, seen = refs[-5:]
    _, planes, rows, lanes = state_ref.shape
    stride = rows + TILE
    span = up_to_tile(FIELDS * HALO * HALO)
    each = across + TILE
    blk, sub = lax.axis_index("blk"), lax.axis_index("sub")

    def place(f, x, own, lo, hi):
        base = (x + HALO) * stride + TILE
        block_ref[f, base:base + rows] = own
        block_ref[f, base - HALO:base] = lo
        block_ref[f, base + rows:base + rows + HALO] = hi

    for f in range(FIELDS):
        for x in range(planes):
            at = (f * planes + x) * HALO
            place(
                f, x, state_ref[f, x],
                ylo_ref[lo_at + at:lo_at + at + HALO], yhi_ref[hi_at + at:hi_at + at + HALO],
            )
    for odd in range(2):

        @pl.when(parity() == odd)
        def _():
            for face_ref, edge_ref, above in (
                (aface_ref, aedge_ref, odd == 0), (bface_ref, bedge_ref, odd == 1),
            ):
                for f in range(FIELDS):
                    for j in range(HALO):
                        at = (f * HALO + j) * HALO
                        place(
                            f, planes + j if above else j - HALO, face_ref[f, j],
                            edge_ref[at:at + HALO], edge_ref[span + at:span + at + HALO],
                        )

    if wall_at is None:
        table = wall_refs[0]
    else:
        for ref, (start, flip_blk, flip_sub) in zip(wall_refs, wall_at):
            device = jnp.bitwise_xor(blk, flip_blk) * count_sub + jnp.bitwise_xor(sub, flip_sub)
            table[pl.ds(pl.multiple_of(device * each, TILE), each)] = ref[start:start + each]
    devices = count_blk * count_sub
    walls = jnp.concatenate(
        [table[d * each:d * each + across] for d in range(devices)], axis=0
    )

    def facing(blk_at, sub_at):
        device = lax.rem(blk_at, count_blk) * count_sub + lax.rem(sub_at, count_sub)
        at = pl.multiple_of(device * each + across, TILE)
        routes = table[pl.ds(at, TILE)][0:1, 0:rows].astype(jnp.int32)
        chosen = (iota((devices * across, rows), 0) == routes).astype(jnp.float32)
        return dot(chosen, walls, 0, 0)

    block_ref[FIELDS] = jnp.zeros(block_ref.shape[1:], jnp.float32)
    for x, blk_at in ((0, blk), (planes, blk + 1)):
        own = facing(blk_at, sub)
        below = facing(blk_at, sub + count_sub - 1)
        above = below if count_sub == 2 else facing(blk_at, sub + 1)
        seen[0:TILE] = jnp.zeros((TILE, lanes), jnp.float32)
        seen[TILE:TILE + rows] = own
        seen[TILE - HALO:TILE] = below[rows - HALO:rows]
        seen[TILE + rows:] = jnp.zeros((TILE, lanes), jnp.float32)
        seen[TILE + rows:TILE + rows + HALO] = above[0:HALO]
        base = (x + HALO) * stride
        rho, mx, my, mz, energy = [
            block_ref[f, base:base + stride + TILE] for f in range(FIELDS)
        ]
        pressure = (gamma_gas - 1.0) * (energy - 0.5 * (mx * mx + my * my + mz * mz) / rho)
        flux = film_coeff * (pressure / rho - seen[...])
        block_ref[FIELDS, base + TILE - HALO:base + TILE + rows + HALO] = flux[
            TILE - HALO:TILE + rows + HALO
        ]
    pick = iota((TILE, lanes), 0)
    cell = iota((TILE, lanes), 1)
    low = ((pick == cell) & (pick < HALO)).astype(jnp.float32)
    high = ((pick + lanes - HALO == cell) & (pick < HALO)).astype(jnp.float32)
    for f in range(FIELDS + 1):
        zlo_ref[f * HALO:(f + 1) * HALO] = dot(low, block_ref[f], 1, 1)[0:HALO]
        zhi_ref[f * HALO:(f + 1) * HALO] = dot(high, block_ref[f], 1, 1)[0:HALO]
    left = zlo_ref.shape[0] - (FIELDS + 1) * HALO
    if left:
        for ref in (zlo_ref, zhi_ref):
            ref[(FIELDS + 1) * HALO:] = jnp.zeros((left, ref.shape[1]), jnp.float32)


def fluid_kernel(planes, rows, block_ref, zlo_ref, zhi_ref, out_ref, base, now, prim, xface, yface, part, comb):
    total, lanes = block_ref.shape[1:]
    wide = 2 * lanes
    stride = rows + TILE
    pick = iota((TILE, lanes), 0)
    cell = iota((TILE, lanes), 1)
    spread = (
        ((pick == cell) & (pick < HALO))
        | ((pick - HALO + lanes - HALO == cell) & (pick >= HALO) & (pick < 2 * HALO))
    ).astype(jnp.float32)
    comb[2 * HALO:] = jnp.zeros((TILE - 2 * HALO, total), jnp.float32)
    for f in range(FIELDS + 1):
        comb[0:HALO] = zhi_ref[f * HALO:(f + 1) * HALO]
        comb[HALO:2 * HALO] = zlo_ref[f * HALO:(f + 1) * HALO]
        base[f, :, 0:lanes] = block_ref[f]
        base[f, :, lanes:wide] = dot(comb[...], spread, 0, 0)

    def flux(d, u, speed, pressure):
        f = [u[1 + d]] + [u[1 + i] * speed for i in range(3)] + [(u[4] + pressure) * speed]
        f[1 + d] = f[1 + d] + pressure
        return f

    def faces(d, lo_u, lo_p, hi_u, hi_p):
        lo_f = flux(d, lo_u, lo_p[d], lo_p[3])
        hi_f = flux(d, hi_u, hi_p[d], hi_p[3])
        fast = jnp.maximum(jnp.abs(lo_p[d]) + lo_p[4], jnp.abs(hi_p[d]) + hi_p[4])
        slow = fast + 2.0 * viscosity
        return [
            (lo_f[i] + hi_f[i]) - (fast if i == 0 else slow) * (hi_u[i] - lo_u[i])
            for i in range(5)
        ]

    def tiles(first, last, body, unroll=1):
        @pl.loop(first // TILE, last // TILE, unroll=unroll)
        def _(i):
            body(pl.multiple_of(i * TILE, TILE))

    for stage in range(3):
        src = base if stage == 0 else now
        margin = 2 - stage
        first = (HALO - margin) * stride
        last = (HALO + planes + margin - 1) * stride + 2 * TILE + rows
        if stage == 2:
            first, last = first + TILE, last - TILE

        def primitives(r, src=src):
            rho, mx, my, mz, energy = [src[f, pl.ds(r, TILE)] for f in range(5)]
            inverse = 1.0 / rho
            ux, uy, uz = mx * inverse, my * inverse, mz * inverse
            pressure = (gamma_gas - 1.0) * (energy - 0.5 * (mx * ux + my * uy + mz * uz))
            sound = jnp.sqrt(gamma_gas * pressure * inverse)
            for k, value in enumerate([ux, uy, uz, pressure, sound]):
                prim[k, pl.ds(r, TILE)] = value

        def load(r, src=src):
            return (
                [src[f, pl.ds(r, TILE)] for f in range(5)],
                [prim[k, pl.ds(r, TILE)] for k in range(5)],
            )

        def along_x(r):
            hi, lo = load(r), load(r - stride)
            for k, value in enumerate(faces(0, *lo, *hi)):
                xface[k, pl.ds(r, TILE)] = value

        def along_y(r, src=src):
            hi = load(r)
            lo = (
                [below(src, r, TILE, f) for f in range(5)],
                [below(prim, r, TILE, k) for k in range(5)],
            )
            for k, value in enumerate(faces(1, *lo, *hi)):
                yface[k, pl.ds(r, TILE)] = value

        def along_z(r):
            hi = load(r)
            lo = [[pltpu.roll(v, 1, axis=1) for v in vs] for vs in hi]
            for k, value in enumerate(faces(2, *lo, *hi)):
                part[k, pl.ds(r, TILE)] = pltpu.roll(value, wide - 1, axis=1) - value

        def finish(r, stage=stage, src=src):
            for k in range(5):
                here = pl.ds(r, TILE)
                rate = part[k, here]
                rate += xface[k, pl.ds(r + stride, TILE)] - xface[k, here]
                rate += above(yface, r, TILE, k) - yface[k, here]
                fresh = src[k, here] - (0.5 * time_step) * rate
                if k == 4:
                    fresh -= time_step * base[5, here]
                if stage == 1:
                    fresh = 0.75 * base[k, here] + 0.25 * fresh
                if stage == 2:
                    fresh = third_part * base[k, here] + two_thirds * fresh
                now[k, here] = fresh

        tiles(max(first - stride, 0), min(last + stride, total), primitives)
        tiles(first, last + stride, along_x)
        tiles(first, last + TILE, along_y)
        tiles(first, last, along_z)
        tiles(first, last, finish)
    for k in range(5):
        for x in range(planes):
            at = (x + HALO) * stride + TILE
            out_ref[k, x] = now[k, at:at + rows, 0:lanes]


def metal_kernel(dims, rows, order, held_ref, other_ref, out_ref, sol, res, dirn, image, diag, cx, cy, cz, czu, caps, heat):
    count_blk, count_sub, along, across = dims
    devices = count_blk * count_sub
    lanes = out_ref.shape[-1]
    cells = along * across
    wide = count_sub * across
    total = count_blk * along * wide
    pad = wide
    blk, sub = lax.axis_index("blk"), lax.axis_index("sub")
    pieces = [(held_ref, k) for k in range(held_ref.shape[0])]
    pieces += [(other_ref, k) for k in range(other_ref.shape[0])]

    zero = jnp.zeros((pad, lanes), jnp.float32)
    for ref in (dirn, cx, cy):
        ref[0:pad] = zero
        ref[pad + total:pad + total + pad] = zero

    walls = []
    for (ref, k), (flip_blk, flip_sub) in zip(pieces, order):
        b, s = jnp.bitwise_xor(blk, flip_blk), jnp.bitwise_xor(sub, flip_sub)
        for x in range(along):
            at = (b * along + x) * wide + s * across
            src = x * across
            for field, (dest, shift) in enumerate(
                ((dirn, pad), (caps, 0), (cx, pad), (cy, pad), (cz, 0))
            ):
                start = field * cells + src
                dest[pl.ds(pl.multiple_of(at + shift, TILE), across)] = ref[
                    k, start:start + across
                ]
    walls = jnp.concatenate(
        [dirn[pad + b * along * wide:pad + b * along * wide + wide] for b in range(count_blk)],
        axis=0,
    )
    heat[...] = jnp.zeros_like(heat)
    for ref, k in pieces:
        at = 5 * cells
        routes = ref[k, at + rows:at + rows + TILE][0:1, 0:rows].astype(jnp.int32)
        chosen = (iota((devices * across, rows), 0) == routes).astype(jnp.float32)
        flux = film_coeff * (ref[k, at:at + rows] - dot(chosen, walls, 0, 0))
        heat[...] += dot(chosen, flux, 1, 0)

    chunk = 32 if total % 32 == 0 else TILE
    none = jnp.zeros((chunk, lanes), jnp.float32)

    def sweep(body, init):
        return lax.fori_loop(
            0, total // chunk, lambda i, c: body(pl.multiple_of(i * chunk, TILE), c), init
        )

    def prepare(r, carry):
        here = pl.ds(r, chunk)
        own = pl.ds(r + pad, chunk)
        upper = pltpu.roll(cz[here], lanes - 1, axis=1)
        czu[here] = upper
        ups = cx[pl.ds(r + pad + wide, chunk)], above(cy, r + pad, chunk)
        links = (cx[own] + ups[0]) + (cy[own] + ups[1]) + (cz[here] + upper)
        diag[here] = caps[here] + links
        v = dirn[own]
        res[here] = -(
            cx[own] * (v - dirn[pl.ds(r + pad - wide, chunk)])
            + ups[0] * (v - dirn[pl.ds(r + pad + wide, chunk)])
            + cy[own] * (v - below(dirn, r + pad, chunk))
            + ups[1] * (v - above(dirn, r + pad, chunk))
            + cz[here] * (v - pltpu.roll(v, 1, axis=1))
            + upper * (v - pltpu.roll(v, lanes - 1, axis=1))
        )
        return carry

    sweep(prepare, 0)
    for x in range(along):
        at = pl.multiple_of((blk * along + x) * wide + sub * across + pad, TILE)
        sol[x * across:(x + 1) * across] = dirn[pl.ds(at, across)]
    for b in range(count_blk):
        at = b * along * wide
        res[at:at + wide] = res[at:at + wide] + heat[b * wide:(b + 1) * wide]

    def start(r, acc):
        here = pl.ds(r, chunk)
        dirn[pl.ds(r + pad, chunk)] = res[here]
        return acc + res[here] * res[here]

    def apply(r, acc):
        here = pl.ds(r, chunk)
        own = pl.ds(r + pad, chunk)
        v = dirn[own]
        value = (
            diag[here] * v
            - cx[own] * dirn[pl.ds(r + pad - wide, chunk)]
            - cx[pl.ds(r + pad + wide, chunk)] * dirn[pl.ds(r + pad + wide, chunk)]
            - cy[own] * below(dirn, r + pad, chunk)
            - above(cy, r + pad, chunk) * above(dirn, r + pad, chunk)
            - cz[here] * pltpu.roll(v, 1, axis=1)
            - czu[here] * pltpu.roll(v, lanes - 1, axis=1)
        )
        image[here] = value
        return acc + v * value

    norm = jnp.sum(sweep(start, none))
    for step in range(ITERS):
        alpha = norm / jnp.sum(sweep(apply, none))
        for x in range(along):
            at = pl.multiple_of((blk * along + x) * wide + sub * across + pad, TILE)
            own = slice(x * across, (x + 1) * across)
            sol[own] = sol[own] + alpha * dirn[pl.ds(at, across)]
        if step + 1 == ITERS:
            break

        def reduce(r, acc, alpha=alpha):
            here = pl.ds(r, chunk)
            value = res[here] - alpha * image[here]
            res[here] = value
            return acc + value * value

        fresh = jnp.sum(sweep(reduce, none))
        beta = fresh / norm

        def turn(r, carry, beta=beta):
            own = pl.ds(r + pad, chunk)
            dirn[own] = res[pl.ds(r, chunk)] + beta * dirn[own]
            return carry

        sweep(turn, 0)
        norm = fresh
    for x in range(along):
        out_ref[x] = sol[x * across:(x + 1) * across]


def swap(value, axis, flip):
    count = lax.axis_size(axis)
    return lax.ppermute(value, axis, [(i, i ^ flip) for i in range(count)])


def outer(value):
    count = lax.axis_size("blk")
    pairs = [(i, (i + 1 if i % 2 else i - 1) % count) for i in range(count)]
    return lax.ppermute(value, "blk", pairs)


def ring(value, axis, step):
    count = lax.axis_size(axis)
    return lax.ppermute(value, axis, [(i, (i + step) % count) for i in range(count)])


def flips(count):
    return [1 << k for k in reversed(range((count - 1).bit_length()))]


def shards(
    mass_per_volume,
    flow_speed_vector,
    normal_stress,
    facing_strip_index,
    solid_kelvin,
    face_coupling,
    substance_index,
    substance_storage,
):
    planes, rows, lanes = mass_per_volume.shape
    along, across, _ = solid_kelvin.shape
    count_blk, count_sub = lax.axis_size("blk"), lax.axis_size("sub")
    devices = count_blk * count_sub
    cells = along * across
    edge = up_to_tile(FIELDS * planes * HALO)
    each = across + TILE
    record = 5 * cells + rows + TILE

    state, yedge, aface, bface, metal, wall = call(
        pack_kernel,
        [
            f32(FIELDS, planes, rows, lanes), f32(2, edge, lanes),
            f32(FIELDS, HALO, rows, lanes), f32(FIELDS, HALO, rows, lanes),
            f32(record, lanes), f32(each, lanes),
        ],
        [
            mass_per_volume, flow_speed_vector, normal_stress,
            facing_strip_index.reshape(1, rows), solid_kelvin, face_coupling[:3],
            substance_index, substance_storage,
        ],
        smem=(7,),
        name="pack",
    )
    paired = count_blk == 4 and count_sub == 2
    span = up_to_tile(FIELDS * HALO * HALO)
    if paired:
        wall_a = swap(wall, "blk", 1)
    bface = outer(bface)
    if paired:
        ypay = jnp.concatenate([yedge.reshape(2 * edge, lanes), wall, wall_a], axis=0)
        yrecv = swap(ypay, "sub", 1)
        ylo, yhi, lo_at, hi_at = yrecv, yrecv, edge, 0
        parts = [wall, wall_a, yrecv]
        starts = [(0, each), (0, each), (2 * edge, 2 * each)]
    else:
        ylo, yhi, lo_at, hi_at = ring(yedge[1], "sub", 1), ring(yedge[0], "sub", -1), 0, 0
        parts, starts = [], []
    aface = swap(aface, "blk", 1)
    metal_b = swap(metal, "blk", flips(count_blk)[0])
    aedge, bedge = call(
        functools.partial(edge_kernel, planes, lo_at, hi_at, starts),
        [f32(2 * span, lanes), f32(2 * span + sum(c for _, c in starts), lanes)],
        [ylo, yhi, *parts],
        name="edges",
    )
    bedge = outer(bedge)
    aedge = swap(aedge, "blk", 1)
    if paired:
        walls = [wall, wall_a, yrecv, yrecv] + 4 * [bedge]
        wall_at = [(0, 0, 0), (0, 1, 0), (2 * edge, 0, 1), (2 * edge + each, 1, 1)]
        wall_at += [(2 * span + k * each, 3 ^ (k & 1), k >> 1) for k in range(4)]
    else:
        walls = [lax.all_gather(wall, ("blk", "sub"), axis=0, tiled=True)]
        wall_at = None
    total = (planes + 2 * HALO) * (rows + TILE) + 2 * TILE
    block, zlo, zhi = call(
        functools.partial(
            assemble_kernel, ((count_blk, count_sub), across), lo_at, hi_at, wall_at
        ),
        [
            f32(FIELDS + 1, total, lanes),
            f32(up_to_tile((FIELDS + 1) * HALO), total),
            f32(up_to_tile((FIELDS + 1) * HALO), total),
        ],
        [state, aface, bface, ylo, yhi, aedge, bedge, *walls],
        scratch=[
            pltpu.VMEM((devices * each, lanes), jnp.float32),
            pltpu.VMEM((rows + 2 * TILE, lanes), jnp.float32),
        ],
        name="assemble",
    )
    zlo, zhi = ring(zhi, "grp", 1), ring(zlo, "grp", -1)

    held, order = metal[None], [(0, 0)]
    steps = [("blk", flip) for flip in flips(count_blk)[:-1]]
    steps += [("sub", flip) for flip in flips(count_sub)]
    for k, (axis, flip) in enumerate(steps):
        other = metal_b[None] if k == 0 else swap(held, axis, flip)
        held = jnp.concatenate([held, other], axis=0)
        order = order + [
            (b ^ flip, s) if axis == "blk" else (b, s ^ flip) for b, s in order
        ]
    other = swap(held, "blk", 1)
    order = order + [(b ^ 1, s) for b, s in order]
    wide = count_sub * across
    cells_all = devices * cells
    metal_next = call(
        functools.partial(metal_kernel, (count_blk, count_sub, along, across), rows, order),
        f32(along, across, lanes),
        [held, other],
        scratch=[
            pltpu.VMEM((cells, lanes), jnp.float32),
            pltpu.VMEM((cells_all, lanes), jnp.float32),
            pltpu.VMEM((cells_all + 2 * wide, lanes), jnp.float32),
            pltpu.VMEM((cells_all, lanes), jnp.float32),
            pltpu.VMEM((cells_all, lanes), jnp.float32),
            pltpu.VMEM((cells_all + 2 * wide, lanes), jnp.float32),
            pltpu.VMEM((cells_all + 2 * wide, lanes), jnp.float32),
            pltpu.VMEM((cells_all, lanes), jnp.float32),
            pltpu.VMEM((cells_all, lanes), jnp.float32),
            pltpu.VMEM((cells_all, lanes), jnp.float32),
            pltpu.VMEM((devices * across, lanes), jnp.float32),
        ],
        name="metal",
    )
    big = pltpu.VMEM((FIELDS, total, 2 * lanes), jnp.float32)
    fluid_next = call(
        functools.partial(fluid_kernel, planes, rows),
        f32(FIELDS, planes, rows, lanes),
        [block, zlo, zhi],
        scratch=[
            pltpu.VMEM((FIELDS + 1, total, 2 * lanes), jnp.float32),
            big, big, big, big, big,
            pltpu.VMEM((TILE, total), jnp.float32),
        ],
        name="fluid",
    )
    return (fluid_next, metal_next)


def solution(mesh):
    in_specs = (
        P("blk", "sub", "grp"),
        P(None, "blk", "sub", "grp"),
        P("blk", "sub", "grp"),
        P("grp", "blk", "sub"),
        P("blk", "sub", "grp"),
        P(None, "blk", "sub", "grp"),
        P("blk", "sub", "grp"),
        P(),
    )
    out_specs = (P(None, "blk", "sub", "grp"), P("blk", "sub", "grp"))
    return jax.shard_map(shards, mesh=mesh, in_specs=in_specs, out_specs=out_specs, check_vma=False)
```

time: 249 us -> 92.7 us (0.37)
  blocking collectives: 101 us -> 0 us
  starting transfers between devices: 71.1 us -> 14 us
  Pallas kernels: 0 us -> 49.4 us
  other arithmetic: 26.2 us -> 1.94 us
  between operations: 15.9 us -> 0.73 us
  waiting for transfers between devices: 29.6 us -> 21.8 us
    psum x4 -> x0, blocking collectives: 60.2 us -> none  [paired_sums(): lax.psum((jnp.sum(equation_misfit * equation_misfit), jnp.sum(equation_mi...]
    ppermute x38 -> x11, starting transfers between devices: 71.1 us -> 14 us  [the longest x7 8.3 us: swap(): return lax.ppermute(value, axis, [(i, i ^ flip) for i in range(count)])]
    pallas_call x0 -> x5, Pallas kernels: none -> 49.4 us  [call(): pl.pallas_call(body, out_shape=out, in_specs=in_specs, out_specs=jax.tree...]
    unnamed x1 -> x0, blocking collectives: 24.7 us -> none
    all_gather x1 -> x0, blocking collectives: 16.1 us -> none  [shards(): lax.all_gather(surface_kelvin, ('blk', 'sub'), axis=0, tiled=True)]
    ppermute x38 -> x11, waiting for transfers between devices: 29.6 us -> 21.8 us  [the longest x7 17.1 us: swap(): return lax.ppermute(value, axis, [(i, i ^ flip) for i in range(count)])]
    sub x13 -> x0, other arithmetic: 5.53 us -> none  [the longest x9 4.44 us: advance_rate(): 0.5 * (left_flux + right_flux)]
    reduce_sum x9 -> x0, other arithmetic: 4.55 us -> none  [the longest x4 2.74 us: paired_sums(): jnp.sum(equation_misfit * image_dir)]
  transfers between devices with their start and end apart: 38 -> 11, of which waited for: 17 -> 8; matrix products, arithmetic and copies ran while one was open for 7% -> 0% of each run, Pallas kernels for 0% -> 39%
where the time goes in v1:
time: 92.7 us; the launch traced here: 92.4 us
  Pallas kernels  49.4 us (53%)
  waiting for transfers between devices  21.8 us (24%)
  starting transfers between devices  14 us (15%)
  local copies, waits for them, and re-layouts  4.48 us (5%)
  other arithmetic  1.94 us (2%)
    pallas_call x5, Pallas kernels, call(): pl.pallas_call(body, out_shape=out, in_specs=in_specs, out_specs=jax.tree...  49.4 us
    ppermute x7, waiting for transfers between devices, swap(): return lax.ppermute(value, axis, [(i, i ^ flip) for i in range(count)])  17.1 us
    ppermute x7, starting transfers between devices, swap(): return lax.ppermute(value, axis, [(i, i ^ flip) for i in range(count)])  8.3 us
    ppermute x2, starting transfers between devices, ring(): lax.ppermute(value, axis, [(i, (i + step) % count) for i in range(count)])  3.82 us
    unnamed x28, local copies, waits for them, and re-layouts  2.94 us
    ppermute x2, waiting for transfers between devices, ring(): lax.ppermute(value, axis, [(i, (i + step) % count) for i in range(count)])  2.52 us
    ppermute x2, waiting for transfers between devices, outer(): return lax.ppermute(value, 'blk', pairs)  2.27 us
    concatenate x2, other arithmetic, shards(): held = jnp.concatenate([held, other], axis=0)  1.93 us
  transfers between devices with their start and end apart: 11, of which 8 were waited for; matrix products, arithmetic and copies ran while one was open for 0% of the time, Pallas kernels for 39%

profile of v1, /device:TPU:0, one launch (start us, length us, event | category | flops | bytes accessed | tf_op | source)
XLA Modules:
  0.0 92.4 jit_solution(16901717379573032214)
XLA Ops:
  0.6 1.5 %slice.3.couple_ref = f32[3,8,8,128]{3,2,1,0:T(8,128)} slice(f32[6,8,8,128]{3,2,1,0:T(8,128)} %param.13), slice={[0:3], [0:8], [0:8], [0:128]} | slice | bytes 196608 | tf_op jit(solution)/shard_map/slice | solution.py:532
  2.2 2.1 %pack.1 = (f32[5,4,32,128]{3,2,1,0:T(8,128)}, f32[2,64,128]{2,1,0:T(8,128)}, f32[5,3,32,128]{3,2,1,0:T(8,128)}, f32[5,3,32,128]{3,2,1,0:T(8,128)}, f32[360,128]{1,0:T(8,128)}, /*index=5*/f32[16,128]{1,0:T(8,128)}) custom-call(f32[4,32,128]{2,1,0:T(8,128)} %rho_ref.1, f32[3,4,32,128]{3,2,1,0:T(8,128)} %vel_ref.1, f32[4,32,128]{2,1,0:T(8,128)} %pre_ref.1, ...), custom_call_target="tpu_custom_call" | custom-call | flops 100000 | bytes 100000 | tf_op jit(solution)/shard_map/pack/pallas_call | solution.py:31
  4.3 3.0 %collective-permute-start.8 = (f32[360,128]{1,0:T(8,128)}, f32[360,128]{1,0:T(8,128)S(1)}, u32[]{:S(2)}, u32[]{:S(2)}) collective-permute-start(f32[360,128]{1,0:T(8,128)} %get-tuple-element.23), channel_id=1, source_target_pairs={{0,4},{2,6},{4,0},{6,2},{1,5},{3,7},{5,1},{7,3},{8,12},{10,14},{12... | collective-permute-start | bytes 552968 | tf_op jit(solution)/shard_map/ppermute | solution.py:486
  7.3 4.8 %collective-permute-done.8 = f32[360,128]{1,0:T(8,128)S(1)} collective-permute-done((f32[360,128]{1,0:T(8,128)}, f32[360,128]{1,0:T(8,128)S(1)}, u32[]{:S(2)}, u32[]{:S(2)}) %collective-permute-start.8) | collective-permute-done | bytes 184352 | tf_op jit(solution)/shard_map/ppermute | solution.py:486
  12.2 0.9 %pad_maximum_fusion.1 = f32[2,360,128]{2,1,0:T(8,128)S(1)} fusion(f32[1,360,128]{2,1,0:T(8,128)S(1)} %bitcast.6, f32[1,360,128]{2,1,0:T(8,128)} %bitcast.4), kind=kLoop, calls=%fused_computation.1 | loop fusion | flops 92160 | bytes 737280 | tf_op jit(solution)/shard_map/concatenate | solution.py:593
  13.1 1.8 %collective-permute-start.9 = (f32[2,360,128]{2,1,0:T(8,128)S(1)}, f32[2,360,128]{2,1,0:T(8,128)S(1)}, u32[]{:S(2)}, u32[]{:S(2)}) collective-permute-start(f32[2,360,128]{2,1,0:T(8,128)S(1)} %pad_maximum_fusion.1), channel_id=1, source_target_pairs={{0,1},{1,0},{2,3},{3,2},{4,5},{5,4},{6,7},{7,6},{8,9},{9,8},{10,11... | collective-permute-start | bytes 1105928 | tf_op jit(solution)/shard_map/ppermute | solution.py:486
  15.0 8.0 %collective-permute-done.9 = f32[2,360,128]{2,1,0:T(8,128)S(1)} collective-permute-done((f32[2,360,128]{2,1,0:T(8,128)S(1)}, f32[2,360,128]{2,1,0:T(8,128)S(1)}, u32[]{:S(2)}, u32[]{:S(2)}) %collective-permute-start.9) | collective-permute-done | bytes 368672 | tf_op jit(solution)/shard_map/ppermute | solution.py:486
  22.9 1.0 %pad_maximum_fusion.held_ref = f32[4,360,128]{2,1,0:T(8,128)S(1)} fusion(f32[2,360,128]{2,1,0:T(8,128)S(1)} %collective-permute-done.9, f32[1,360,128]{2,1,0:T(8,128)S(1)} %bitcast.7, f32[1,360,128]{2,1,0:T(8,128)} %bitcast.5), kind=kLoop, calls=%fused_computation | loop fusion | flops 368640 | bytes 1474560 | tf_op jit(solution)/shard_map/concatenate | solution.py:593
  24.0 0.5 collective-permute-start.2
  24.6 1.5 %collective-permute-start.1 = (f32[5,3,32,128]{3,2,1,0:T(8,128)S(1)}, f32[5,3,32,128]{3,2,1,0:T(8,128)S(1)}, u32[]{:S(2)}, u32[]{:S(2)}) collective-permute-start(f32[5,3,32,128]{3,2,1,0:T(8,128)S(1)} %copy-done.12), channel_id=1, source_target_pairs={{0,6},{2,4},{4,2},{6,0},{1,7},{3,5},{5,3},{7,1},{8,14},{10,12},{12... | collective-permute-start | bytes 737288 | tf_op jit(solution)/shard_map/ppermute | solution.py:492
  26.1 0.1 collective-permute-done.2.refs_3_.refs_8_
  26.3 1.6 %collective-permute-start.3 = (f32[160,128]{1,0:T(8,128)S(1)}, f32[160,128]{1,0:T(8,128)S(1)}, u32[]{:S(2)}, u32[]{:S(2)}) collective-permute-start(f32[160,128]{1,0:T(8,128)S(1)} %pad_maximum_fusion.2), channel_id=1, source_target_pairs={{0,1},{1,0},{2,3},{3,2},{4,5},{5,4},{6,7},{7,6},{8,9},{9,8},{10,11... | collective-permute-start | bytes 245768 | tf_op jit(solution)/shard_map/ppermute | solution.py:486
  27.8 3.0 %collective-permute-done.3.refs_0_.refs_1_.refs_4_.refs_3_.refs_9_.refs_10_ = f32[160,128]{1,0:T(8,128)S(1)} collective-permute-done((f32[160,128]{1,0:T(8,128)S(1)}, f32[160,128]{1,0:T(8,128)S(1)}, u32[]{:S(2)}, u32[]{:S(2)}) %collective-permute-start.3) | collective-permute-done | bytes 81952 | tf_op jit(solution)/shard_map/ppermute | solution.py:486
  30.8 0.6 copy-done
  31.4 1.7 %edges.1 = (f32[96,128]{1,0:T(8,128)}, f32[160,128]{1,0:T(8,128)}) custom-call(f32[160,128]{1,0:T(8,128)} %copy-done, f32[160,128]{1,0:T(8,128)} %copy-done, f32[16,128]{1,0:T(8,128)} %get-tuple-element.17.refs_2_.refs_7_, f32[16,128]{1,0:T(8,128)} %copy-done.7, f32[160,128]{1,0:T(8,128)} %copy-done), custom_call_target="tpu_custom_call" | custom-call | flops 100000 | bytes 100000 | tf_op jit(solution)/shard_map/edges/pallas_call | solution.py:31
  33.1 0.3 collective-permute-start.5
  33.5 1.2 %collective-permute-start.4 = (f32[96,128]{1,0:T(8,128)}, f32[96,128]{1,0:T(8,128)S(1)}, u32[]{:S(2)}, u32[]{:S(2)}) collective-permute-start(f32[96,128]{1,0:T(8,128)} %get-tuple-element.18), channel_id=1, source_target_pairs={{0,2},{2,0},{4,6},{6,4},{1,3},{3,1},{5,7},{7,5},{8,10},{10,8},{12,... | collective-permute-start | bytes 147464 | tf_op jit(solution)/shard_map/ppermute | solution.py:486
  34.7 1.1 %collective-permute-done.4.refs_5_ = f32[96,128]{1,0:T(8,128)S(1)} collective-permute-done((f32[96,128]{1,0:T(8,128)}, f32[96,128]{1,0:T(8,128)S(1)}, u32[]{:S(2)}, u32[]{:S(2)}) %collective-permute-start.4) | collective-permute-done | bytes 49184 | tf_op jit(solution)/shard_map/ppermute | solution.py:486
  35.8 2.3 %collective-permute-done.5.refs_6_.refs_11_.refs_12_.refs_13_.refs_14_ = f32[160,128]{1,0:T(8,128)S(1)} collective-permute-done((f32[160,128]{1,0:T(8,128)}, f32[160,128]{1,0:T(8,128)S(1)}, u32[]{:S(2)}, u32[]{:S(2)}) %collective-permute-start.5) | collective-permute-done | bytes 81952 | tf_op jit(solution)/shard_map/ppermute | solution.py:492
  38.1 0.6 copy-done.2
  38.7 0.1 copy-done.4
  38.8 0.1 copy-done.5
  38.9 5.3 %assemble.1 = (f32[6,416,128]{2,1,0:T(8,128)}, f32[24,416]{1,0:T(8,128)}, f32[24,416]{1,0:T(8,128)}) custom-call(f32[5,4,32,128]{3,2,1,0:T(8,128)} %get-tuple-element.13.refs_0_, f32[5,3,32,128]{3,2,1,0:T(8,128)} %copy-done.4, f32[5,3,32,128]{3,2,1,0:T(8,128)} %copy-done.5, f32[160,128]{1,0:T(8,128)} %copy-done, f32[160,128]{1,0:T(8,128)} %copy-done, ...), custom_call_target="tpu_custom_call" | custom-call | flops 100000 | bytes 100000 | tf_op jit(solution)/shard_map/assemble/pallas_call | solution.py:31
  44.2 1.5 %collective-permute-start.6 = (f32[24,416]{1,0:T(8,128)}, f32[24,416]{1,0:T(8,128)S(1)}, u32[]{:S(2)}, u32[]{:S(2)}) collective-permute-start(f32[24,416]{1,0:T(8,128)} %get-tuple-element.21), channel_id=1, source_target_pairs={{0,8},{8,16},{16,24},{24,0},{1,9},{9,17},{17,25},{25,1},{2,10},{10... | collective-permute-start | bytes 119816 | tf_op jit(solution)/shard_map/ppermute | solution.py:497
  45.7 2.3 %collective-permute-start.7 = (f32[24,416]{1,0:T(8,128)}, f32[24,416]{1,0:T(8,128)S(1)}, u32[]{:S(2)}, u32[]{:S(2)}) collective-permute-start(f32[24,416]{1,0:T(8,128)} %get-tuple-element.22), channel_id=1, source_target_pairs={{0,24},{8,0},{16,8},{24,16},{1,25},{9,1},{17,9},{25,17},{2,26},{10... | collective-permute-start | bytes 119816 | tf_op jit(solution)/shard_map/ppermute | solution.py:497
  48.0 2.4 %collective-permute-done.6.zlo_ref = f32[24,416]{1,0:T(8,128)S(1)} collective-permute-done((f32[24,416]{1,0:T(8,128)}, f32[24,416]{1,0:T(8,128)S(1)}, u32[]{:S(2)}, u32[]{:S(2)}) %collective-permute-start.6) | collective-permute-done | bytes 39968 | tf_op jit(solution)/shard_map/ppermute | solution.py:497
  50.4 0.1 collective-permute-done.7.zhi_ref
  50.5 0.5 copy-done.10
  51.0 0.2 copy-done.11
  51.2 28.9 %fluid.1 = f32[5,4,32,128]{3,2,1,0:T(8,128)} custom-call(f32[6,416,128]{2,1,0:T(8,128)} %get-tuple-element.20.block_ref, f32[24,416]{1,0:T(8,128)} %copy-done.10, f32[24,416]{1,0:T(8,128)} %copy-done.11), custom_call_target="tpu_custom_call" | custom-call | flops 100000 | bytes 100000 | tf_op jit(solution)/shard_map/fluid/pallas_call | solution.py:31
  80.1 0.9 copy-done.3
  80.9 11.4 %metal.1 = f32[8,8,128]{2,1,0:T(8,128)} custom-call(f32[4,360,128]{2,1,0:T(8,128)} %copy-done.1, f32[4,360,128]{2,1,0:T(8,128)} %copy-done.3), custom_call_target="tpu_custom_call" | custom-call | flops 100000 | bytes 100000 | tf_op jit(solution)/shard_map/metal/pallas_call | solution.py:31
  (27 shorter events, 0.2 us)
Async XLA Ops:
  4.3 19.8 %copy-start.6 = (f32[16,128]{1,0:T(8,128)S(1)}, f32[16,128]{1,0:T(8,128)}, u32[]{:S(2)}) copy-start(f32[16,128]{1,0:T(8,128)} %get-tuple-element.17.refs_2_.refs_7_) | copy-start | bytes 24580
  4.3 20.3 %copy-start.13 = (f32[5,3,32,128]{3,2,1,0:T(8,128)S(1)}, f32[5,3,32,128]{3,2,1,0:T(8,128)}, u32[]{:S(2)}) copy-start(f32[5,3,32,128]{3,2,1,0:T(8,128)} %get-tuple-element.14) | copy-start | bytes 737284
  4.3 20.3 %copy-start.12 = (f32[5,3,32,128]{3,2,1,0:T(8,128)S(1)}, f32[5,3,32,128]{3,2,1,0:T(8,128)}, u32[]{:S(2)}) copy-start(f32[5,3,32,128]{3,2,1,0:T(8,128)} %get-tuple-element.15) | copy-start | bytes 737284
  4.3 22.0 %copy-start.8 = (f32[2,64,128]{2,1,0:T(8,128)S(1)}, f32[2,64,128]{2,1,0:T(8,128)}, u32[]{:S(2)}) copy-start(f32[2,64,128]{2,1,0:T(8,128)} %get-tuple-element.16) | copy-start | bytes 196612
  4.3 7.9 %collective-permute-start.8 = (f32[360,128]{1,0:T(8,128)}, f32[360,128]{1,0:T(8,128)S(1)}, u32[]{:S(2)}, u32[]{:S(2)}) collective-permute-start(f32[360,128]{1,0:T(8,128)} %get-tuple-element.23), channel_id=1, source_target_pairs={{0,4},{2,6},{4,0},{6,2},{1,5},{3,7},{5,1},{7,3},{8,12},{10,14},{12... | collective-permute-start | bytes 552968 | tf_op jit(solution)/shard_map/ppermute | solution.py:486
  13.1 9.8 %collective-permute-start.9 = (f32[2,360,128]{2,1,0:T(8,128)S(1)}, f32[2,360,128]{2,1,0:T(8,128)S(1)}, u32[]{:S(2)}, u32[]{:S(2)}) collective-permute-start(f32[2,360,128]{2,1,0:T(8,128)S(1)} %pad_maximum_fusion.1), channel_id=1, source_target_pairs={{0,1},{1,0},{2,3},{3,2},{4,5},{5,4},{6,7},{7,6},{8,9},{9,8},{10,11... | collective-permute-start | bytes 1105928 | tf_op jit(solution)/shard_map/ppermute | solution.py:486
  23.9 56.1 %copy-start.1 = (f32[4,360,128]{2,1,0:T(8,128)}, f32[4,360,128]{2,1,0:T(8,128)S(1)}, u32[]{:S(2)}) copy-start(f32[4,360,128]{2,1,0:T(8,128)S(1)} %pad_maximum_fusion.held_ref) | copy-start | bytes 2211844
  23.9 56.1 %collective-permute-start.10 = (f32[4,360,128]{2,1,0:T(8,128)S(1)}, f32[4,360,128]{2,1,0:T(8,128)S(1)}, u32[]{:S(2)}, u32[]{:S(2)}) collective-permute-start(f32[4,360,128]{2,1,0:T(8,128)S(1)} %pad_maximum_fusion.held_ref), channel_id=1, source_target_pairs={{0,2},{2,0},{4,6},{6,4},{1,3},{3,1},{5,7},{7,5},{8,10},{10,8},{12,... | collective-permute-start | bytes 2211848 | tf_op jit(solution)/shard_map/ppermute | solution.py:486
  24.0 2.2 %collective-permute-start.2 = (f32[16,128]{1,0:T(8,128)S(1)}, f32[16,128]{1,0:T(8,128)S(1)}, u32[]{:S(2)}, u32[]{:S(2)}) collective-permute-start(f32[16,128]{1,0:T(8,128)S(1)} %copy-done.6), channel_id=1, source_target_pairs={{0,2},{2,0},{4,6},{6,4},{1,3},{3,1},{5,7},{7,5},{8,10},{10,8},{12,... | collective-permute-start | bytes 24584 | tf_op jit(solution)/shard_map/ppermute | solution.py:486
  24.5 13.6 %collective-permute-start = (f32[5,3,32,128]{3,2,1,0:T(8,128)S(1)}, f32[5,3,32,128]{3,2,1,0:T(8,128)S(1)}, u32[]{:S(2)}, u32[]{:S(2)}) collective-permute-start(f32[5,3,32,128]{3,2,1,0:T(8,128)S(1)} %copy-done.13), channel_id=1, source_target_pairs={{0,2},{2,0},{4,6},{6,4},{1,3},{3,1},{5,7},{7,5},{8,10},{10,8},{12,... | collective-permute-start | bytes 737288 | tf_op jit(solution)/shard_map/ppermute | solution.py:486
  24.6 13.5 %collective-permute-start.1 = (f32[5,3,32,128]{3,2,1,0:T(8,128)S(1)}, f32[5,3,32,128]{3,2,1,0:T(8,128)S(1)}, u32[]{:S(2)}, u32[]{:S(2)}) collective-permute-start(f32[5,3,32,128]{3,2,1,0:T(8,128)S(1)} %copy-done.12), channel_id=1, source_target_pairs={{0,6},{2,4},{4,2},{6,0},{1,7},{3,5},{5,3},{7,1},{8,14},{10,12},{12... | collective-permute-start | bytes 737288 | tf_op jit(solution)/shard_map/ppermute | solution.py:492
  26.2 4.6 %copy-start.7 = (f32[16,128]{1,0:T(8,128)}, f32[16,128]{1,0:T(8,128)S(1)}, u32[]{:S(2)}) copy-start(f32[16,128]{1,0:T(8,128)S(1)} %collective-permute-done.2.refs_3_.refs_8_) | copy-start | bytes 24580
  26.3 4.6 %collective-permute-start.3 = (f32[160,128]{1,0:T(8,128)S(1)}, f32[160,128]{1,0:T(8,128)S(1)}, u32[]{:S(2)}, u32[]{:S(2)}) collective-permute-start(f32[160,128]{1,0:T(8,128)S(1)} %pad_maximum_fusion.2), channel_id=1, source_target_pairs={{0,1},{1,0},{2,3},{3,2},{4,5},{5,4},{6,7},{7,6},{8,9},{9,8},{10,11... | collective-permute-start | bytes 245768 | tf_op jit(solution)/shard_map/ppermute | solution.py:486
  30.8 0.6 copy-start
  33.1 4.9 %collective-permute-start.5 = (f32[160,128]{1,0:T(8,128)}, f32[160,128]{1,0:T(8,128)S(1)}, u32[]{:S(2)}, u32[]{:S(2)}) collective-permute-start(f32[160,128]{1,0:T(8,128)} %get-tuple-element.19), channel_id=1, source_target_pairs={{0,6},{2,4},{4,2},{6,0},{1,7},{3,5},{5,3},{7,1},{8,14},{10,12},{12... | collective-permute-start | bytes 245768 | tf_op jit(solution)/shard_map/ppermute | solution.py:492
  33.5 2.3 %collective-permute-start.4 = (f32[96,128]{1,0:T(8,128)}, f32[96,128]{1,0:T(8,128)S(1)}, u32[]{:S(2)}, u32[]{:S(2)}) collective-permute-start(f32[96,128]{1,0:T(8,128)} %get-tuple-element.18), channel_id=1, source_target_pairs={{0,2},{2,0},{4,6},{6,4},{1,3},{3,1},{5,7},{7,5},{8,10},{10,8},{12,... | collective-permute-start | bytes 147464 | tf_op jit(solution)/shard_map/ppermute | solution.py:486
  35.8 2.3 %copy-start.9 = (f32[96,128]{1,0:T(8,128)}, f32[96,128]{1,0:T(8,128)S(1)}, u32[]{:S(2)}) copy-start(f32[96,128]{1,0:T(8,128)S(1)} %collective-permute-done.4.refs_5_) | copy-start | bytes 147460
  38.1 0.6 copy-start.2
  38.1 0.7 copy-start.4
  38.1 0.8 copy-start.5
  44.2 6.2 %collective-permute-start.6 = (f32[24,416]{1,0:T(8,128)}, f32[24,416]{1,0:T(8,128)S(1)}, u32[]{:S(2)}, u32[]{:S(2)}) collective-permute-start(f32[24,416]{1,0:T(8,128)} %get-tuple-element.21), channel_id=1, source_target_pairs={{0,8},{8,16},{16,24},{24,0},{1,9},{9,17},{17,25},{25,1},{2,10},{10... | collective-permute-start | bytes 119816 | tf_op jit(solution)/shard_map/ppermute | solution.py:497
  45.7 4.8 %collective-permute-start.7 = (f32[24,416]{1,0:T(8,128)}, f32[24,416]{1,0:T(8,128)S(1)}, u32[]{:S(2)}, u32[]{:S(2)}) collective-permute-start(f32[24,416]{1,0:T(8,128)} %get-tuple-element.22), channel_id=1, source_target_pairs={{0,24},{8,0},{16,8},{24,16},{1,25},{9,1},{17,9},{25,17},{2,26},{10... | collective-permute-start | bytes 119816 | tf_op jit(solution)/shard_map/ppermute | solution.py:497
  50.4 0.6 copy-start.10
  50.5 0.6 copy-start.11
  80.1 0.9 copy-start.3

commit v2 on v1

v2 whole, which is shorter than its diff:
```python
import functools
import math

import jax
import jax.numpy as jnp
from jax import lax
from jax.experimental import pallas as pl
from jax.experimental.pallas import tpu as pltpu
from jax.sharding import PartitionSpec as P


ITERS = 4
HALO = 3
TILE = 8
FIELDS = 5

gamma_gas = 1.4
time_step = 0.1
viscosity = 0.05
film_coeff = 1.0
third_part = 1.0 / 3.0
two_thirds = 2.0 / 3.0

HIGHEST = lax.Precision.HIGHEST
SPARE_BYTES = 6 * 1024 * 1024


def bytes_of(shapes):
    total = 0
    for shape in shapes:
        *lead, rows, lanes = (1, 1, *shape)
        total += 4 * math.prod(lead) * up_to_tile(rows) * (-(-lanes // 128) * 128)
    return total


def call(body, out, inputs, hbm=(), cost=100_000, scratch=()):
    inputs = [
        pltpu.with_memory_space_constraint(x, pltpu.HBM) if i in hbm else x
        for i, x in enumerate(inputs)
    ]
    limit = SPARE_BYTES + bytes_of(
        [x.shape for i, x in enumerate(inputs) if i not in hbm]
        + [x.shape for x in jax.tree.leaves(out)]
        + [x for x in scratch if isinstance(x, tuple)]
    )
    return pl.pallas_call(
        body,
        out_shape=out,
        in_specs=[
            pl.BlockSpec(memory_space=pltpu.HBM if i in hbm else pltpu.VMEM)
            for i in range(len(inputs))
        ],
        out_specs=jax.tree.map(lambda _: pl.BlockSpec(memory_space=pltpu.VMEM), out),
        scratch_shapes=[
            pltpu.VMEM(x, jnp.float32) if isinstance(x, tuple) else x for x in scratch
        ],
        cost_estimate=pl.CostEstimate(flops=cost, bytes_accessed=cost, transcendentals=0),
        compiler_params=pltpu.CompilerParams(vmem_limit_bytes=limit),
    )(*inputs)


def f32(*shape):
    return jax.ShapeDtypeStruct(shape, jnp.float32)


def up_to_tile(count):
    return -(-count // TILE) * TILE


def iota(shape, dim):
    return lax.broadcasted_iota(jnp.int32, shape, dim)


def dot(a, b, a_dim, b_dim):
    return lax.dot_general(
        a, b, (((a_dim,), (b_dim,)), ((), ())), precision=HIGHEST,
        preferred_element_type=jnp.float32,
    )


def parity():
    return lax.rem(lax.axis_index("blk"), 2)


def pack_kernel(
    rho_hbm, vel_hbm, pre_hbm, route_hbm, kelvin_hbm, couple_hbm, kind_hbm, store_hbm,
    state_ref, yedge_ref, apay_ref, bpay_ref, metal_ref, wall_ref,
    rho_ref, vel_ref, pre_ref, route_ref, kind_ref, store_ref, arrived,
):
    planes, rows, lanes = rho_ref.shape
    cells = kind_ref.shape[0]
    across = wall_ref.shape[0] - TILE
    face = FIELDS * HALO * rows
    copies = [
        pltpu.make_async_copy(src, dst, arrived.at[k])
        for k, (src, dst) in enumerate((
            (rho_hbm, rho_ref), (vel_hbm, vel_ref), (pre_hbm, pre_ref),
            (kelvin_hbm, metal_ref.at[0:cells]),
            (couple_hbm.at[0:3 * cells], metal_ref.at[2 * cells:5 * cells]),
            (kind_hbm, kind_ref), (store_hbm, store_ref), (route_hbm, route_ref),
        ))
    ]
    for copy in copies:
        copy.start()
    for copy in copies[:3]:
        copy.wait()
    for x in range(planes):
        rho = rho_ref[x]
        vel = [vel_ref[d, x] for d in range(3)]
        mom = [rho * v for v in vel]
        kinetic = mom[0] * vel[0] + mom[1] * vel[1] + mom[2] * vel[2]
        energy = pre_ref[x] / (gamma_gas - 1.0) + 0.5 * kinetic
        for f, value in enumerate([rho, *mom, energy]):
            state_ref[f, x] = value
    used = FIELDS * planes * HALO
    for f in range(FIELDS):
        for x in range(planes):
            at = (f * planes + x) * HALO
            yedge_ref[0, at:at + HALO] = state_ref[f, x, 0:HALO]
            yedge_ref[1, at:at + HALO] = state_ref[f, x, rows - HALO:rows]
    if yedge_ref.shape[1] > used:
        for side in range(2):
            yedge_ref[side, used:] = jnp.zeros(
                (yedge_ref.shape[1] - used, lanes), jnp.float32
            )
    for odd in range(2):

        @pl.when(parity() == odd)
        def _():
            for f in range(FIELDS):
                for j in range(HALO):
                    at = (f * HALO + j) * rows
                    apay_ref[at:at + rows] = state_ref[f, j + (planes - HALO) * (1 - odd)]
                    bpay_ref[at:at + rows] = state_ref[f, j + (planes - HALO) * odd]

    for copy in copies[3:]:
        copy.wait()
    wall_ref[0:across] = metal_ref[0:across]
    wall_ref[across:across + TILE] = jnp.zeros((TILE, lanes), jnp.float32)
    wall_ref[across:across + 1, 0:rows] = route_ref[...].astype(jnp.float32)
    kind = kind_ref[...]
    capacity = jnp.zeros((cells, lanes), jnp.float32)
    for m in range(store_ref.shape[0]):
        capacity = jnp.where(kind == m, store_ref[m], capacity)
    metal_ref[cells:2 * cells] = capacity
    metal_ref[5 * cells:5 * cells + rows] = pre_ref[0] / rho_ref[0]
    metal_ref[5 * cells + rows:5 * cells + rows + TILE] = wall_ref[across:across + TILE]
    record = 5 * cells + rows + TILE
    apay_ref[face:face + record] = metal_ref[...]
    bpay_ref[face:face + record] = metal_ref[...]


def edge_kernel(planes, lo_at, hi_at, starts, *refs):
    ylo_ref, yhi_ref = refs[0], refs[1]
    parts, (aedge_ref, bedge_ref) = refs[2:-2], refs[-2:]
    used = FIELDS * HALO * HALO
    span = up_to_tile(used)
    for odd in range(2):

        @pl.when(parity() == odd)
        def _():
            for out, first in (
                (aedge_ref, (planes - HALO) * (1 - odd)),
                (bedge_ref, (planes - HALO) * odd),
            ):
                for f in range(FIELDS):
                    for side, (ref, base) in enumerate(((ylo_ref, lo_at), (yhi_ref, hi_at))):
                        at = side * span + f * HALO * HALO
                        src = base + (f * planes + first) * HALO
                        out[at:at + HALO * HALO] = ref[src:src + HALO * HALO]

    for out in (aedge_ref, bedge_ref):
        for side in range(2):
            if span > used:
                out[side * span + used:(side + 1) * span] = jnp.zeros(
                    (span - used, ylo_ref.shape[1]), jnp.float32
                )
    at = 2 * span
    for ref, (start, count) in zip(parts, starts):
        bedge_ref[at:at + count] = ref[start:start + count]
        at += count


def assemble_kernel(dims, lo_at, hi_at, wall_at, *refs):
    axes, across = dims
    count_blk, count_sub = axes
    state_ref, aface_ref, bface_ref, ylo_ref, yhi_ref, aedge_ref, bedge_ref = refs[:7]
    wall_refs = refs[7:-5]
    block_ref, zlo_ref, zhi_ref, table, seen = refs[-5:]
    _, planes, rows, lanes = state_ref.shape
    deep, stride = block_ref.shape[1:3]
    span = up_to_tile(FIELDS * HALO * HALO)
    each = across + TILE
    blk, sub = lax.axis_index("blk"), lax.axis_index("sub")

    def place(f, x, own, lo, hi):
        block_ref[f, x + HALO, 0:rows] = own
        block_ref[f, x + HALO, rows:rows + HALO] = hi
        block_ref[f, x + HALO, stride - HALO:stride] = lo

    for f in range(FIELDS):
        for x in range(planes):
            at = (f * planes + x) * HALO
            place(
                f, x, state_ref[f, x],
                ylo_ref[lo_at + at:lo_at + at + HALO], yhi_ref[hi_at + at:hi_at + at + HALO],
            )
    for odd in range(2):

        @pl.when(parity() == odd)
        def _():
            for face_ref, edge_ref, above in (
                (aface_ref, aedge_ref, odd == 0), (bface_ref, bedge_ref, odd == 1),
            ):
                for f in range(FIELDS):
                    for j in range(HALO):
                        at = (f * HALO + j) * HALO
                        place(
                            f, planes + j if above else j - HALO,
                            face_ref[(f * HALO + j) * rows:(f * HALO + j + 1) * rows],
                            edge_ref[at:at + HALO], edge_ref[span + at:span + at + HALO],
                        )

    if wall_at is None:
        table = wall_refs[0]
    else:
        for ref, (start, flip_blk, flip_sub) in zip(wall_refs, wall_at):
            device = jnp.bitwise_xor(blk, flip_blk) * count_sub + jnp.bitwise_xor(sub, flip_sub)
            table[pl.ds(pl.multiple_of(device * each, TILE), each)] = ref[start:start + each]
    devices = count_blk * count_sub
    walls = jnp.concatenate(
        [table[d * each:d * each + across] for d in range(devices)], axis=0
    )

    def facing(blk_at, sub_at):
        device = lax.rem(blk_at, count_blk) * count_sub + lax.rem(sub_at, count_sub)
        at = pl.multiple_of(device * each + across, TILE)
        routes = table[pl.ds(at, TILE)][0:1, 0:rows].astype(jnp.int32)
        chosen = (iota((devices * across, rows), 0) == routes).astype(jnp.float32)
        return dot(chosen, walls, 0, 0)

    block_ref[FIELDS] = jnp.zeros(block_ref.shape[1:], jnp.float32)
    for x, blk_at in ((0, blk), (planes, blk + 1)):
        below = facing(blk_at, sub + count_sub - 1)
        above = below if count_sub == 2 else facing(blk_at, sub + 1)
        seen[0:rows] = facing(blk_at, sub)
        seen[rows:] = jnp.zeros((stride - rows, lanes), jnp.float32)
        seen[rows:rows + HALO] = above[0:HALO]
        seen[stride - HALO:stride] = below[rows - HALO:rows]
        rho, mx, my, mz, energy = [block_ref[f, x + HALO] for f in range(FIELDS)]
        pressure = (gamma_gas - 1.0) * (energy - 0.5 * (mx * mx + my * my + mz * mz) / rho)
        block_ref[FIELDS, x + HALO] = film_coeff * (pressure / rho - seen[...])
    pick = iota((TILE, lanes), 0)
    cell = iota((TILE, lanes), 1)
    chosen = (
        ((pick == cell) & (pick < HALO))
        | ((pick - HALO + lanes - HALO == cell) & (pick >= HALO) & (pick < 2 * HALO))
    ).astype(jnp.float32)
    size = deep * stride
    for f in range(FIELDS + 1):
        ends = dot(chosen, block_ref[f].reshape(size, lanes), 1, 1)
        zlo_ref[f * HALO:(f + 1) * HALO, 0:size] = ends[0:HALO]
        zhi_ref[f * HALO:(f + 1) * HALO, 0:size] = ends[HALO:2 * HALO]
    used = (FIELDS + 1) * HALO
    for ref in (zlo_ref, zhi_ref):
        if ref.shape[1] > size:
            ref[:, size:] = jnp.zeros((ref.shape[0], ref.shape[1] - size), jnp.float32)
        if ref.shape[0] > used:
            ref[used:] = jnp.zeros((ref.shape[0] - used, ref.shape[1]), jnp.float32)


def primitives(u):
    rho, mx, my, mz, energy = u
    inverse = 1.0 / rho
    ux, uy, uz = mx * inverse, my * inverse, mz * inverse
    pressure = (gamma_gas - 1.0) * (energy - 0.5 * (mx * ux + my * uy + mz * uz))
    sound = jnp.sqrt(gamma_gas * pressure * inverse)
    return [
        ux, uy, uz, jnp.abs(ux) + sound, jnp.abs(uy) + sound, jnp.abs(uz) + sound,
        pressure, energy + pressure,
    ]


def faces(d, lo, hi):
    def flux(v):
        speed, pressure, enthalpy = v[5], v[7], v[8]
        f = [v[1 + d]] + [v[1 + i] * speed for i in range(3)] + [enthalpy * speed]
        f[1 + d] = f[1 + d] + pressure
        return f

    below, here = flux(lo), flux(hi)
    fast = jnp.maximum(lo[6], hi[6])
    slow = fast + 2.0 * viscosity
    return [
        (below[i] + here[i]) - (fast if i == 0 else slow) * (hi[i] - lo[i]) for i in range(5)
    ]


def fluid_kernel(
    block_ref, above_ref, below_ref, low_ref, high_ref, out_ref,
    now, prim, xface, ends, slab_base, slab, comb,
):
    _, planes, rows, lanes = out_ref.shape
    deep, stride = block_ref.shape[1:3]
    size = deep * stride
    wide = slab.shape[2]
    group = TILE
    part = FIELDS * TILE
    source = iota((lanes, FIELDS * lanes), 0)
    target = iota((lanes, FIELDS * lanes), 1)
    field = lax.rem(source, part) // TILE
    end = lax.rem(source, TILE)
    spread = (
        ((end == 0) & (target == field * lanes))
        | ((end == 1) & (target == field * lanes + lanes - 1))
    ) & (source < 3 * part)
    spread = spread.astype(jnp.float32).astype(jnp.bfloat16)
    comb[...] = jnp.zeros(comb.shape, jnp.float32)
    slab_base[...] = jnp.zeros(slab_base.shape, jnp.float32)
    for f in range(FIELDS + 1):
        at = slice(f * HALO, (f + 1) * HALO)
        slab_base[f, 0:HALO] = below_ref[at]
        slab_base[f, HALO:2 * HALO] = low_ref[at]
        slab_base[f, group:group + HALO] = high_ref[at]
        slab_base[f, group + HALO:group + 2 * HALO] = above_ref[at]
    for f in range(FIELDS):
        slab[f] = slab_base[f]

    @pl.loop(0, deep)
    def _(x):
        for f in range(FIELDS):
            now[f, x] = block_ref[f, x]

    first_row = lax.rem(iota((2 * TILE, wide), 1), stride) == 0
    last_row = lax.rem(iota((2 * TILE, wide), 1), stride) == stride - 1

    def lane_roll(v, shift):
        return pltpu.roll(v, shift % wide, axis=1)

    def advance(old, change, start, sink, a, b):
        fresh = old - (0.5 * time_step) * change
        if sink is not None:
            fresh = fresh - time_step * sink
        return a * start + b * fresh

    lane = iota((stride, lanes), 1)

    @pl.loop(0, 3)
    def _(stage):
        a = jnp.where(stage == 0, 0.0, jnp.where(stage == 1, 0.75, third_part))
        b = jnp.where(stage == 0, 1.0, jnp.where(stage == 1, 0.25, two_thirds))

        u = [slab[f] for f in range(FIELDS)]
        q = primitives(u)
        hi = u + [q[2], q[5], q[6], q[7]]
        lo = [pltpu.roll(v, 1, axis=0) for v in hi]
        zface = faces(2, lo, hi)
        for f in range(FIELDS):
            comb[f * TILE:f * TILE + 1] = zface[f][HALO:HALO + 1]
            comb[f * TILE + 1:f * TILE + 2] = zface[f][group + HALO:group + HALO + 1]
        change = [pltpu.roll(v, 2 * TILE - 1, axis=0) - v for v in zface]
        hi = u + [q[0], q[3], q[6], q[7]]
        face = faces(0, [lane_roll(v, stride) for v in hi], hi)
        change = [c + (lane_roll(v, -stride) - v) for c, v in zip(change, face)]
        hi = u + [q[1], q[4], q[6], q[7]]
        lo = [
            jnp.where(first_row, lane_roll(v, 1 - stride), lane_roll(v, 1)) for v in hi
        ]
        face = faces(1, lo, hi)
        change = [
            c + (jnp.where(last_row, lane_roll(v, stride - 1), lane_roll(v, -1)) - v)
            for c, v in zip(change, face)
        ]
        for f in range(FIELDS):
            sink = slab_base[FIELDS] if f == FIELDS - 1 else None
            slab[f] = advance(u[f], change[f], slab_base[f], sink, a, b)
        whole = comb[0:part]
        for k in range(2):
            piece = whole.astype(jnp.bfloat16).astype(jnp.float32)
            comb[k * part:(k + 1) * part] = piece
            whole = whole - piece
        comb[2 * part:3 * part] = whole
        turned = jnp.transpose(comb[...]).astype(jnp.bfloat16)
        moved = lax.dot_general(
            turned, spread, (((1,), (0,)), ((), ())), preferred_element_type=jnp.float32
        )
        for f in range(FIELDS):
            ends[f] = moved[0:size, f * lanes:(f + 1) * lanes].reshape(deep, stride, lanes)

        low = stage + 1
        high = deep - 1 - stage

        @pl.loop(low - 1, high + 1)
        def _(x):
            for k, value in enumerate(primitives([now[f, x] for f in range(FIELDS)])):
                prim[k, x] = value

        def cells(x, d):
            return [now[f, x] for f in range(FIELDS)] + [
                prim[d, x], prim[3 + d, x], prim[6, x], prim[7, x]
            ]

        @pl.loop(low, high + 1)
        def _(x):
            new = faces(0, cells(x - 1, 0), cells(x, 0))
            old = lax.rem(x, 2)
            for f in range(FIELDS):
                xface[old, f] = new[f]

            @pl.when(x > low)
            def _():
                p = x - 1
                change = [new[f] - xface[1 - old, f] for f in range(FIELDS)]
                hi = cells(p, 1)
                lo = [pltpu.roll(v, 1, axis=0) for v in hi]
                face = faces(1, lo, hi)
                change = [
                    c + (pltpu.roll(v, stride - 1, axis=0) - v) for c, v in zip(change, face)
                ]
                hi = cells(p, 2)
                lo = [pltpu.roll(v, 1, axis=1) for v in hi]
                face = faces(2, lo, hi)
                for f in range(FIELDS):
                    end = ends[f, p]
                    top = jnp.where(lane == lanes - 1, end, pltpu.roll(face[f], lanes - 1, axis=1))
                    low_face = jnp.where(lane == 0, end, face[f])
                    sink = block_ref[FIELDS, p] if f == FIELDS - 1 else None
                    now[f, p] = advance(
                        now[f, p], change[f] + (top - low_face), block_ref[f, p], sink, a, b
                    )

    for f in range(FIELDS):
        for x in range(planes):
            out_ref[f, x] = now[f, x + HALO, 0:rows]


def metal_kernel(dims, rows, where, order, *refs):
    count_blk, count_sub, along, across = dims
    devices = count_blk * count_sub
    pieces = [(refs[k], start) for k, start in where]
    (
        out_ref, sol, res, dirn, image, diag, cx, cy, cz, cyu, czu, caps, heat, route, faced,
    ) = refs[-15:]
    lanes = out_ref.shape[-1]
    cells = along * across
    wide = count_sub * across
    deep = count_blk * along
    blk, sub = lax.axis_index("blk"), lax.axis_index("sub")
    mine = blk * along
    side = pl.multiple_of(sub * across, TILE)

    zero = jnp.zeros((wide, lanes), jnp.float32)
    for ref in (dirn, cx):
        ref[0] = zero
        ref[deep + 1] = zero

    for n, ((ref, first), (flip_blk, flip_sub)) in enumerate(zip(pieces, order)):
        b = jnp.bitwise_xor(blk, flip_blk) * along
        y = pl.multiple_of(jnp.bitwise_xor(sub, flip_sub) * across, TILE)
        for field, (dest, shift) in enumerate(((dirn, 1), (caps, 0), (cx, 1), (cy, 0), (cz, 0))):
            start = first + field * cells
            dest[pl.ds(b + shift, along), pl.ds(y, across)] = ref[
                start:start + cells
            ].reshape(along, across, lanes)
        start = first + 5 * cells
        faced[n * rows:(n + 1) * rows] = ref[start:start + rows]
        route[:, n * rows:(n + 1) * rows] = ref[start + rows:start + rows + TILE][:, 0:rows]

    walls = jnp.concatenate([dirn[1 + b * along] for b in range(count_blk)], axis=0)
    strips = devices * across
    chosen = (
        iota((strips, devices * rows), 0) == route[0:1].astype(jnp.int32)
    ).astype(jnp.float32)
    flux = film_coeff * (faced[...] - dot(chosen, walls, 0, 0))
    heat[...] = dot(chosen, flux, 1, 0)

    chunk = 4 if deep % 4 == 0 else 1
    none = jnp.zeros((TILE, lanes), jnp.float32)

    def sweep(body, init):
        return lax.fori_loop(0, deep // chunk, lambda i, c: body(i * chunk, c), init)

    def fold(value):
        return jnp.sum(value.reshape(-1, TILE, lanes), axis=0)

    def turned(v, step, axis):
        return pltpu.roll(v, step % v.shape[axis], axis=axis)

    def prepare(x, carry):
        here, own = pl.ds(x, chunk), pl.ds(x + 1, chunk)
        ups = cx[pl.ds(x + 2, chunk)], turned(cy[here], -1, 1), turned(cz[here], -1, 2)
        cyu[here] = ups[1]
        czu[here] = ups[2]
        diag[here] = caps[here] + ((cx[own] + ups[0]) + (cy[here] + ups[1]) + (cz[here] + ups[2]))
        v = dirn[own]
        res[here] = (
            cx[own] * (dirn[pl.ds(x, chunk)] - v)
            + ups[0] * (dirn[pl.ds(x + 2, chunk)] - v)
            + (cy[here] * (turned(v, 1, 1) - v) + ups[1] * (turned(v, -1, 1) - v))
            + (cz[here] * (turned(v, 1, 2) - v) + ups[2] * (turned(v, -1, 2) - v))
        )
        return carry

    sweep(prepare, 0)
    sol[...] = dirn[pl.ds(mine + 1, along), pl.ds(side, across)]
    for b in range(count_blk):
        res[b * along] = res[b * along] + heat[b * wide:(b + 1) * wide]

    def start(x, acc):
        here = pl.ds(x, chunk)
        dirn[pl.ds(x + 1, chunk)] = res[here]
        return acc + fold(res[here] * res[here])

    def apply(x, acc):
        here, own = pl.ds(x, chunk), pl.ds(x + 1, chunk)
        v = dirn[own]
        value = (
            diag[here] * v
            - (cx[own] * dirn[pl.ds(x, chunk)] + cx[pl.ds(x + 2, chunk)] * dirn[pl.ds(x + 2, chunk)])
            - (cy[here] * turned(v, 1, 1) + cyu[here] * turned(v, -1, 1))
            - (cz[here] * turned(v, 1, 2) + czu[here] * turned(v, -1, 2))
        )
        image[here] = value
        return acc + fold(v * value)

    norm = jnp.sum(sweep(start, none))
    for step in range(ITERS):
        alpha = norm / jnp.sum(sweep(apply, none))
        sol[...] = sol[...] + alpha * dirn[pl.ds(mine + 1, along), pl.ds(side, across)]
        if step + 1 == ITERS:
            break

        def reduce(x, acc, alpha=alpha):
            here = pl.ds(x, chunk)
            value = res[here] - alpha * image[here]
            res[here] = value
            return acc + fold(value * value)

        fresh = jnp.sum(sweep(reduce, none))
        beta = fresh / norm

        def turn(x, carry, beta=beta):
            own = pl.ds(x + 1, chunk)
            dirn[own] = res[pl.ds(x, chunk)] + beta * dirn[own]
            return carry

        sweep(turn, 0)
        norm = fresh
    out_ref[...] = sol[...]


def swap(value, axis, flip):
    count = lax.axis_size(axis)
    return lax.ppermute(value, axis, [(i, i ^ flip) for i in range(count)])


def outer(value):
    count = lax.axis_size("blk")
    pairs = [(i, (i + 1 if i % 2 else i - 1) % count) for i in range(count)]
    return lax.ppermute(value, "blk", pairs)


def ring(value, axis, step):
    count = lax.axis_size(axis)
    return lax.ppermute(value, axis, [(i, (i + step) % count) for i in range(count)])


def flips(count):
    return [1 << k for k in reversed(range((count - 1).bit_length()))]


def shards(
    mass_per_volume,
    flow_speed_vector,
    normal_stress,
    facing_strip_index,
    solid_kelvin,
    face_coupling,
    substance_index,
    substance_storage,
):
    planes, rows, lanes = mass_per_volume.shape
    along, across, _ = solid_kelvin.shape
    count_blk, count_sub = lax.axis_size("blk"), lax.axis_size("sub")
    devices = count_blk * count_sub
    cells = along * across
    edge = up_to_tile(FIELDS * planes * HALO)
    each = across + TILE
    record = 5 * cells + rows + TILE

    face = FIELDS * HALO * rows
    state, yedge, apay, bpay, metal, wall = call(
        pack_kernel,
        [
            f32(FIELDS, planes, rows, lanes), f32(2, edge, lanes),
            f32(face + record, lanes), f32(face + record, lanes),
            f32(record, lanes), f32(each, lanes),
        ],
        [
            mass_per_volume, flow_speed_vector, normal_stress,
            facing_strip_index.reshape(1, rows), solid_kelvin.reshape(cells, lanes),
            face_coupling.reshape(6 * cells, lanes), substance_index.reshape(cells, lanes),
            substance_storage,
        ],
        hbm=tuple(range(8)),
        scratch=[
            (planes, rows, lanes), (3, planes, rows, lanes), (planes, rows, lanes),
            pltpu.VMEM((1, rows), jnp.int32), pltpu.VMEM((cells, lanes), jnp.int32),
            pltpu.SMEM(substance_storage.shape, jnp.float32), pltpu.SemaphoreType.DMA((8,)),
        ],
    )
    paired = count_blk == 4 and count_sub == 2
    span = up_to_tile(FIELDS * HALO * HALO)
    bpay = outer(bpay)
    if paired:
        wall_a = swap(wall, "blk", 1)
        ypay = jnp.concatenate([yedge.reshape(2 * edge, lanes), wall, wall_a], axis=0)
        yrecv = swap(ypay, "sub", 1)
        ylo, yhi, lo_at, hi_at = yrecv, yrecv, edge, 0
        parts = [wall, wall_a, yrecv]
        starts = [(0, each), (0, each), (2 * edge, 2 * each)]
    else:
        ylo, yhi, lo_at, hi_at = ring(yedge[1], "sub", 1), ring(yedge[0], "sub", -1), 0, 0
        parts, starts = [], []
    apay = swap(apay, "blk", 1)
    aedge, bedge = call(
        functools.partial(edge_kernel, planes, lo_at, hi_at, starts),
        [f32(2 * span, lanes), f32(2 * span + sum(c for _, c in starts), lanes)],
        [ylo, yhi, *parts],
    )
    bedge = outer(bedge)
    aedge = swap(aedge, "blk", 1)
    if paired:
        walls = [wall, wall_a, yrecv, yrecv] + 4 * [bedge]
        wall_at = [(0, 0, 0), (0, 1, 0), (2 * edge, 0, 1), (2 * edge + each, 1, 1)]
        wall_at += [(2 * span + k * each, 3 ^ (k & 1), k >> 1) for k in range(4)]
    else:
        walls = [lax.all_gather(wall, ("blk", "sub"), axis=0, tiled=True)]
        wall_at = None
    deep, stride = planes + 2 * HALO, rows + TILE
    ends_rows = up_to_tile((FIELDS + 1) * HALO)
    wide_lanes = -(-deep * stride // lanes) * lanes
    block, zlo, zhi = call(
        functools.partial(
            assemble_kernel, ((count_blk, count_sub), across), lo_at, hi_at, wall_at
        ),
        [
            f32(FIELDS + 1, deep, stride, lanes),
            f32(ends_rows, wide_lanes),
            f32(ends_rows, wide_lanes),
        ],
        [state, apay, bpay, ylo, yhi, aedge, bedge, *walls],
        scratch=[(devices * each, lanes), (stride, lanes)],
    )
    zbelow = ring(zhi, "grp", 1)
    zabove = ring(zlo, "grp", -1)

    if paired:
        far = bpay[face:]
        near_y = swap(metal, "sub", 1)
        far_y = swap(far, "sub", 1)
        mates = swap(jnp.concatenate([far, near_y], axis=0), "blk", 1)
        mate_far_y = swap(far_y, "blk", 1)
        pieces = [metal, apay, bpay, near_y, far_y, mates, mate_far_y]
        where = [(0, 0), (1, face), (2, face), (3, 0), (4, 0), (5, 0), (5, record), (6, 0)]
        order = [(0, 0), (1, 0), (3, 0), (0, 1), (3, 1), (2, 0), (1, 1), (2, 1)]
    else:
        held, order = metal, [(0, 0)]
        steps = [("blk", flip) for flip in flips(count_blk)]
        steps += [("sub", flip) for flip in flips(count_sub)]
        for axis, flip in steps:
            held = jnp.concatenate([held, swap(held, axis, flip)], axis=0)
            order = order + [
                (b ^ flip, s) if axis == "blk" else (b, s ^ flip) for b, s in order
            ]
        pieces, where = [held], [(0, k * record) for k in range(devices)]
    wide = count_sub * across
    deep_metal = count_blk * along
    field = (deep_metal, wide, lanes)
    padded = (deep_metal + 2, wide, lanes)
    metal_next = call(
        functools.partial(
            metal_kernel, (count_blk, count_sub, along, across), rows, where, order
        ),
        f32(along, across, lanes),
        pieces,
        scratch=[
            (along, across, lanes), field, padded, field, field, padded, field, field, field,
            field, field, (devices * across, lanes), (TILE, devices * rows), (devices * rows, lanes),
        ],
    )
    fluid_next = call(
        fluid_kernel,
        f32(FIELDS, planes, rows, lanes),
        [block, zabove, zbelow, zlo, zhi],
        scratch=[
            (FIELDS, deep, stride, lanes), (8, deep, stride, lanes), (2, FIELDS, stride, lanes),
            (FIELDS, deep, stride, lanes), (FIELDS + 1, 2 * TILE, wide_lanes),
            (FIELDS, 2 * TILE, wide_lanes), (lanes, wide_lanes),
        ],
    )
    return (fluid_next, metal_next)


def solution(mesh):
    in_specs = (
        P("blk", "sub", "grp"),
        P(None, "blk", "sub", "grp"),
        P("blk", "sub", "grp"),
        P("grp", "blk", "sub"),
        P("blk", "sub", "grp"),
        P(None, "blk", "sub", "grp"),
        P("blk", "sub", "grp"),
        P(),
    )
    out_specs = (P(None, "blk", "sub", "grp"), P("blk", "sub", "grp"))
    return jax.shard_map(shards, mesh=mesh, in_specs=in_specs, out_specs=out_specs, check_vma=False)
```

time: 92.7 us -> 55.4 us (0.60)
  Pallas kernels: 49.4 us -> 18.1 us
  local copies, waits for them, and re-layouts: 4.48 us -> 0.01 us
  other arithmetic: 1.94 us -> 0.03 us
  waiting for transfers between devices: 21.8 us -> 22.9 us
    pallas_call x5, Pallas kernels: 49.4 us -> 18.1 us  [call(): pl.pallas_call(body, out_shape=out, in_specs=[pl.BlockSpec(memory_space=p...]
    ppermute x7 -> x8, waiting for transfers between devices: 17.1 us -> 6.92 us  [swap(): return lax.ppermute(value, axis, [(i, i ^ flip) for i in range(count)])]
    ppermute x2, waiting for transfers between devices: 2.27 us -> 10.1 us  [outer(): return lax.ppermute(value, 'blk', pairs)]
    ppermute x2, waiting for transfers between devices: 2.52 us -> 5.88 us  [ring(): lax.ppermute(value, axis, [(i, (i + step) % count) for i in range(count)])]
    unnamed x28 -> x0, local copies, waits for them, and re-layouts: 2.94 us -> none
    ppermute x7 -> x8, starting transfers between devices: 8.3 us -> 6.04 us  [swap(): return lax.ppermute(value, axis, [(i, i ^ flip) for i in range(count)])]
    concatenate x2 -> x1, other arithmetic: 1.93 us -> 0.02 us  [shards(): mates = swap(jnp.concatenate([far, near_y], axis=0), 'blk', 1)]
    ppermute x2, starting transfers between devices: 1.84 us -> 3.39 us  [outer(): return lax.ppermute(value, 'blk', pairs)]
  transfers between devices with their start and end apart: 11 -> 12, of which waited for: 8 -> 8; matrix products, arithmetic and copies ran while one was open for 0% -> 0% of each run, Pallas kernels for 39% -> 19%
where the time goes in v2:
time: 55.4 us; the launch traced here: 55.2 us
  waiting for transfers between devices  22.9 us (41%)
  Pallas kernels  18.1 us (33%)
  starting transfers between devices  13.5 us (24%)
  between operations  0.68 us (1%)
    pallas_call x5, Pallas kernels, call(): pl.pallas_call(body, out_shape=out, in_specs=[pl.BlockSpec(memory_space=p...  18.1 us
    ppermute x2, waiting for transfers between devices, outer(): return lax.ppermute(value, 'blk', pairs)  10.1 us
    ppermute x8, waiting for transfers between devices, swap(): return lax.ppermute(value, axis, [(i, i ^ flip) for i in range(count)])  6.92 us
    ppermute x8, starting transfers between devices, swap(): return lax.ppermute(value, axis, [(i, i ^ flip) for i in range(count)])  6.04 us
    ppermute x2, waiting for transfers between devices, ring(): lax.ppermute(value, axis, [(i, (i + step) % count) for i in range(count)])  5.88 us
    ppermute x2, starting transfers between devices, ring(): lax.ppermute(value, axis, [(i, (i + step) % count) for i in range(count)])  4.06 us
    ppermute x2, starting transfers between devices, outer(): return lax.ppermute(value, 'blk', pairs)  3.39 us
  transfers between devices with their start and end apart: 12, of which 8 were waited for; matrix products, arithmetic and copies ran while one was open for 0% of the time, Pallas kernels for 19%

profile of v2, /device:TPU:0, one launch (start us, length us, event | category | flops | bytes accessed | tf_op | source)
XLA Modules:
  0.0 55.2 jit_solution(14612253031799207594)
XLA Ops:
  0.6 1.2 %shard_map.95 = (f32[5,4,32,128]{3,2,1,0:T(8,128)S(1)}, f32[2,64,128]{2,1,0:T(8,128)S(1)}, f32[840,128]{1,0:T(8,128)S(1)}, f32[840,128]{1,0:T(8,128)S(1)}, f32[3...) custom-call(f32[4,32,128]{2,1,0:T(8,128)} %rho_hbm.1, f32[3,4,32,128]{3,2,1,0:T(8,128)} %vel_hbm.1, f32[4,32,128]{2,1,0:T(8,128)} %pre_hbm.1, ...), custom_call_target="tpu_custom_call" | custom-call | flops 100000 | bytes 100000 | tf_op jit(solution)/shard_map/pallas_call | solution.py:46
  1.8 2.5 %collective-permute-start.1 = (f32[840,128]{1,0:T(8,128)S(1)}, f32[840,128]{1,0:T(8,128)S(1)}, u32[]{:S(2)}, u32[]{:S(2)}) collective-permute-start(f32[840,128]{1,0:T(8,128)S(1)} %get-tuple-element.15), channel_id=1, source_target_pairs={{0,6},{2,4},{4,2},{6,0},{1,7},{3,5},{5,3},{7,1},{8,14},{10,12},{12... | collective-permute-start | bytes 1290248 | tf_op jit(solution)/shard_map/ppermute | solution.py:560
  4.3 1.5 %collective-permute-start.8 = (f32[360,128]{1,0:T(8,128)S(1)}, f32[360,128]{1,0:T(8,128)S(1)}, u32[]{:S(2)}, u32[]{:S(2)}) collective-permute-start(f32[360,128]{1,0:T(8,128)S(1)} %get-tuple-element.23.refs_0_), channel_id=1, source_target_pairs={{0,1},{1,0},{2,3},{3,2},{4,5},{5,4},{6,7},{7,6},{8,9},{9,8},{10,11... | collective-permute-start | bytes 552968 | tf_op jit(solution)/shard_map/ppermute | solution.py:554
  5.8 0.4 collective-permute-start
  6.2 8.4 %collective-permute-done.1.refs_2_ = f32[840,128]{1,0:T(8,128)S(1)} collective-permute-done((f32[840,128]{1,0:T(8,128)S(1)}, f32[840,128]{1,0:T(8,128)S(1)}, u32[]{:S(2)}, u32[]{:S(2)}) %collective-permute-start.1) | collective-permute-done | bytes 430112 | tf_op jit(solution)/shard_map/ppermute | solution.py:560
  14.6 2.5 %collective-permute-start.9 = (f32[360,128]{1,0:T(8,128)S(1)}, f32[360,128]{1,0:T(8,128)S(1)}, u32[]{:S(2)}, u32[]{:S(2)}) collective-permute-start(f32[360,128]{1,0:T(8,128)S(1)} %slice.4), channel_id=1, source_target_pairs={{0,1},{1,0},{2,3},{3,2},{4,5},{5,4},{6,7},{7,6},{8,9},{9,8},{10,11... | collective-permute-start | bytes 552968 | tf_op jit(solution)/shard_map/ppermute | solution.py:554
  17.1 0.0 collective-permute-done.8.refs_3_
  17.2 0.1 collective-permute-start.10
  17.2 0.5 collective-permute-start.2
  17.7 1.2 %collective-permute-done.2.refs_3_.refs_8_ = f32[16,128]{1,0:T(8,128)S(1)} collective-permute-done((f32[16,128]{1,0:T(8,128)S(1)}, f32[16,128]{1,0:T(8,128)S(1)}, u32[]{:S(2)}, u32[]{:S(2)}) %collective-permute-start.2) | collective-permute-done | bytes 8224 | tf_op jit(solution)/shard_map/ppermute | solution.py:554
  18.9 0.0 collective-permute-start.3
  19.0 3.5 %collective-permute-done.9.refs_4_ = f32[360,128]{1,0:T(8,128)S(1)} collective-permute-done((f32[360,128]{1,0:T(8,128)S(1)}, f32[360,128]{1,0:T(8,128)S(1)}, u32[]{:S(2)}, u32[]{:S(2)}) %collective-permute-start.9) | collective-permute-done | bytes 184352 | tf_op jit(solution)/shard_map/ppermute | solution.py:554
  22.4 0.0 collective-permute-start.11
  22.4 1.4 %collective-permute-done.3.refs_0_.refs_1_.refs_4_.refs_3_.refs_9_.refs_10_ = f32[160,128]{1,0:T(8,128)S(1)} collective-permute-done((f32[160,128]{1,0:T(8,128)S(1)}, f32[160,128]{1,0:T(8,128)S(1)}, u32[]{:S(2)}, u32[]{:S(2)}) %collective-permute-start.3) | collective-permute-done | bytes 81952 | tf_op jit(solution)/shard_map/ppermute | solution.py:554
  23.8 0.9 %collective-permute-start.5 = (f32[160,128]{1,0:T(8,128)S(1)}, f32[160,128]{1,0:T(8,128)S(1)}, u32[]{:S(2)}, u32[]{:S(2)}) collective-permute-start(f32[160,128]{1,0:T(8,128)S(1)} %get-tuple-element.19), channel_id=1, source_target_pairs={{0,6},{2,4},{4,2},{6,0},{1,7},{3,5},{5,3},{7,1},{8,14},{10,12},{12... | collective-permute-start | bytes 245768 | tf_op jit(solution)/shard_map/ppermute | solution.py:560
  24.7 1.0 %collective-permute-start.4 = (f32[96,128]{1,0:T(8,128)S(1)}, f32[96,128]{1,0:T(8,128)S(1)}, u32[]{:S(2)}, u32[]{:S(2)}) collective-permute-start(f32[96,128]{1,0:T(8,128)S(1)} %get-tuple-element.18), channel_id=1, source_target_pairs={{0,2},{2,0},{4,6},{6,4},{1,3},{3,1},{5,7},{7,5},{8,10},{10,8},{12,... | collective-permute-start | bytes 147464 | tf_op jit(solution)/shard_map/ppermute | solution.py:554
  25.8 0.9 %collective-permute-done.4.refs_5_ = f32[96,128]{1,0:T(8,128)S(1)} collective-permute-done((f32[96,128]{1,0:T(8,128)S(1)}, f32[96,128]{1,0:T(8,128)S(1)}, u32[]{:S(2)}, u32[]{:S(2)}) %collective-permute-start.4) | collective-permute-done | bytes 49184 | tf_op jit(solution)/shard_map/ppermute | solution.py:554
  26.6 1.7 %collective-permute-done.5.refs_6_.refs_11_.refs_12_.refs_13_.refs_14_ = f32[160,128]{1,0:T(8,128)S(1)} collective-permute-done((f32[160,128]{1,0:T(8,128)S(1)}, f32[160,128]{1,0:T(8,128)S(1)}, u32[]{:S(2)}, u32[]{:S(2)}) %collective-permute-start.5) | collective-permute-done | bytes 81952 | tf_op jit(solution)/shard_map/ppermute | solution.py:560
  28.3 0.0 collective-permute-done.refs_1_
  28.3 1.7 %shard_map.97 = (f32[6,10,40,128]{3,2,1,0:T(8,128)S(1)}, f32[24,512]{1,0:T(8,128)S(1)}, f32[24,512]{1,0:T(8,128)S(1)}) custom-call(f32[5,4,32,128]{3,2,1,0:T(8,128)S(1)} %get-tuple-element.13.refs_0_, f32[840,128]{1,0:T(8,128)S(1)} %collective-permute-done.refs_1_, f32[840,128]{1,0:T(8,128)S(1)} %collective-permute-done.1.refs_2_, ...), custom_call_target="tpu_custom_call" | custom-call | flops 100000 | bytes 100000 | tf_op jit(solution)/shard_map/pallas_call | solution.py:46
  30.1 4.1 %collective-permute-start.6 = (f32[24,512]{1,0:T(8,128)S(1)}, f32[24,512]{1,0:T(8,128)S(1)}, u32[]{:S(2)}, u32[]{:S(2)}) collective-permute-start(f32[24,512]{1,0:T(8,128)S(1)} %get-tuple-element.21.low_ref), channel_id=1, source_target_pairs={{0,24},{8,0},{16,8},{24,16},{1,25},{9,1},{17,9},{25,17},{2,26},{10... | collective-permute-start | bytes 147464 | tf_op jit(solution)/shard_map/ppermute | solution.py:565
  34.1 0.0 collective-permute-start.7
  34.1 1.8 %collective-permute-done.6.above_ref = f32[24,512]{1,0:T(8,128)S(1)} collective-permute-done((f32[24,512]{1,0:T(8,128)S(1)}, f32[24,512]{1,0:T(8,128)S(1)}, u32[]{:S(2)}, u32[]{:S(2)}) %collective-permute-start.6) | collective-permute-done | bytes 49184 | tf_op jit(solution)/shard_map/ppermute | solution.py:565
  35.9 4.1 %collective-permute-done.7.below_ref = f32[24,512]{1,0:T(8,128)S(1)} collective-permute-done((f32[24,512]{1,0:T(8,128)S(1)}, f32[24,512]{1,0:T(8,128)S(1)}, u32[]{:S(2)}, u32[]{:S(2)}) %collective-permute-start.7) | collective-permute-done | bytes 49184 | tf_op jit(solution)/shard_map/ppermute | solution.py:565
  40.0 8.5 %shard_map.98 = f32[5,4,32,128]{3,2,1,0:T(8,128)} custom-call(f32[6,10,40,128]{3,2,1,0:T(8,128)S(1)} %get-tuple-element.20.block_ref, f32[24,512]{1,0:T(8,128)S(1)} %collective-permute-done.6.above_ref, f32[24,512]{1,0:T(8,128)S(1)} %collective-permute-done.7.below_ref, f32[24,512]{1,0:T(8,128)S(1)} %get-tuple-element.21.low_ref, ...), custom_call_target="tpu_custom_call" | custom-call | flops 100000 | bytes 100000 | tf_op jit(solution)/shard_map/pallas_call | solution.py:46
  48.5 0.0 collective-permute-done.10.refs_5_
  48.5 0.0 collective-permute-done.11.refs_6_
  48.5 6.7 %shard_map.99 = f32[8,8,128]{2,1,0:T(8,128)} custom-call(f32[360,128]{1,0:T(8,128)S(1)} %get-tuple-element.23.refs_0_, f32[840,128]{1,0:T(8,128)S(1)} %collective-permute-done.refs_1_, f32[840,128]{1,0:T(8,128)S(1)} %collective-permute-done.1.refs_2_, f32[360,128]{1,0:T(8,128)S(1)} %collective-permute-done.8.refs_3_, ...), custom_call_target="tpu_custom_call" | custom-call | flops 100000 | bytes 100000 | tf_op jit(solution)/shard_map/pallas_call | solution.py:46
  (4 shorter events, 0.1 us)
Async XLA Ops:
  1.8 12.8 %collective-permute-start.1 = (f32[840,128]{1,0:T(8,128)S(1)}, f32[840,128]{1,0:T(8,128)S(1)}, u32[]{:S(2)}, u32[]{:S(2)}) collective-permute-start(f32[840,128]{1,0:T(8,128)S(1)} %get-tuple-element.15), channel_id=1, source_target_pairs={{0,6},{2,4},{4,2},{6,0},{1,7},{3,5},{5,3},{7,1},{8,14},{10,12},{12... | collective-permute-start | bytes 1290248 | tf_op jit(solution)/shard_map/ppermute | solution.py:560
  4.3 12.8 %collective-permute-start.8 = (f32[360,128]{1,0:T(8,128)S(1)}, f32[360,128]{1,0:T(8,128)S(1)}, u32[]{:S(2)}, u32[]{:S(2)}) collective-permute-start(f32[360,128]{1,0:T(8,128)S(1)} %get-tuple-element.23.refs_0_), channel_id=1, source_target_pairs={{0,1},{1,0},{2,3},{3,2},{4,5},{5,4},{6,7},{7,6},{8,9},{9,8},{10,11... | collective-permute-start | bytes 552968 | tf_op jit(solution)/shard_map/ppermute | solution.py:554
  5.8 22.5 %collective-permute-start = (f32[840,128]{1,0:T(8,128)S(1)}, f32[840,128]{1,0:T(8,128)S(1)}, u32[]{:S(2)}, u32[]{:S(2)}) collective-permute-start(f32[840,128]{1,0:T(8,128)S(1)} %get-tuple-element.14), channel_id=1, source_target_pairs={{0,2},{2,0},{4,6},{6,4},{1,3},{3,1},{5,7},{7,5},{8,10},{10,8},{12,... | collective-permute-start | bytes 1290248 | tf_op jit(solution)/shard_map/ppermute | solution.py:554
  14.6 7.8 %collective-permute-start.9 = (f32[360,128]{1,0:T(8,128)S(1)}, f32[360,128]{1,0:T(8,128)S(1)}, u32[]{:S(2)}, u32[]{:S(2)}) collective-permute-start(f32[360,128]{1,0:T(8,128)S(1)} %slice.4), channel_id=1, source_target_pairs={{0,1},{1,0},{2,3},{3,2},{4,5},{5,4},{6,7},{7,6},{8,9},{9,8},{10,11... | collective-permute-start | bytes 552968 | tf_op jit(solution)/shard_map/ppermute | solution.py:554
  17.2 31.4 %collective-permute-start.10 = (f32[720,128]{1,0:T(8,128)S(1)}, f32[720,128]{1,0:T(8,128)S(1)}, u32[]{:S(2)}, u32[]{:S(2)}) collective-permute-start(f32[720,128]{1,0:T(8,128)S(1)} %pad_maximum_fusion), channel_id=1, source_target_pairs={{0,2},{2,0},{4,6},{6,4},{1,3},{3,1},{5,7},{7,5},{8,10},{10,8},{12,... | collective-permute-start | bytes 1105928 | tf_op jit(solution)/shard_map/ppermute | solution.py:554
  17.2 1.7 %collective-permute-start.2 = (f32[16,128]{1,0:T(8,128)S(1)}, f32[16,128]{1,0:T(8,128)S(1)}, u32[]{:S(2)}, u32[]{:S(2)}) collective-permute-start(f32[16,128]{1,0:T(8,128)S(1)} %get-tuple-element.17.refs_2_.refs_7_), channel_id=1, source_target_pairs={{0,2},{2,0},{4,6},{6,4},{1,3},{3,1},{5,7},{7,5},{8,10},{10,8},{12,... | collective-permute-start | bytes 24584 | tf_op jit(solution)/shard_map/ppermute | solution.py:554
  18.9 4.9 %collective-permute-start.3 = (f32[160,128]{1,0:T(8,128)S(1)}, f32[160,128]{1,0:T(8,128)S(1)}, u32[]{:S(2)}, u32[]{:S(2)}) collective-permute-start(f32[160,128]{1,0:T(8,128)S(1)} %pad_maximum_fusion.1), channel_id=1, source_target_pairs={{0,1},{1,0},{2,3},{3,2},{4,5},{5,4},{6,7},{7,6},{8,9},{9,8},{10,11... | collective-permute-start | bytes 245768 | tf_op jit(solution)/shard_map/ppermute | solution.py:554
  22.4 26.1 %collective-permute-start.11 = (f32[360,128]{1,0:T(8,128)S(1)}, f32[360,128]{1,0:T(8,128)S(1)}, u32[]{:S(2)}, u32[]{:S(2)}) collective-permute-start(f32[360,128]{1,0:T(8,128)S(1)} %collective-permute-done.9.refs_4_), channel_id=1, source_target_pairs={{0,2},{2,0},{4,6},{6,4},{1,3},{3,1},{5,7},{7,5},{8,10},{10,8},{12,... | collective-permute-start | bytes 552968 | tf_op jit(solution)/shard_map/ppermute | solution.py:554
  23.8 4.5 %collective-permute-start.5 = (f32[160,128]{1,0:T(8,128)S(1)}, f32[160,128]{1,0:T(8,128)S(1)}, u32[]{:S(2)}, u32[]{:S(2)}) collective-permute-start(f32[160,128]{1,0:T(8,128)S(1)} %get-tuple-element.19), channel_id=1, source_target_pairs={{0,6},{2,4},{4,2},{6,0},{1,7},{3,5},{5,3},{7,1},{8,14},{10,12},{12... | collective-permute-start | bytes 245768 | tf_op jit(solution)/shard_map/ppermute | solution.py:560
  24.7 1.9 %collective-permute-start.4 = (f32[96,128]{1,0:T(8,128)S(1)}, f32[96,128]{1,0:T(8,128)S(1)}, u32[]{:S(2)}, u32[]{:S(2)}) collective-permute-start(f32[96,128]{1,0:T(8,128)S(1)} %get-tuple-element.18), channel_id=1, source_target_pairs={{0,2},{2,0},{4,6},{6,4},{1,3},{3,1},{5,7},{7,5},{8,10},{10,8},{12,... | collective-permute-start | bytes 147464 | tf_op jit(solution)/shard_map/ppermute | solution.py:554
  30.1 5.9 %collective-permute-start.6 = (f32[24,512]{1,0:T(8,128)S(1)}, f32[24,512]{1,0:T(8,128)S(1)}, u32[]{:S(2)}, u32[]{:S(2)}) collective-permute-start(f32[24,512]{1,0:T(8,128)S(1)} %get-tuple-element.21.low_ref), channel_id=1, source_target_pairs={{0,24},{8,0},{16,8},{24,16},{1,25},{9,1},{17,9},{25,17},{2,26},{10... | collective-permute-start | bytes 147464 | tf_op jit(solution)/shard_map/ppermute | solution.py:565
  34.1 5.9 %collective-permute-start.7 = (f32[24,512]{1,0:T(8,128)S(1)}, f32[24,512]{1,0:T(8,128)S(1)}, u32[]{:S(2)}, u32[]{:S(2)}) collective-permute-start(f32[24,512]{1,0:T(8,128)S(1)} %get-tuple-element.22.high_ref), channel_id=1, source_target_pairs={{0,8},{8,16},{16,24},{24,0},{1,9},{9,17},{17,25},{25,1},{2,10},{10... | collective-permute-start | bytes 147464 | tf_op jit(solution)/shard_map/ppermute | solution.py:565

commit v3 on v2

--- a/solution.py
+++ b/solution.py
@@ -13,6 +13,7 @@
 HALO = 3
 TILE = 8
 FIELDS = 5
+ROWS = 512
 
 gamma_gas = 1.4
 time_step = 0.1
@@ -75,6 +76,25 @@
     return lax.dot_general(
         a, b, (((a_dim,), (b_dim,)), ((), ())), precision=HIGHEST,
         preferred_element_type=jnp.float32,
+    )
+
+
+def pieces_of(value):
+    out = []
+    for _ in range(2):
+        piece = value.astype(jnp.bfloat16)
+        out.append(piece)
+        value = value - piece.astype(jnp.float32)
+    return out + [value.astype(jnp.bfloat16)]
+
+
+def select_sum(chosen, value, dim):
+    flags = chosen.astype(jnp.float32).astype(jnp.bfloat16)
+    return sum(
+        lax.dot_general(
+            flags, piece, (((dim,), (0,)), ((), ())), preferred_element_type=jnp.float32
+        )
+        for piece in reversed(pieces_of(value))
     )
 
 
@@ -236,8 +256,7 @@
         device = lax.rem(blk_at, count_blk) * count_sub + lax.rem(sub_at, count_sub)
         at = pl.multiple_of(device * each + across, TILE)
         routes = table[pl.ds(at, TILE)][0:1, 0:rows].astype(jnp.int32)
-        chosen = (iota((devices * across, rows), 0) == routes).astype(jnp.float32)
-        return dot(chosen, walls, 0, 0)
+        return select_sum(iota((devices * across, rows), 0) == routes, walls, 0)
 
     block_ref[FIELDS] = jnp.zeros(block_ref.shape[1:], jnp.float32)
     for x, blk_at in ((0, blk), (planes, blk + 1)):
@@ -300,7 +319,7 @@
     block_ref, above_ref, below_ref, low_ref, high_ref, out_ref,
     now, prim, xface, ends, slab_base, slab, comb,
 ):
-    _, planes, rows, lanes = out_ref.shape
+    _, _, rows, lanes = out_ref.shape
     deep, stride = block_ref.shape[1:3]
     size = deep * stride
     wide = slab.shape[2]
@@ -326,29 +345,25 @@
     for f in range(FIELDS):
         slab[f] = slab_base[f]
 
-    @pl.loop(0, deep)
-    def _(x):
-        for f in range(FIELDS):
-            now[f, x] = block_ref[f, x]
-
     first_row = lax.rem(iota((2 * TILE, wide), 1), stride) == 0
     last_row = lax.rem(iota((2 * TILE, wide), 1), stride) == stride - 1
 
     def lane_roll(v, shift):
         return pltpu.roll(v, shift % wide, axis=1)
 
-    def advance(old, change, start, sink, a, b):
+    def advance(stage, old, change, start, sink):
         fresh = old - (0.5 * time_step) * change
         if sink is not None:
             fresh = fresh - time_step * sink
-        return a * start + b * fresh
+        if stage == 0:
+            return fresh
+        if stage == 1:
+            return 0.75 * start + 0.25 * fresh
+        return third_part * start + two_thirds * fresh
 
     lane = iota((stride, lanes), 1)
-
-    @pl.loop(0, 3)
-    def _(stage):
-        a = jnp.where(stage == 0, 0.0, jnp.where(stage == 1, 0.75, third_part))
-        b = jnp.where(stage == 0, 1.0, jnp.where(stage == 1, 0.25, two_thirds))
+    for stage in range(3):
+        src = block_ref if stage == 0 else now
 
         u = [slab[f] for f in range(FIELDS)]
         q = primitives(u)
@@ -373,7 +388,7 @@
         ]
         for f in range(FIELDS):
             sink = slab_base[FIELDS] if f == FIELDS - 1 else None
-            slab[f] = advance(u[f], change[f], slab_base[f], sink, a, b)
+            slab[f] = advance(stage, u[f], change[f], slab_base[f], sink)
         whole = comb[0:part]
         for k in range(2):
             piece = whole.astype(jnp.bfloat16).astype(jnp.float32)
@@ -389,49 +404,42 @@
 
         low = stage + 1
         high = deep - 1 - stage
-
-        @pl.loop(low - 1, high + 1)
-        def _(x):
-            for k, value in enumerate(primitives([now[f, x] for f in range(FIELDS)])):
+        for x in range(low - 1, high + 1):
+            for k, value in enumerate(primitives([src[f, x] for f in range(FIELDS)])):
                 prim[k, x] = value
 
-        def cells(x, d):
-            return [now[f, x] for f in range(FIELDS)] + [
+        def cells(x, d, src=src):
+            return [src[f, x] for f in range(FIELDS)] + [
                 prim[d, x], prim[3 + d, x], prim[6, x], prim[7, x]
             ]
 
-        @pl.loop(low, high + 1)
-        def _(x):
+        for x in range(low, high + 1):
             new = faces(0, cells(x - 1, 0), cells(x, 0))
-            old = lax.rem(x, 2)
             for f in range(FIELDS):
-                xface[old, f] = new[f]
-
-            @pl.when(x > low)
-            def _():
-                p = x - 1
-                change = [new[f] - xface[1 - old, f] for f in range(FIELDS)]
-                hi = cells(p, 1)
-                lo = [pltpu.roll(v, 1, axis=0) for v in hi]
-                face = faces(1, lo, hi)
-                change = [
-                    c + (pltpu.roll(v, stride - 1, axis=0) - v) for c, v in zip(change, face)
-                ]
-                hi = cells(p, 2)
-                lo = [pltpu.roll(v, 1, axis=1) for v in hi]
-                face = faces(2, lo, hi)
-                for f in range(FIELDS):
-                    end = ends[f, p]
-                    top = jnp.where(lane == lanes - 1, end, pltpu.roll(face[f], lanes - 1, axis=1))
-                    low_face = jnp.where(lane == 0, end, face[f])
-                    sink = block_ref[FIELDS, p] if f == FIELDS - 1 else None
-                    now[f, p] = advance(
-                        now[f, p], change[f] + (top - low_face), block_ref[f, p], sink, a, b
-                    )
-
-    for f in range(FIELDS):
-        for x in range(planes):
-            out_ref[f, x] = now[f, x + HALO, 0:rows]
+                xface[x % 2, f] = new[f]
+            if x == low:
+                continue
+            p = x - 1
+            change = [new[f] - xface[p % 2, f] for f in range(FIELDS)]
+            hi = cells(p, 1)
+            lo = [pltpu.roll(v, 1, axis=0) for v in hi]
+            face = faces(1, lo, hi)
+            change = [c + (pltpu.roll(v, stride - 1, axis=0) - v) for c, v in zip(change, face)]
+            hi = cells(p, 2)
+            lo = [pltpu.roll(v, 1, axis=1) for v in hi]
+            face = faces(2, lo, hi)
+            for f in range(FIELDS):
+                end = ends[f, p]
+                top = jnp.where(lane == lanes - 1, end, pltpu.roll(face[f], lanes - 1, axis=1))
+                bottom = jnp.where(lane == 0, end, face[f])
+                sink = block_ref[FIELDS, p] if f == FIELDS - 1 else None
+                value = advance(
+                    stage, src[f, p], change[f] + (top - bottom), block_ref[f, p], sink
+                )
+                if stage == 2:
+                    out_ref[f, p - HALO] = value[0:rows]
+                else:
+                    now[f, p] = value
 
 
 def metal_kernel(dims, rows, where, order, *refs):
@@ -439,8 +447,9 @@
     devices = count_blk * count_sub
     pieces = [(refs[k], start) for k, start in where]
     (
-        out_ref, sol, res, dirn, image, diag, cx, cy, cz, cyu, czu, caps, heat, route, faced,
-    ) = refs[-15:]
+        out_ref, sol, kelvin, res, dirn, drift, image, diag, cx, cy, cz, cyu, czu, caps, heat,
+        route, faced,
+    ) = refs[-17:]
     lanes = out_ref.shape[-1]
     cells = along * across
     wide = count_sub * across
@@ -450,14 +459,14 @@
     side = pl.multiple_of(sub * across, TILE)
 
     zero = jnp.zeros((wide, lanes), jnp.float32)
-    for ref in (dirn, cx):
+    for ref in (kelvin, res, cx):
         ref[0] = zero
         ref[deep + 1] = zero
 
     for n, ((ref, first), (flip_blk, flip_sub)) in enumerate(zip(pieces, order)):
         b = jnp.bitwise_xor(blk, flip_blk) * along
         y = pl.multiple_of(jnp.bitwise_xor(sub, flip_sub) * across, TILE)
-        for field, (dest, shift) in enumerate(((dirn, 1), (caps, 0), (cx, 1), (cy, 0), (cz, 0))):
+        for field, (dest, shift) in enumerate(((kelvin, 1), (caps, 0), (cx, 1), (cy, 0), (cz, 0))):
             start = first + field * cells
             dest[pl.ds(b + shift, along), pl.ds(y, across)] = ref[
                 start:start + cells
@@ -466,15 +475,13 @@
         faced[n * rows:(n + 1) * rows] = ref[start:start + rows]
         route[:, n * rows:(n + 1) * rows] = ref[start + rows:start + rows + TILE][:, 0:rows]
 
-    walls = jnp.concatenate([dirn[1 + b * along] for b in range(count_blk)], axis=0)
+    walls = jnp.concatenate([kelvin[1 + b * along] for b in range(count_blk)], axis=0)
     strips = devices * across
-    chosen = (
-        iota((strips, devices * rows), 0) == route[0:1].astype(jnp.int32)
-    ).astype(jnp.float32)
-    flux = film_coeff * (faced[...] - dot(chosen, walls, 0, 0))
-    heat[...] = dot(chosen, flux, 1, 0)
-
-    chunk = 4 if deep % 4 == 0 else 1
+    chosen = iota((strips, devices * rows), 0) == route[0:1].astype(jnp.int32)
+    flux = film_coeff * (faced[...] - select_sum(chosen, walls, 0))
+    heat[...] = select_sum(chosen, flux, 1)
+
+    chunk = math.gcd(deep, max(1, ROWS // wide))
     none = jnp.zeros((TILE, lanes), jnp.float32)
 
     def sweep(body, init):
@@ -482,6 +489,13 @@
 
     def fold(value):
         return jnp.sum(value.reshape(-1, TILE, lanes), axis=0)
+
+    def total(value):
+        one = jnp.sum(jnp.sum(value, axis=0, keepdims=True), axis=1, keepdims=True)
+        return jnp.broadcast_to(one, (TILE, lanes))
+
+    def times(factor, value):
+        return (factor * value.reshape(-1, TILE, lanes)).reshape(value.shape)
 
     def turned(v, step, axis):
         return pltpu.roll(v, step % v.shape[axis], axis=axis)
@@ -492,61 +506,61 @@
         cyu[here] = ups[1]
         czu[here] = ups[2]
         diag[here] = caps[here] + ((cx[own] + ups[0]) + (cy[here] + ups[1]) + (cz[here] + ups[2]))
-        v = dirn[own]
-        res[here] = (
-            cx[own] * (dirn[pl.ds(x, chunk)] - v)
-            + ups[0] * (dirn[pl.ds(x + 2, chunk)] - v)
+        v = kelvin[own]
+        res[own] = (
+            cx[own] * (kelvin[pl.ds(x, chunk)] - v)
+            + ups[0] * (kelvin[pl.ds(x + 2, chunk)] - v)
             + (cy[here] * (turned(v, 1, 1) - v) + ups[1] * (turned(v, -1, 1) - v))
             + (cz[here] * (turned(v, 1, 2) - v) + ups[2] * (turned(v, -1, 2) - v))
         )
         return carry
 
     sweep(prepare, 0)
-    sol[...] = dirn[pl.ds(mine + 1, along), pl.ds(side, across)]
     for b in range(count_blk):
-        res[b * along] = res[b * along] + heat[b * wide:(b + 1) * wide]
-
-    def start(x, acc):
-        here = pl.ds(x, chunk)
-        dirn[pl.ds(x + 1, chunk)] = res[here]
-        return acc + fold(res[here] * res[here])
-
-    def apply(x, acc):
+        at = b * along + 1
+        res[at] = res[at] + heat[b * wide:(b + 1) * wide]
+
+    def apply(x, sums):
         here, own = pl.ds(x, chunk), pl.ds(x + 1, chunk)
-        v = dirn[own]
+        v = res[own]
         value = (
             diag[here] * v
-            - (cx[own] * dirn[pl.ds(x, chunk)] + cx[pl.ds(x + 2, chunk)] * dirn[pl.ds(x + 2, chunk)])
+            - (cx[own] * res[pl.ds(x, chunk)] + cx[pl.ds(x + 2, chunk)] * res[pl.ds(x + 2, chunk)])
             - (cy[here] * turned(v, 1, 1) + cyu[here] * turned(v, -1, 1))
             - (cz[here] * turned(v, 1, 2) + czu[here] * turned(v, -1, 2))
         )
         image[here] = value
-        return acc + fold(v * value)
-
-    norm = jnp.sum(sweep(start, none))
+        return sums[0] + fold(v * v), sums[1] + fold(v * value)
+
+    mine_at = pl.ds(mine, along), pl.ds(side, across)
+    sol[...] = kelvin[pl.ds(mine + 1, along), pl.ds(side, across)]
+    norm = alpha = beta = None
     for step in range(ITERS):
-        alpha = norm / jnp.sum(sweep(apply, none))
-        sol[...] = sol[...] + alpha * dirn[pl.ds(mine + 1, along), pl.ds(side, across)]
+        fresh, product = (total(v) for v in sweep(apply, (none, none)))
+        if step == 0:
+            alpha = fresh / product
+        else:
+            beta = fresh / norm
+            alpha = fresh / (product - beta * fresh / alpha)
+        norm = fresh
         if step + 1 == ITERS:
+            towards = res[pl.ds(mine + 1, along), pl.ds(side, across)] + times(beta, dirn[mine_at])
+            out_ref[...] = sol[...] + times(alpha, towards)
             break
 
-        def reduce(x, acc, alpha=alpha):
-            here = pl.ds(x, chunk)
-            value = res[here] - alpha * image[here]
-            res[here] = value
-            return acc + fold(value * value)
-
-        fresh = jnp.sum(sweep(reduce, none))
-        beta = fresh / norm
-
-        def turn(x, carry, beta=beta):
-            own = pl.ds(x + 1, chunk)
-            dirn[own] = res[pl.ds(x, chunk)] + beta * dirn[own]
+        def update(x, carry, step=step, alpha=alpha, beta=beta):
+            here, own = pl.ds(x, chunk), pl.ds(x + 1, chunk)
+            towards, moved = res[own], image[here]
+            if step:
+                towards = towards + times(beta, dirn[here])
+                moved = moved + times(beta, drift[here])
+            dirn[here] = towards
+            drift[here] = moved
+            res[own] = res[own] - times(alpha, moved)
             return carry
 
-        sweep(turn, 0)
-        norm = fresh
-    out_ref[...] = sol[...]
+        sweep(update, 0)
+        sol[...] = sol[...] + times(alpha, dirn[mine_at])
 
 
 def swap(value, axis, flip):
@@ -685,8 +699,8 @@
         f32(along, across, lanes),
         pieces,
         scratch=[
-            (along, across, lanes), field, padded, field, field, padded, field, field, field,
-            field, field, (devices * across, lanes), (TILE, devices * rows), (devices * rows, lanes),
+            (along, across, lanes), padded, padded, field, field, field, field, padded, field,
+            field, field, field, field, (devices * across, lanes), (TILE, devices * rows), (devices * rows, lanes),
         ],
     )
     fluid_next = call(

time: 55.4 us -> 48 us (0.87)
  Pallas kernels: 18.1 us -> 10.8 us
    pallas_call x5, Pallas kernels: 18.1 us -> 10.8 us  [call(): pl.pallas_call(body, out_shape=out, in_specs=[pl.BlockSpec(memory_space=p...]
  transfers between devices with their start and end apart: 12 -> 12, of which waited for: 8 -> 8; matrix products, arithmetic and copies ran while one was open for 0% -> 0% of each run, Pallas kernels for 19% -> 15%
where the time goes in v3:
time: 48 us; the launch traced here: 47.9 us
  waiting for transfers between devices  22.9 us (48%)
  starting transfers between devices  13.5 us (28%)
  Pallas kernels  10.8 us (22%)
  between operations  0.68 us (1%)
    pallas_call x5, Pallas kernels, call(): pl.pallas_call(body, out_shape=out, in_specs=[pl.BlockSpec(memory_space=p...  10.8 us
    ppermute x2, waiting for transfers between devices, outer(): return lax.ppermute(value, 'blk', pairs)  10.1 us
    ppermute x8, waiting for transfers between devices, swap(): return lax.ppermute(value, axis, [(i, i ^ flip) for i in range(count)])  6.92 us
    ppermute x8, starting transfers between devices, swap(): return lax.ppermute(value, axis, [(i, i ^ flip) for i in range(count)])  6.04 us
    ppermute x2, waiting for transfers between devices, ring(): lax.ppermute(value, axis, [(i, (i + step) % count) for i in range(count)])  5.88 us
    ppermute x2, starting transfers between devices, ring(): lax.ppermute(value, axis, [(i, (i + step) % count) for i in range(count)])  4.06 us
    ppermute x2, starting transfers between devices, outer(): return lax.ppermute(value, 'blk', pairs)  3.39 us
  transfers between devices with their start and end apart: 12, of which 8 were waited for; matrix products, arithmetic and copies ran while one was open for 0% of the time, Pallas kernels for 15%

profile of v3, /device:TPU:0, one launch (start us, length us, event | category | flops | bytes accessed | tf_op | source)
XLA Modules:
  0.0 47.9 jit_solution(7405574892560257890)
XLA Ops:
  0.6 1.2 %shard_map.95 = (f32[5,4,32,128]{3,2,1,0:T(8,128)S(1)}, f32[2,64,128]{2,1,0:T(8,128)S(1)}, f32[840,128]{1,0:T(8,128)S(1)}, f32[840,128]{1,0:T(8,128)S(1)}, f32[3...) custom-call(f32[4,32,128]{2,1,0:T(8,128)} %rho_hbm.1, f32[3,4,32,128]{3,2,1,0:T(8,128)} %vel_hbm.1, f32[4,32,128]{2,1,0:T(8,128)} %pre_hbm.1, ...), custom_call_target="tpu_custom_call" | custom-call | flops 100000 | bytes 100000 | tf_op jit(solution)/shard_map/pallas_call | solution.py:47
  1.8 2.5 %collective-permute-start.1 = (f32[840,128]{1,0:T(8,128)S(1)}, f32[840,128]{1,0:T(8,128)S(1)}, u32[]{:S(2)}, u32[]{:S(2)}) collective-permute-start(f32[840,128]{1,0:T(8,128)S(1)} %get-tuple-element.15), channel_id=1, source_target_pairs={{0,6},{2,4},{4,2},{6,0},{1,7},{3,5},{5,3},{7,1},{8,14},{10,12},{12... | collective-permute-start | bytes 1290248 | tf_op jit(solution)/shard_map/ppermute | solution.py:574
  4.3 1.5 %collective-permute-start.8 = (f32[360,128]{1,0:T(8,128)S(1)}, f32[360,128]{1,0:T(8,128)S(1)}, u32[]{:S(2)}, u32[]{:S(2)}) collective-permute-start(f32[360,128]{1,0:T(8,128)S(1)} %get-tuple-element.23.refs_0_), channel_id=1, source_target_pairs={{0,1},{1,0},{2,3},{3,2},{4,5},{5,4},{6,7},{7,6},{8,9},{9,8},{10,11... | collective-permute-start | bytes 552968 | tf_op jit(solution)/shard_map/ppermute | solution.py:568
  5.8 0.4 collective-permute-start
  6.2 8.4 %collective-permute-done.1.refs_2_ = f32[840,128]{1,0:T(8,128)S(1)} collective-permute-done((f32[840,128]{1,0:T(8,128)S(1)}, f32[840,128]{1,0:T(8,128)S(1)}, u32[]{:S(2)}, u32[]{:S(2)}) %collective-permute-start.1) | collective-permute-done | bytes 430112 | tf_op jit(solution)/shard_map/ppermute | solution.py:574
  14.6 2.5 %collective-permute-start.9 = (f32[360,128]{1,0:T(8,128)S(1)}, f32[360,128]{1,0:T(8,128)S(1)}, u32[]{:S(2)}, u32[]{:S(2)}) collective-permute-start(f32[360,128]{1,0:T(8,128)S(1)} %slice.4), channel_id=1, source_target_pairs={{0,1},{1,0},{2,3},{3,2},{4,5},{5,4},{6,7},{7,6},{8,9},{9,8},{10,11... | collective-permute-start | bytes 552968 | tf_op jit(solution)/shard_map/ppermute | solution.py:568
  17.1 0.0 collective-permute-done.8.refs_3_
  17.2 0.1 collective-permute-start.10
  17.2 0.5 %collective-permute-start.2 = (f32[16,128]{1,0:T(8,128)S(1)}, f32[16,128]{1,0:T(8,128)S(1)}, u32[]{:S(2)}, u32[]{:S(2)}) collective-permute-start(f32[16,128]{1,0:T(8,128)S(1)} %get-tuple-element.17.refs_2_.refs_7_), channel_id=1, source_target_pairs={{0,2},{2,0},{4,6},{6,4},{1,3},{3,1},{5,7},{7,5},{8,10},{10,8},{12,... | collective-permute-start | bytes 24584 | tf_op jit(solution)/shard_map/ppermute | solution.py:568
  17.7 1.2 %collective-permute-done.2.refs_3_.refs_8_ = f32[16,128]{1,0:T(8,128)S(1)} collective-permute-done((f32[16,128]{1,0:T(8,128)S(1)}, f32[16,128]{1,0:T(8,128)S(1)}, u32[]{:S(2)}, u32[]{:S(2)}) %collective-permute-start.2) | collective-permute-done | bytes 8224 | tf_op jit(solution)/shard_map/ppermute | solution.py:568
  18.9 0.0 collective-permute-start.3
  19.0 3.5 %collective-permute-done.9.refs_4_ = f32[360,128]{1,0:T(8,128)S(1)} collective-permute-done((f32[360,128]{1,0:T(8,128)S(1)}, f32[360,128]{1,0:T(8,128)S(1)}, u32[]{:S(2)}, u32[]{:S(2)}) %collective-permute-start.9) | collective-permute-done | bytes 184352 | tf_op jit(solution)/shard_map/ppermute | solution.py:568
  22.4 0.0 collective-permute-start.11
  22.4 1.4 %collective-permute-done.3.refs_0_.refs_1_.refs_4_.refs_3_.refs_9_.refs_10_ = f32[160,128]{1,0:T(8,128)S(1)} collective-permute-done((f32[160,128]{1,0:T(8,128)S(1)}, f32[160,128]{1,0:T(8,128)S(1)}, u32[]{:S(2)}, u32[]{:S(2)}) %collective-permute-start.3) | collective-permute-done | bytes 81952 | tf_op jit(solution)/shard_map/ppermute | solution.py:568
  23.8 0.9 %collective-permute-start.5 = (f32[160,128]{1,0:T(8,128)S(1)}, f32[160,128]{1,0:T(8,128)S(1)}, u32[]{:S(2)}, u32[]{:S(2)}) collective-permute-start(f32[160,128]{1,0:T(8,128)S(1)} %get-tuple-element.19), channel_id=1, source_target_pairs={{0,6},{2,4},{4,2},{6,0},{1,7},{3,5},{5,3},{7,1},{8,14},{10,12},{12... | collective-permute-start | bytes 245768 | tf_op jit(solution)/shard_map/ppermute | solution.py:574
  24.7 1.0 %collective-permute-start.4 = (f32[96,128]{1,0:T(8,128)S(1)}, f32[96,128]{1,0:T(8,128)S(1)}, u32[]{:S(2)}, u32[]{:S(2)}) collective-permute-start(f32[96,128]{1,0:T(8,128)S(1)} %get-tuple-element.18), channel_id=1, source_target_pairs={{0,2},{2,0},{4,6},{6,4},{1,3},{3,1},{5,7},{7,5},{8,10},{10,8},{12,... | collective-permute-start | bytes 147464 | tf_op jit(solution)/shard_map/ppermute | solution.py:568
  25.8 0.9 %collective-permute-done.4.refs_5_ = f32[96,128]{1,0:T(8,128)S(1)} collective-permute-done((f32[96,128]{1,0:T(8,128)S(1)}, f32[96,128]{1,0:T(8,128)S(1)}, u32[]{:S(2)}, u32[]{:S(2)}) %collective-permute-start.4) | collective-permute-done | bytes 49184 | tf_op jit(solution)/shard_map/ppermute | solution.py:568
  26.6 1.7 %collective-permute-done.5.refs_6_.refs_11_.refs_12_.refs_13_.refs_14_ = f32[160,128]{1,0:T(8,128)S(1)} collective-permute-done((f32[160,128]{1,0:T(8,128)S(1)}, f32[160,128]{1,0:T(8,128)S(1)}, u32[]{:S(2)}, u32[]{:S(2)}) %collective-permute-start.5) | collective-permute-done | bytes 81952 | tf_op jit(solution)/shard_map/ppermute | solution.py:574
  28.3 0.0 collective-permute-done.refs_1_
  28.3 1.6 %shard_map.97 = (f32[6,10,40,128]{3,2,1,0:T(8,128)S(1)}, f32[24,512]{1,0:T(8,128)S(1)}, f32[24,512]{1,0:T(8,128)S(1)}) custom-call(f32[5,4,32,128]{3,2,1,0:T(8,128)S(1)} %get-tuple-element.13.refs_0_, f32[840,128]{1,0:T(8,128)S(1)} %collective-permute-done.refs_1_, f32[840,128]{1,0:T(8,128)S(1)} %collective-permute-done.1.refs_2_, ...), custom_call_target="tpu_custom_call" | custom-call | flops 100000 | bytes 100000 | tf_op jit(solution)/shard_map/pallas_call | solution.py:47
  30.0 4.1 %collective-permute-start.6 = (f32[24,512]{1,0:T(8,128)S(1)}, f32[24,512]{1,0:T(8,128)S(1)}, u32[]{:S(2)}, u32[]{:S(2)}) collective-permute-start(f32[24,512]{1,0:T(8,128)S(1)} %get-tuple-element.21.low_ref), channel_id=1, source_target_pairs={{0,24},{8,0},{16,8},{24,16},{1,25},{9,1},{17,9},{25,17},{2,26},{10... | collective-permute-start | bytes 147464 | tf_op jit(solution)/shard_map/ppermute | solution.py:579
  34.0 0.0 collective-permute-start.7
  34.0 1.8 %collective-permute-done.6.above_ref = f32[24,512]{1,0:T(8,128)S(1)} collective-permute-done((f32[24,512]{1,0:T(8,128)S(1)}, f32[24,512]{1,0:T(8,128)S(1)}, u32[]{:S(2)}, u32[]{:S(2)}) %collective-permute-start.6) | collective-permute-done | bytes 49184 | tf_op jit(solution)/shard_map/ppermute | solution.py:579
  35.8 4.1 %collective-permute-done.7.below_ref = f32[24,512]{1,0:T(8,128)S(1)} collective-permute-done((f32[24,512]{1,0:T(8,128)S(1)}, f32[24,512]{1,0:T(8,128)S(1)}, u32[]{:S(2)}, u32[]{:S(2)}) %collective-permute-start.7) | collective-permute-done | bytes 49184 | tf_op jit(solution)/shard_map/ppermute | solution.py:579
  39.9 5.5 %shard_map.98 = f32[5,4,32,128]{3,2,1,0:T(8,128)} custom-call(f32[6,10,40,128]{3,2,1,0:T(8,128)S(1)} %get-tuple-element.20.block_ref, f32[24,512]{1,0:T(8,128)S(1)} %collective-permute-done.6.above_ref, f32[24,512]{1,0:T(8,128)S(1)} %collective-permute-done.7.below_ref, f32[24,512]{1,0:T(8,128)S(1)} %get-tuple-element.21.low_ref, ...), custom_call_target="tpu_custom_call" | custom-call | flops 100000 | bytes 100000 | tf_op jit(solution)/shard_map/pallas_call | solution.py:47
  45.4 0.0 collective-permute-done.10.refs_5_
  45.4 0.0 collective-permute-done.11.refs_6_
  45.4 2.5 %shard_map.99 = f32[8,8,128]{2,1,0:T(8,128)} custom-call(f32[360,128]{1,0:T(8,128)S(1)} %get-tuple-element.23.refs_0_, f32[840,128]{1,0:T(8,128)S(1)} %collective-permute-done.refs_1_, f32[840,128]{1,0:T(8,128)S(1)} %collective-permute-done.1.refs_2_, f32[360,128]{1,0:T(8,128)S(1)} %collective-permute-done.8.refs_3_, ...), custom_call_target="tpu_custom_call" | custom-call | flops 100000 | bytes 100000 | tf_op jit(solution)/shard_map/pallas_call | solution.py:47
  (4 shorter events, 0.1 us)
Async XLA Ops:
  1.8 12.8 %collective-permute-start.1 = (f32[840,128]{1,0:T(8,128)S(1)}, f32[840,128]{1,0:T(8,128)S(1)}, u32[]{:S(2)}, u32[]{:S(2)}) collective-permute-start(f32[840,128]{1,0:T(8,128)S(1)} %get-tuple-element.15), channel_id=1, source_target_pairs={{0,6},{2,4},{4,2},{6,0},{1,7},{3,5},{5,3},{7,1},{8,14},{10,12},{12... | collective-permute-start | bytes 1290248 | tf_op jit(solution)/shard_map/ppermute | solution.py:574
  4.3 12.8 %collective-permute-start.8 = (f32[360,128]{1,0:T(8,128)S(1)}, f32[360,128]{1,0:T(8,128)S(1)}, u32[]{:S(2)}, u32[]{:S(2)}) collective-permute-start(f32[360,128]{1,0:T(8,128)S(1)} %get-tuple-element.23.refs_0_), channel_id=1, source_target_pairs={{0,1},{1,0},{2,3},{3,2},{4,5},{5,4},{6,7},{7,6},{8,9},{9,8},{10,11... | collective-permute-start | bytes 552968 | tf_op jit(solution)/shard_map/ppermute | solution.py:568
  5.8 22.5 %collective-permute-start = (f32[840,128]{1,0:T(8,128)S(1)}, f32[840,128]{1,0:T(8,128)S(1)}, u32[]{:S(2)}, u32[]{:S(2)}) collective-permute-start(f32[840,128]{1,0:T(8,128)S(1)} %get-tuple-element.14), channel_id=1, source_target_pairs={{0,2},{2,0},{4,6},{6,4},{1,3},{3,1},{5,7},{7,5},{8,10},{10,8},{12,... | collective-permute-start | bytes 1290248 | tf_op jit(solution)/shard_map/ppermute | solution.py:568
  14.6 7.8 %collective-permute-start.9 = (f32[360,128]{1,0:T(8,128)S(1)}, f32[360,128]{1,0:T(8,128)S(1)}, u32[]{:S(2)}, u32[]{:S(2)}) collective-permute-start(f32[360,128]{1,0:T(8,128)S(1)} %slice.4), channel_id=1, source_target_pairs={{0,1},{1,0},{2,3},{3,2},{4,5},{5,4},{6,7},{7,6},{8,9},{9,8},{10,11... | collective-permute-start | bytes 552968 | tf_op jit(solution)/shard_map/ppermute | solution.py:568
  17.2 28.2 %collective-permute-start.10 = (f32[720,128]{1,0:T(8,128)S(1)}, f32[720,128]{1,0:T(8,128)S(1)}, u32[]{:S(2)}, u32[]{:S(2)}) collective-permute-start(f32[720,128]{1,0:T(8,128)S(1)} %pad_maximum_fusion), channel_id=1, source_target_pairs={{0,2},{2,0},{4,6},{6,4},{1,3},{3,1},{5,7},{7,5},{8,10},{10,8},{12,... | collective-permute-start | bytes 1105928 | tf_op jit(solution)/shard_map/ppermute | solution.py:568
  17.2 1.7 %collective-permute-start.2 = (f32[16,128]{1,0:T(8,128)S(1)}, f32[16,128]{1,0:T(8,128)S(1)}, u32[]{:S(2)}, u32[]{:S(2)}) collective-permute-start(f32[16,128]{1,0:T(8,128)S(1)} %get-tuple-element.17.refs_2_.refs_7_), channel_id=1, source_target_pairs={{0,2},{2,0},{4,6},{6,4},{1,3},{3,1},{5,7},{7,5},{8,10},{10,8},{12,... | collective-permute-start | bytes 24584 | tf_op jit(solution)/shard_map/ppermute | solution.py:568
  18.9 4.9 %collective-permute-start.3 = (f32[160,128]{1,0:T(8,128)S(1)}, f32[160,128]{1,0:T(8,128)S(1)}, u32[]{:S(2)}, u32[]{:S(2)}) collective-permute-start(f32[160,128]{1,0:T(8,128)S(1)} %pad_maximum_fusion.1), channel_id=1, source_target_pairs={{0,1},{1,0},{2,3},{3,2},{4,5},{5,4},{6,7},{7,6},{8,9},{9,8},{10,11... | collective-permute-start | bytes 245768 | tf_op jit(solution)/shard_map/ppermute | solution.py:568
  22.4 23.0 %collective-permute-start.11 = (f32[360,128]{1,0:T(8,128)S(1)}, f32[360,128]{1,0:T(8,128)S(1)}, u32[]{:S(2)}, u32[]{:S(2)}) collective-permute-start(f32[360,128]{1,0:T(8,128)S(1)} %collective-permute-done.9.refs_4_), channel_id=1, source_target_pairs={{0,2},{2,0},{4,6},{6,4},{1,3},{3,1},{5,7},{7,5},{8,10},{10,8},{12,... | collective-permute-start | bytes 552968 | tf_op jit(solution)/shard_map/ppermute | solution.py:568
  23.8 4.5 %collective-permute-start.5 = (f32[160,128]{1,0:T(8,128)S(1)}, f32[160,128]{1,0:T(8,128)S(1)}, u32[]{:S(2)}, u32[]{:S(2)}) collective-permute-start(f32[160,128]{1,0:T(8,128)S(1)} %get-tuple-element.19), channel_id=1, source_target_pairs={{0,6},{2,4},{4,2},{6,0},{1,7},{3,5},{5,3},{7,1},{8,14},{10,12},{12... | collective-permute-start | bytes 245768 | tf_op jit(solution)/shard_map/ppermute | solution.py:574
  24.7 1.9 %collective-permute-start.4 = (f32[96,128]{1,0:T(8,128)S(1)}, f32[96,128]{1,0:T(8,128)S(1)}, u32[]{:S(2)}, u32[]{:S(2)}) collective-permute-start(f32[96,128]{1,0:T(8,128)S(1)} %get-tuple-element.18), channel_id=1, source_target_pairs={{0,2},{2,0},{4,6},{6,4},{1,3},{3,1},{5,7},{7,5},{8,10},{10,8},{12,... | collective-permute-start | bytes 147464 | tf_op jit(solution)/shard_map/ppermute | solution.py:568
  30.0 5.9 %collective-permute-start.6 = (f32[24,512]{1,0:T(8,128)S(1)}, f32[24,512]{1,0:T(8,128)S(1)}, u32[]{:S(2)}, u32[]{:S(2)}) collective-permute-start(f32[24,512]{1,0:T(8,128)S(1)} %get-tuple-element.21.low_ref), channel_id=1, source_target_pairs={{0,24},{8,0},{16,8},{24,16},{1,25},{9,1},{17,9},{25,17},{2,26},{10... | collective-permute-start | bytes 147464 | tf_op jit(solution)/shard_map/ppermute | solution.py:579
  34.0 5.9 %collective-permute-start.7 = (f32[24,512]{1,0:T(8,128)S(1)}, f32[24,512]{1,0:T(8,128)S(1)}, u32[]{:S(2)}, u32[]{:S(2)}) collective-permute-start(f32[24,512]{1,0:T(8,128)S(1)} %get-tuple-element.22.high_ref), channel_id=1, source_target_pairs={{0,8},{8,16},{16,24},{24,0},{1,9},{9,17},{17,25},{25,1},{2,10},{10... | collective-permute-start | bytes 147464 | tf_op jit(solution)/shard_map/ppermute | solution.py:579

commit v4 on v3

--- a/solution.py
+++ b/solution.py
@@ -98,8 +98,8 @@
     )
 
 
-def parity():
-    return lax.rem(lax.axis_index("blk"), 2)
+def parity(axis="blk"):
+    return lax.rem(lax.axis_index(axis), 2)
 
 
 def pack_kernel(
@@ -167,7 +167,6 @@
     metal_ref[5 * cells + rows:5 * cells + rows + TILE] = wall_ref[across:across + TILE]
     record = 5 * cells + rows + TILE
     apay_ref[face:face + record] = metal_ref[...]
-    bpay_ref[face:face + record] = metal_ref[...]
 
 
 def edge_kernel(planes, lo_at, hi_at, starts, *refs):
@@ -206,7 +205,7 @@
     count_blk, count_sub = axes
     state_ref, aface_ref, bface_ref, ylo_ref, yhi_ref, aedge_ref, bedge_ref = refs[:7]
     wall_refs = refs[7:-5]
-    block_ref, zlo_ref, zhi_ref, table, seen = refs[-5:]
+    block_ref, inner_ref, outer_ref, table, seen = refs[-5:]
     _, planes, rows, lanes = state_ref.shape
     deep, stride = block_ref.shape[1:3]
     span = up_to_tile(FIELDS * HALO * HALO)
@@ -276,12 +275,14 @@
         | ((pick - HALO + lanes - HALO == cell) & (pick >= HALO) & (pick < 2 * HALO))
     ).astype(jnp.float32)
     size = deep * stride
+    upper = parity("grp") == 1
     for f in range(FIELDS + 1):
         ends = dot(chosen, block_ref[f].reshape(size, lanes), 1, 1)
-        zlo_ref[f * HALO:(f + 1) * HALO, 0:size] = ends[0:HALO]
-        zhi_ref[f * HALO:(f + 1) * HALO, 0:size] = ends[HALO:2 * HALO]
+        low, high = ends[0:HALO], ends[HALO:2 * HALO]
+        inner_ref[f * HALO:(f + 1) * HALO, 0:size] = jnp.where(upper, low, high)
+        outer_ref[f * HALO:(f + 1) * HALO, 0:size] = jnp.where(upper, high, low)
     used = (FIELDS + 1) * HALO
-    for ref in (zlo_ref, zhi_ref):
+    for ref in (inner_ref, outer_ref):
         if ref.shape[1] > size:
             ref[:, size:] = jnp.zeros((ref.shape[0], ref.shape[1] - size), jnp.float32)
         if ref.shape[0] > used:
@@ -315,9 +316,63 @@
     ]
 
 
+def advance(stage, old, change, start, sink):
+    fresh = old - (0.5 * time_step) * change
+    if sink is not None:
+        fresh = fresh - time_step * sink
+    if stage == 0:
+        return fresh
+    if stage == 1:
+        return 0.75 * start + 0.25 * fresh
+    return third_part * start + two_thirds * fresh
+
+
+def plane_stage(stage, src, block_ref, ends, put, prim, xface):
+    deep, stride, lanes = src.shape[1:]
+    lane = iota((stride, lanes), 1)
+    low, high = stage + 1, deep - 1 - stage
+    for x in range(low - 1, high + 1):
+        for k, value in enumerate(primitives([src[f, x] for f in range(FIELDS)])):
+            prim[k, x] = value
+
+    def cells(x, d):
+        return [src[f, x] for f in range(FIELDS)] + [
+            prim[d, x], prim[3 + d, x], prim[6, x], prim[7, x]
+        ]
+
+    for x in range(low, high + 1):
+        new = faces(0, cells(x - 1, 0), cells(x, 0))
+        for f in range(FIELDS):
+            xface[x % 2, f] = new[f]
+        if x == low:
+            continue
+        p = x - 1
+        change = [new[f] - xface[p % 2, f] for f in range(FIELDS)]
+        hi = cells(p, 1)
+        lo = [pltpu.roll(v, 1, axis=0) for v in hi]
+        face = faces(1, lo, hi)
+        change = [c + (pltpu.roll(v, stride - 1, axis=0) - v) for c, v in zip(change, face)]
+        hi = cells(p, 2)
+        lo = [pltpu.roll(v, 1, axis=1) for v in hi]
+        face = [jnp.where(lane == 0, 0.0, v) for v in faces(2, lo, hi)]
+        for f in range(FIELDS):
+            total = change[f] + (pltpu.roll(face[f], lanes - 1, axis=1) - face[f])
+            if ends is not None:
+                total = total + ends[f, p]
+            sink = block_ref[FIELDS, p] if f == FIELDS - 1 else None
+            put(f, p, advance(stage, src[f, p], total, block_ref[f, p], sink))
+
+
+def begin_kernel(block_ref, now_ref, prim, xface):
+    def put(f, p, value):
+        now_ref[f, p] = value
+
+    plane_stage(0, block_ref, block_ref, None, put, prim, xface)
+
+
 def fluid_kernel(
-    block_ref, above_ref, below_ref, low_ref, high_ref, out_ref,
-    now, prim, xface, ends, slab_base, slab, comb,
+    block_ref, now, inner_own, outer_own, inner_ref, outer_ref, out_ref,
+    prim, xface, ends, slab_base, slab, comb,
 ):
     _, _, rows, lanes = out_ref.shape
     deep, stride = block_ref.shape[1:3]
@@ -329,19 +384,21 @@
     target = iota((lanes, FIELDS * lanes), 1)
     field = lax.rem(source, part) // TILE
     end = lax.rem(source, TILE)
-    spread = (
-        ((end == 0) & (target == field * lanes))
-        | ((end == 1) & (target == field * lanes + lanes - 1))
-    ) & (source < 3 * part)
-    spread = spread.astype(jnp.float32).astype(jnp.bfloat16)
+    at_low = (end == 0) & (target == field * lanes) & (source < 3 * part)
+    at_high = (end == 1) & (target == field * lanes + lanes - 1) & (source < 3 * part)
+    spread = (at_high.astype(jnp.float32) - at_low.astype(jnp.float32)).astype(jnp.bfloat16)
     comb[...] = jnp.zeros(comb.shape, jnp.float32)
     slab_base[...] = jnp.zeros(slab_base.shape, jnp.float32)
+    upper = parity("grp") == 1
     for f in range(FIELDS + 1):
         at = slice(f * HALO, (f + 1) * HALO)
-        slab_base[f, 0:HALO] = below_ref[at]
-        slab_base[f, HALO:2 * HALO] = low_ref[at]
-        slab_base[f, group:group + HALO] = high_ref[at]
-        slab_base[f, group + HALO:group + 2 * HALO] = above_ref[at]
+        inner_z, outer_z, inner, outer = (
+            ref[at] for ref in (inner_own, outer_own, inner_ref, outer_ref)
+        )
+        slab_base[f, 0:HALO] = jnp.where(upper, inner, outer)
+        slab_base[f, HALO:2 * HALO] = jnp.where(upper, inner_z, outer_z)
+        slab_base[f, group:group + HALO] = jnp.where(upper, outer_z, inner_z)
+        slab_base[f, group + HALO:group + 2 * HALO] = jnp.where(upper, outer, inner)
     for f in range(FIELDS):
         slab[f] = slab_base[f]
 
@@ -351,20 +408,13 @@
     def lane_roll(v, shift):
         return pltpu.roll(v, shift % wide, axis=1)
 
-    def advance(stage, old, change, start, sink):
-        fresh = old - (0.5 * time_step) * change
-        if sink is not None:
-            fresh = fresh - time_step * sink
-        if stage == 0:
-            return fresh
-        if stage == 1:
-            return 0.75 * start + 0.25 * fresh
-        return third_part * start + two_thirds * fresh
-
-    lane = iota((stride, lanes), 1)
+    def put(f, p, value):
+        if stage == 2:
+            out_ref[f, p - HALO] = value[0:rows]
+        else:
+            now[f, p] = value
+
     for stage in range(3):
-        src = block_ref if stage == 0 else now
-
         u = [slab[f] for f in range(FIELDS)]
         q = primitives(u)
         hi = u + [q[2], q[5], q[6], q[7]]
@@ -402,44 +452,12 @@
         for f in range(FIELDS):
             ends[f] = moved[0:size, f * lanes:(f + 1) * lanes].reshape(deep, stride, lanes)
 
-        low = stage + 1
-        high = deep - 1 - stage
-        for x in range(low - 1, high + 1):
-            for k, value in enumerate(primitives([src[f, x] for f in range(FIELDS)])):
-                prim[k, x] = value
-
-        def cells(x, d, src=src):
-            return [src[f, x] for f in range(FIELDS)] + [
-                prim[d, x], prim[3 + d, x], prim[6, x], prim[7, x]
-            ]
-
-        for x in range(low, high + 1):
-            new = faces(0, cells(x - 1, 0), cells(x, 0))
-            for f in range(FIELDS):
-                xface[x % 2, f] = new[f]
-            if x == low:
-                continue
-            p = x - 1
-            change = [new[f] - xface[p % 2, f] for f in range(FIELDS)]
-            hi = cells(p, 1)
-            lo = [pltpu.roll(v, 1, axis=0) for v in hi]
-            face = faces(1, lo, hi)
-            change = [c + (pltpu.roll(v, stride - 1, axis=0) - v) for c, v in zip(change, face)]
-            hi = cells(p, 2)
-            lo = [pltpu.roll(v, 1, axis=1) for v in hi]
-            face = faces(2, lo, hi)
-            for f in range(FIELDS):
-                end = ends[f, p]
-                top = jnp.where(lane == lanes - 1, end, pltpu.roll(face[f], lanes - 1, axis=1))
-                bottom = jnp.where(lane == 0, end, face[f])
-                sink = block_ref[FIELDS, p] if f == FIELDS - 1 else None
-                value = advance(
-                    stage, src[f, p], change[f] + (top - bottom), block_ref[f, p], sink
-                )
-                if stage == 2:
-                    out_ref[f, p - HALO] = value[0:rows]
-                else:
-                    now[f, p] = value
+        if stage == 0:
+            for p in range(1, deep - 1):
+                for f in range(FIELDS):
+                    now[f, p] = now[f, p] - (0.5 * time_step) * ends[f, p]
+        else:
+            plane_stage(stage, now, block_ref, ends, put, prim, xface)
 
 
 def metal_kernel(dims, rows, where, order, *refs):
@@ -568,10 +586,10 @@
     return lax.ppermute(value, axis, [(i, i ^ flip) for i in range(count)])
 
 
-def outer(value):
-    count = lax.axis_size("blk")
+def outer(value, axis="blk"):
+    count = lax.axis_size(axis)
     pairs = [(i, (i + 1 if i % 2 else i - 1) % count) for i in range(count)]
-    return lax.ppermute(value, "blk", pairs)
+    return lax.ppermute(value, axis, pairs)
 
 
 def ring(value, axis, step):
@@ -607,7 +625,7 @@
         pack_kernel,
         [
             f32(FIELDS, planes, rows, lanes), f32(2, edge, lanes),
-            f32(face + record, lanes), f32(face + record, lanes),
+            f32(face + record, lanes), f32(face, lanes),
             f32(record, lanes), f32(each, lanes),
         ],
         [
@@ -654,7 +672,7 @@
     deep, stride = planes + 2 * HALO, rows + TILE
     ends_rows = up_to_tile((FIELDS + 1) * HALO)
     wide_lanes = -(-deep * stride // lanes) * lanes
-    block, zlo, zhi = call(
+    block, inner_z, outer_z = call(
         functools.partial(
             assemble_kernel, ((count_blk, count_sub), across), lo_at, hi_at, wall_at
         ),
@@ -666,18 +684,24 @@
         [state, apay, bpay, ylo, yhi, aedge, bedge, *walls],
         scratch=[(devices * each, lanes), (stride, lanes)],
     )
-    zbelow = ring(zhi, "grp", 1)
-    zabove = ring(zlo, "grp", -1)
+    inner_got = swap(inner_z, "grp", 1)
+    outer_got = outer(outer_z, "grp")
+    whole = (FIELDS, deep, stride, lanes)
+    work = [(8, deep, stride, lanes), (2, FIELDS, stride, lanes)]
+    first = call(begin_kernel, f32(*whole), [block], scratch=work)
 
     if paired:
-        far = bpay[face:]
         near_y = swap(metal, "sub", 1)
-        far_y = swap(far, "sub", 1)
-        mates = swap(jnp.concatenate([far, near_y], axis=0), "blk", 1)
-        mate_far_y = swap(far_y, "blk", 1)
-        pieces = [metal, apay, bpay, near_y, far_y, mates, mate_far_y]
-        where = [(0, 0), (1, face), (2, face), (3, 0), (4, 0), (5, 0), (5, record), (6, 0)]
-        order = [(0, 0), (1, 0), (3, 0), (0, 1), (3, 1), (2, 0), (1, 1), (2, 1)]
+        far = swap(metal, "blk", 2)
+        pairs = [
+            (b * count_sub + s, (b ^ 2) * count_sub + (s ^ 1))
+            for b in range(count_blk) for s in range(count_sub)
+        ]
+        far_y = lax.ppermute(metal, ("blk", "sub"), pairs)
+        mates = swap(jnp.concatenate([near_y, far_y, far], axis=0), "blk", 1)
+        pieces = [metal, apay, far, near_y, far_y, mates]
+        where = [(0, 0), (1, face), (2, 0), (3, 0), (4, 0)] + [(5, k * record) for k in range(3)]
+        order = [(0, 0), (1, 0), (2, 0), (0, 1), (2, 1), (1, 1), (3, 1), (3, 0)]
     else:
         held, order = metal, [(0, 0)]
         steps = [("blk", flip) for flip in flips(count_blk)]
@@ -706,11 +730,10 @@
     fluid_next = call(
         fluid_kernel,
         f32(FIELDS, planes, rows, lanes),
-        [block, zabove, zbelow, zlo, zhi],
+        [block, first, inner_z, outer_z, inner_got, outer_got],
         scratch=[
-            (FIELDS, deep, stride, lanes), (8, deep, stride, lanes), (2, FIELDS, stride, lanes),
-            (FIELDS, deep, stride, lanes), (FIELDS + 1, 2 * TILE, wide_lanes),
-            (FIELDS, 2 * TILE, wide_lanes), (lanes, wide_lanes),
+            *work, whole, (FIELDS + 1, 2 * TILE, wide_lanes), (FIELDS, 2 * TILE, wide_lanes),
+            (lanes, wide_lanes),
         ],
     )
     return (fluid_next, metal_next)

time: 48 us -> 42.7 us (0.89)
  waiting for transfers between devices: 22.9 us -> 17 us
  starting transfers between devices: 13.5 us -> 14 us
    ppermute x4, waiting for transfers between devices: 16 us -> 9.15 us  [the longest x1 4.84 us: shards(): far_y = lax.ppermute(metal, ('blk', 'sub'), pairs)]
    ppermute x4, starting transfers between devices: 7.45 us -> 8.43 us  [the longest x3 4.44 us: outer(): return lax.ppermute(value, axis, pairs)]
    ppermute x8, waiting for transfers between devices: 6.92 us -> 7.81 us  [swap(): return lax.ppermute(value, axis, [(i, i ^ flip) for i in range(count)])]
    ppermute x8, starting transfers between devices: 6.04 us -> 5.53 us  [swap(): return lax.ppermute(value, axis, [(i, i ^ flip) for i in range(count)])]
    pallas_call x5 -> x6, Pallas kernels: 10.8 us -> 10.9 us  [call(): pl.pallas_call(body, out_shape=out, in_specs=[pl.BlockSpec(memory_space=p...]
  transfers between devices with their start and end apart: 12 -> 12, of which waited for: 8 -> 7; matrix products, arithmetic and copies ran while one was open for 0% -> 0% of each run, Pallas kernels for 15% -> 17%
where the time goes in v4:
time: 42.7 us; the launch traced here: 42.5 us
  waiting for transfers between devices  17 us (40%)
  starting transfers between devices  14 us (33%)
  Pallas kernels  10.9 us (26%)
  between operations  0.69 us (2%)
    pallas_call x6, Pallas kernels, call(): pl.pallas_call(body, out_shape=out, in_specs=[pl.BlockSpec(memory_space=p...  10.9 us
    ppermute x8, waiting for transfers between devices, swap(): return lax.ppermute(value, axis, [(i, i ^ flip) for i in range(count)])  7.81 us
    ppermute x8, starting transfers between devices, swap(): return lax.ppermute(value, axis, [(i, i ^ flip) for i in range(count)])  5.53 us
    ppermute x1, waiting for transfers between devices, shards(): far_y = lax.ppermute(metal, ('blk', 'sub'), pairs)  4.84 us
    ppermute x3, starting transfers between devices, outer(): return lax.ppermute(value, axis, pairs)  4.44 us
    ppermute x3, waiting for transfers between devices, outer(): return lax.ppermute(value, axis, pairs)  4.31 us
    ppermute x1, starting transfers between devices, shards(): far_y = lax.ppermute(metal, ('blk', 'sub'), pairs)  3.99 us
  transfers between devices with their start and end apart: 12, of which 7 were waited for; matrix products, arithmetic and copies ran while one was open for 0% of the time, Pallas kernels for 17%

profile of v4, /device:TPU:0, one launch (start us, length us, event | category | flops | bytes accessed | tf_op | source)
XLA Modules:
  0.0 42.5 jit_solution(16625758715644253158)
XLA Ops:
  0.6 1.2 %shard_map.95 = (f32[5,4,32,128]{3,2,1,0:T(8,128)S(1)}, f32[2,64,128]{2,1,0:T(8,128)S(1)}, f32[840,128]{1,0:T(8,128)S(1)}, f32[480,128]{1,0:T(8,128)S(1)}, f32[3...) custom-call(f32[4,32,128]{2,1,0:T(8,128)} %rho_hbm.1, f32[3,4,32,128]{3,2,1,0:T(8,128)} %vel_hbm.1, f32[4,32,128]{2,1,0:T(8,128)} %pre_hbm.1, ...), custom_call_target="tpu_custom_call" | custom-call | flops 100000 | bytes 100000 | tf_op jit(solution)/shard_map/pallas_call | solution.py:47
  1.8 4.0 %collective-permute-start.10 = (f32[360,128]{1,0:T(8,128)S(1)}, f32[360,128]{1,0:T(8,128)S(1)}, u32[]{:S(2)}, u32[]{:S(2)}) collective-permute-start(f32[360,128]{1,0:T(8,128)S(1)} %get-tuple-element.23.refs_0_), channel_id=1, source_target_pairs={{0,5},{1,4},{2,7},{3,6},{4,1},{5,0},{6,3},{7,2},{8,13},{9,12},{10,... | collective-permute-start | bytes 552968 | tf_op jit(solution)/shard_map/ppermute | solution.py:700
  5.8 0.5 %collective-permute-start.8 = (f32[360,128]{1,0:T(8,128)S(1)}, f32[360,128]{1,0:T(8,128)S(1)}, u32[]{:S(2)}, u32[]{:S(2)}) collective-permute-start(f32[360,128]{1,0:T(8,128)S(1)} %get-tuple-element.23.refs_0_), channel_id=1, source_target_pairs={{0,4},{2,6},{4,0},{6,2},{1,5},{3,7},{5,1},{7,3},{8,12},{10,14},{12... | collective-permute-start | bytes 552968 | tf_op jit(solution)/shard_map/ppermute | solution.py:586
  6.3 0.1 collective-permute-start.9
  6.5 4.8 %collective-permute-done.10.refs_4_ = f32[360,128]{1,0:T(8,128)S(1)} collective-permute-done((f32[360,128]{1,0:T(8,128)S(1)}, f32[360,128]{1,0:T(8,128)S(1)}, u32[]{:S(2)}, u32[]{:S(2)}) %collective-permute-start.10) | collective-permute-done | bytes 184352 | tf_op jit(solution)/shard_map/ppermute | solution.py:700
  11.3 3.4 %collective-permute-done.8.refs_2_ = f32[360,128]{1,0:T(8,128)S(1)} collective-permute-done((f32[360,128]{1,0:T(8,128)S(1)}, f32[360,128]{1,0:T(8,128)S(1)}, u32[]{:S(2)}, u32[]{:S(2)}) %collective-permute-start.8) | collective-permute-done | bytes 184352 | tf_op jit(solution)/shard_map/ppermute | solution.py:586
  14.7 0.0 collective-permute-done.9.refs_3_
  14.7 0.1 collective-permute-start.11
  14.8 0.5 %collective-permute-start = (f32[840,128]{1,0:T(8,128)S(1)}, f32[840,128]{1,0:T(8,128)S(1)}, u32[]{:S(2)}, u32[]{:S(2)}) collective-permute-start(f32[840,128]{1,0:T(8,128)S(1)} %get-tuple-element.14), channel_id=1, source_target_pairs={{0,2},{2,0},{4,6},{6,4},{1,3},{3,1},{5,7},{7,5},{8,10},{10,8},{12,... | collective-permute-start | bytes 1290248 | tf_op jit(solution)/shard_map/ppermute | solution.py:586
  15.3 0.1 collective-permute-start.2
  15.4 1.5 %collective-permute-start.1 = (f32[480,128]{1,0:T(8,128)S(1)}, f32[480,128]{1,0:T(8,128)S(1)}, u32[]{:S(2)}, u32[]{:S(2)}) collective-permute-start(f32[480,128]{1,0:T(8,128)S(1)} %get-tuple-element.15), channel_id=1, source_target_pairs={{0,6},{2,4},{4,2},{6,0},{1,7},{3,5},{5,3},{7,1},{8,14},{10,12},{12... | collective-permute-start | bytes 737288 | tf_op jit(solution)/shard_map/ppermute | solution.py:592
  16.9 0.5 %collective-permute-done.2.refs_3_.refs_8_ = f32[16,128]{1,0:T(8,128)S(1)} collective-permute-done((f32[16,128]{1,0:T(8,128)S(1)}, f32[16,128]{1,0:T(8,128)S(1)}, u32[]{:S(2)}, u32[]{:S(2)}) %collective-permute-start.2) | collective-permute-done | bytes 8224 | tf_op jit(solution)/shard_map/ppermute | solution.py:586
  17.4 1.4 %collective-permute-start.3 = (f32[160,128]{1,0:T(8,128)S(1)}, f32[160,128]{1,0:T(8,128)S(1)}, u32[]{:S(2)}, u32[]{:S(2)}) collective-permute-start(f32[160,128]{1,0:T(8,128)S(1)} %pad_maximum_fusion.1), channel_id=1, source_target_pairs={{0,1},{1,0},{2,3},{3,2},{4,5},{5,4},{6,7},{7,6},{8,9},{9,8},{10,11... | collective-permute-start | bytes 245768 | tf_op jit(solution)/shard_map/ppermute | solution.py:586
  18.8 3.1 %collective-permute-done.3.refs_0_.refs_1_.refs_4_.refs_3_.refs_9_.refs_10_ = f32[160,128]{1,0:T(8,128)S(1)} collective-permute-done((f32[160,128]{1,0:T(8,128)S(1)}, f32[160,128]{1,0:T(8,128)S(1)}, u32[]{:S(2)}, u32[]{:S(2)}) %collective-permute-start.3) | collective-permute-done | bytes 81952 | tf_op jit(solution)/shard_map/ppermute | solution.py:586
  21.9 0.4 %collective-permute-start.5 = (f32[160,128]{1,0:T(8,128)S(1)}, f32[160,128]{1,0:T(8,128)S(1)}, u32[]{:S(2)}, u32[]{:S(2)}) collective-permute-start(f32[160,128]{1,0:T(8,128)S(1)} %get-tuple-element.19), channel_id=1, source_target_pairs={{0,6},{2,4},{4,2},{6,0},{1,7},{3,5},{5,3},{7,1},{8,14},{10,12},{12... | collective-permute-start | bytes 245768 | tf_op jit(solution)/shard_map/ppermute | solution.py:592
  22.3 1.2 %collective-permute-start.4 = (f32[96,128]{1,0:T(8,128)S(1)}, f32[96,128]{1,0:T(8,128)S(1)}, u32[]{:S(2)}, u32[]{:S(2)}) collective-permute-start(f32[96,128]{1,0:T(8,128)S(1)} %get-tuple-element.18), channel_id=1, source_target_pairs={{0,2},{2,0},{4,6},{6,4},{1,3},{3,1},{5,7},{7,5},{8,10},{10,8},{12,... | collective-permute-start | bytes 147464 | tf_op jit(solution)/shard_map/ppermute | solution.py:586
  23.6 0.9 %collective-permute-done.4.refs_5_ = f32[96,128]{1,0:T(8,128)S(1)} collective-permute-done((f32[96,128]{1,0:T(8,128)S(1)}, f32[96,128]{1,0:T(8,128)S(1)}, u32[]{:S(2)}, u32[]{:S(2)}) %collective-permute-start.4) | collective-permute-done | bytes 49184 | tf_op jit(solution)/shard_map/ppermute | solution.py:586
  24.5 2.2 %collective-permute-done.5.refs_6_.refs_11_.refs_12_.refs_13_.refs_14_ = f32[160,128]{1,0:T(8,128)S(1)} collective-permute-done((f32[160,128]{1,0:T(8,128)S(1)}, f32[160,128]{1,0:T(8,128)S(1)}, u32[]{:S(2)}, u32[]{:S(2)}) %collective-permute-start.5) | collective-permute-done | bytes 81952 | tf_op jit(solution)/shard_map/ppermute | solution.py:592
  26.7 0.0 collective-permute-done.1.refs_2_
  26.7 0.0 collective-permute-done.refs_1_
  26.7 1.6 %shard_map.97 = (f32[6,10,40,128]{3,2,1,0:T(8,128)S(1)}, f32[24,512]{1,0:T(8,128)S(1)}, f32[24,512]{1,0:T(8,128)S(1)}) custom-call(f32[5,4,32,128]{3,2,1,0:T(8,128)S(1)} %get-tuple-element.13.refs_0_, f32[840,128]{1,0:T(8,128)S(1)} %collective-permute-done.refs_1_, f32[480,128]{1,0:T(8,128)S(1)} %collective-permute-done.1.refs_2_, ...), custom_call_target="tpu_custom_call" | custom-call | flops 100000 | bytes 100000 | tf_op jit(solution)/shard_map/pallas_call | solution.py:47
  28.3 1.6 %collective-permute-start.6 = (f32[24,512]{1,0:T(8,128)S(1)}, f32[24,512]{1,0:T(8,128)S(1)}, u32[]{:S(2)}, u32[]{:S(2)}) collective-permute-start(f32[24,512]{1,0:T(8,128)S(1)} %get-tuple-element.21.inner_own), channel_id=1, source_target_pairs={{0,8},{8,0},{16,24},{24,16},{1,9},{9,1},{17,25},{25,17},{2,10},{10... | collective-permute-start | bytes 147464 | tf_op jit(solution)/shard_map/ppermute | solution.py:586
  29.9 2.5 %collective-permute-start.7 = (f32[24,512]{1,0:T(8,128)S(1)}, f32[24,512]{1,0:T(8,128)S(1)}, u32[]{:S(2)}, u32[]{:S(2)}) collective-permute-start(f32[24,512]{1,0:T(8,128)S(1)} %get-tuple-element.22.outer_own), channel_id=1, source_target_pairs={{0,24},{8,16},{16,8},{24,0},{1,25},{9,17},{17,9},{25,1},{2,26},{10... | collective-permute-start | bytes 147464 | tf_op jit(solution)/shard_map/ppermute | solution.py:592
  32.4 1.3 %shard_map.98.now = f32[5,10,40,128]{3,2,1,0:T(8,128)S(1)} custom-call(f32[6,10,40,128]{3,2,1,0:T(8,128)S(1)} %get-tuple-element.20.block_ref), custom_call_target="tpu_custom_call" | custom-call | flops 100000 | bytes 100000 | tf_op jit(solution)/shard_map/pallas_call | solution.py:47
  33.7 0.0 collective-permute-done.6.inner_ref
  33.7 2.1 %collective-permute-done.7.outer_ref = f32[24,512]{1,0:T(8,128)S(1)} collective-permute-done((f32[24,512]{1,0:T(8,128)S(1)}, f32[24,512]{1,0:T(8,128)S(1)}, u32[]{:S(2)}, u32[]{:S(2)}) %collective-permute-start.7) | collective-permute-done | bytes 49184 | tf_op jit(solution)/shard_map/ppermute | solution.py:592
  35.8 4.2 %shard_map.99 = f32[5,4,32,128]{3,2,1,0:T(8,128)} custom-call(f32[6,10,40,128]{3,2,1,0:T(8,128)S(1)} %get-tuple-element.20.block_ref, f32[5,10,40,128]{3,2,1,0:T(8,128)S(1)} %shard_map.98.now, f32[24,512]{1,0:T(8,128)S(1)} %get-tuple-element.21.inner_own, f32[24,512]{1,0:T(8,128)S(1)} %get-tuple-element.22.outer_own, ...), custom_call_target="tpu_custom_call" | custom-call | flops 100000 | bytes 100000 | tf_op jit(solution)/shard_map/pallas_call | solution.py:47
  40.0 0.0 collective-permute-done.11.refs_5_
  40.0 2.5 %shard_map.100 = f32[8,8,128]{2,1,0:T(8,128)} custom-call(f32[360,128]{1,0:T(8,128)S(1)} %get-tuple-element.23.refs_0_, f32[840,128]{1,0:T(8,128)S(1)} %collective-permute-done.refs_1_, f32[360,128]{1,0:T(8,128)S(1)} %collective-permute-done.8.refs_2_, f32[360,128]{1,0:T(8,128)S(1)} %collective-permute-done.9.refs_3_, ...), custom_call_target="tpu_custom_call" | custom-call | flops 100000 | bytes 100000 | tf_op jit(solution)/shard_map/pallas_call | solution.py:47
  (3 shorter events, 0.1 us)
Async XLA Ops:
  1.8 9.5 %collective-permute-start.10 = (f32[360,128]{1,0:T(8,128)S(1)}, f32[360,128]{1,0:T(8,128)S(1)}, u32[]{:S(2)}, u32[]{:S(2)}) collective-permute-start(f32[360,128]{1,0:T(8,128)S(1)} %get-tuple-element.23.refs_0_), channel_id=1, source_target_pairs={{0,5},{1,4},{2,7},{3,6},{4,1},{5,0},{6,3},{7,2},{8,13},{9,12},{10,... | collective-permute-start | bytes 552968 | tf_op jit(solution)/shard_map/ppermute | solution.py:700
  5.8 8.9 %collective-permute-start.8 = (f32[360,128]{1,0:T(8,128)S(1)}, f32[360,128]{1,0:T(8,128)S(1)}, u32[]{:S(2)}, u32[]{:S(2)}) collective-permute-start(f32[360,128]{1,0:T(8,128)S(1)} %get-tuple-element.23.refs_0_), channel_id=1, source_target_pairs={{0,4},{2,6},{4,0},{6,2},{1,5},{3,7},{5,1},{7,3},{8,12},{10,14},{12... | collective-permute-start | bytes 552968 | tf_op jit(solution)/shard_map/ppermute | solution.py:586
  6.3 8.3 %collective-permute-start.9 = (f32[360,128]{1,0:T(8,128)S(1)}, f32[360,128]{1,0:T(8,128)S(1)}, u32[]{:S(2)}, u32[]{:S(2)}) collective-permute-start(f32[360,128]{1,0:T(8,128)S(1)} %get-tuple-element.23.refs_0_), channel_id=1, source_target_pairs={{0,1},{1,0},{2,3},{3,2},{4,5},{5,4},{6,7},{7,6},{8,9},{9,8},{10,11... | collective-permute-start | bytes 552968 | tf_op jit(solution)/shard_map/ppermute | solution.py:586
  14.7 25.3 %collective-permute-start.11 = (f32[1080,128]{1,0:T(8,128)S(1)}, f32[1080,128]{1,0:T(8,128)S(1)}, u32[]{:S(2)}, u32[]{:S(2)}) collective-permute-start(f32[1080,128]{1,0:T(8,128)S(1)} %pad_maximum_fusion), channel_id=1, source_target_pairs={{0,2},{2,0},{4,6},{6,4},{1,3},{3,1},{5,7},{7,5},{8,10},{10,8},{12,... | collective-permute-start | bytes 1658888 | tf_op jit(solution)/shard_map/ppermute | solution.py:586
  14.8 11.8 %collective-permute-start = (f32[840,128]{1,0:T(8,128)S(1)}, f32[840,128]{1,0:T(8,128)S(1)}, u32[]{:S(2)}, u32[]{:S(2)}) collective-permute-start(f32[840,128]{1,0:T(8,128)S(1)} %get-tuple-element.14), channel_id=1, source_target_pairs={{0,2},{2,0},{4,6},{6,4},{1,3},{3,1},{5,7},{7,5},{8,10},{10,8},{12,... | collective-permute-start | bytes 1290248 | tf_op jit(solution)/shard_map/ppermute | solution.py:586
  15.3 2.1 %collective-permute-start.2 = (f32[16,128]{1,0:T(8,128)S(1)}, f32[16,128]{1,0:T(8,128)S(1)}, u32[]{:S(2)}, u32[]{:S(2)}) collective-permute-start(f32[16,128]{1,0:T(8,128)S(1)} %get-tuple-element.17.refs_2_.refs_7_), channel_id=1, source_target_pairs={{0,2},{2,0},{4,6},{6,4},{1,3},{3,1},{5,7},{7,5},{8,10},{10,8},{12,... | collective-permute-start | bytes 24584 | tf_op jit(solution)/shard_map/ppermute | solution.py:586
  15.4 11.3 %collective-permute-start.1 = (f32[480,128]{1,0:T(8,128)S(1)}, f32[480,128]{1,0:T(8,128)S(1)}, u32[]{:S(2)}, u32[]{:S(2)}) collective-permute-start(f32[480,128]{1,0:T(8,128)S(1)} %get-tuple-element.15), channel_id=1, source_target_pairs={{0,6},{2,4},{4,2},{6,0},{1,7},{3,5},{5,3},{7,1},{8,14},{10,12},{12... | collective-permute-start | bytes 737288 | tf_op jit(solution)/shard_map/ppermute | solution.py:592
  17.4 4.5 %collective-permute-start.3 = (f32[160,128]{1,0:T(8,128)S(1)}, f32[160,128]{1,0:T(8,128)S(1)}, u32[]{:S(2)}, u32[]{:S(2)}) collective-permute-start(f32[160,128]{1,0:T(8,128)S(1)} %pad_maximum_fusion.1), channel_id=1, source_target_pairs={{0,1},{1,0},{2,3},{3,2},{4,5},{5,4},{6,7},{7,6},{8,9},{9,8},{10,11... | collective-permute-start | bytes 245768 | tf_op jit(solution)/shard_map/ppermute | solution.py:586
  21.9 4.8 %collective-permute-start.5 = (f32[160,128]{1,0:T(8,128)S(1)}, f32[160,128]{1,0:T(8,128)S(1)}, u32[]{:S(2)}, u32[]{:S(2)}) collective-permute-start(f32[160,128]{1,0:T(8,128)S(1)} %get-tuple-element.19), channel_id=1, source_target_pairs={{0,6},{2,4},{4,2},{6,0},{1,7},{3,5},{5,3},{7,1},{8,14},{10,12},{12... | collective-permute-start | bytes 245768 | tf_op jit(solution)/shard_map/ppermute | solution.py:592
  22.3 2.1 %collective-permute-start.4 = (f32[96,128]{1,0:T(8,128)S(1)}, f32[96,128]{1,0:T(8,128)S(1)}, u32[]{:S(2)}, u32[]{:S(2)}) collective-permute-start(f32[96,128]{1,0:T(8,128)S(1)} %get-tuple-element.18), channel_id=1, source_target_pairs={{0,2},{2,0},{4,6},{6,4},{1,3},{3,1},{5,7},{7,5},{8,10},{10,8},{12,... | collective-permute-start | bytes 147464 | tf_op jit(solution)/shard_map/ppermute | solution.py:586
  28.3 5.4 %collective-permute-start.6 = (f32[24,512]{1,0:T(8,128)S(1)}, f32[24,512]{1,0:T(8,128)S(1)}, u32[]{:S(2)}, u32[]{:S(2)}) collective-permute-start(f32[24,512]{1,0:T(8,128)S(1)} %get-tuple-element.21.inner_own), channel_id=1, source_target_pairs={{0,8},{8,0},{16,24},{24,16},{1,9},{9,1},{17,25},{25,17},{2,10},{10... | collective-permute-start | bytes 147464 | tf_op jit(solution)/shard_map/ppermute | solution.py:586
  29.9 5.9 %collective-permute-start.7 = (f32[24,512]{1,0:T(8,128)S(1)}, f32[24,512]{1,0:T(8,128)S(1)}, u32[]{:S(2)}, u32[]{:S(2)}) collective-permute-start(f32[24,512]{1,0:T(8,128)S(1)} %get-tuple-element.22.outer_own), channel_id=1, source_target_pairs={{0,24},{8,16},{16,8},{24,0},{1,25},{9,17},{17,9},{25,1},{2,26},{10... | collective-permute-start | bytes 147464 | tf_op jit(solution)/shard_map/ppermute | solution.py:592

commit v5 on v4

--- a/solution.py
+++ b/solution.py
@@ -13,6 +13,7 @@
 HALO = 3
 TILE = 8
 FIELDS = 5
+NEAR = 2 * HALO
 ROWS = 512
 
 gamma_gas = 1.4
@@ -22,7 +23,6 @@
 third_part = 1.0 / 3.0
 two_thirds = 2.0 / 3.0
 
-HIGHEST = lax.Precision.HIGHEST
 SPARE_BYTES = 6 * 1024 * 1024
 
 
@@ -72,13 +72,6 @@
     return lax.broadcasted_iota(jnp.int32, shape, dim)
 
 
-def dot(a, b, a_dim, b_dim):
-    return lax.dot_general(
-        a, b, (((a_dim,), (b_dim,)), ((), ())), precision=HIGHEST,
-        preferred_element_type=jnp.float32,
-    )
-
-
 def pieces_of(value):
     out = []
     for _ in range(2):
@@ -109,7 +102,7 @@
 ):
     planes, rows, lanes = rho_ref.shape
     cells = kind_ref.shape[0]
-    across = wall_ref.shape[0] - TILE
+    across = wall_ref.shape[0] - 1
     face = FIELDS * HALO * rows
     copies = [
         pltpu.make_async_copy(src, dst, arrived.at[k])
@@ -136,13 +129,8 @@
     for f in range(FIELDS):
         for x in range(planes):
             at = (f * planes + x) * HALO
-            yedge_ref[0, at:at + HALO] = state_ref[f, x, 0:HALO]
-            yedge_ref[1, at:at + HALO] = state_ref[f, x, rows - HALO:rows]
-    if yedge_ref.shape[1] > used:
-        for side in range(2):
-            yedge_ref[side, used:] = jnp.zeros(
-                (yedge_ref.shape[1] - used, lanes), jnp.float32
-            )
+            yedge_ref[at:at + HALO] = state_ref[f, x, 0:HALO]
+            yedge_ref[used + at:used + at + HALO] = state_ref[f, x, rows - HALO:rows]
     for odd in range(2):
 
         @pl.when(parity() == odd)
@@ -156,7 +144,7 @@
     for copy in copies[3:]:
         copy.wait()
     wall_ref[0:across] = metal_ref[0:across]
-    wall_ref[across:across + TILE] = jnp.zeros((TILE, lanes), jnp.float32)
+    wall_ref[across:across + 1] = jnp.zeros((1, lanes), jnp.float32)
     wall_ref[across:across + 1, 0:rows] = route_ref[...].astype(jnp.float32)
     kind = kind_ref[...]
     capacity = jnp.zeros((cells, lanes), jnp.float32)
@@ -164,37 +152,39 @@
         capacity = jnp.where(kind == m, store_ref[m], capacity)
     metal_ref[cells:2 * cells] = capacity
     metal_ref[5 * cells:5 * cells + rows] = pre_ref[0] / rho_ref[0]
-    metal_ref[5 * cells + rows:5 * cells + rows + TILE] = wall_ref[across:across + TILE]
+    metal_ref[5 * cells + rows:5 * cells + rows + TILE] = jnp.zeros((TILE, lanes), jnp.float32)
+    metal_ref[5 * cells + rows:5 * cells + rows + 1] = wall_ref[across:across + 1]
     record = 5 * cells + rows + TILE
     apay_ref[face:face + record] = metal_ref[...]
+
+
+def corner_rows():
+    at, out = 0, []
+    for j in range(1, HALO):
+        out.append((j, at, HALO - j))
+        at += HALO - j
+    return out, at
 
 
 def edge_kernel(planes, lo_at, hi_at, starts, *refs):
     ylo_ref, yhi_ref = refs[0], refs[1]
     parts, (aedge_ref, bedge_ref) = refs[2:-2], refs[-2:]
-    used = FIELDS * HALO * HALO
-    span = up_to_tile(used)
+    corners, each = corner_rows()
     for odd in range(2):
 
         @pl.when(parity() == odd)
         def _():
-            for out, first in (
-                (aedge_ref, (planes - HALO) * (1 - odd)),
-                (bedge_ref, (planes - HALO) * odd),
-            ):
+            for out, last in ((aedge_ref, odd == 0), (bedge_ref, odd == 1)):
                 for f in range(FIELDS):
-                    for side, (ref, base) in enumerate(((ylo_ref, lo_at), (yhi_ref, hi_at))):
-                        at = side * span + f * HALO * HALO
-                        src = base + (f * planes + first) * HALO
-                        out[at:at + HALO * HALO] = ref[src:src + HALO * HALO]
-
-    for out in (aedge_ref, bedge_ref):
-        for side in range(2):
-            if span > used:
-                out[side * span + used:(side + 1) * span] = jnp.zeros(
-                    (span - used, ylo_ref.shape[1]), jnp.float32
-                )
-    at = 2 * span
+                    for j, first, count in corners:
+                        src = (f * planes + (planes - j if last else j - 1)) * HALO
+                        lo, hi = lo_at + src + HALO - count, hi_at + src
+                        at = f * each + first
+                        out[at:at + count] = ylo_ref[lo:lo + count]
+                        at += FIELDS * each
+                        out[at:at + count] = yhi_ref[hi:hi + count]
+
+    at = 2 * FIELDS * each
     for ref, (start, count) in zip(parts, starts):
         bedge_ref[at:at + count] = ref[start:start + count]
         at += count
@@ -203,49 +193,48 @@
 def assemble_kernel(dims, lo_at, hi_at, wall_at, *refs):
     axes, across = dims
     count_blk, count_sub = axes
-    state_ref, aface_ref, bface_ref, ylo_ref, yhi_ref, aedge_ref, bedge_ref = refs[:7]
-    wall_refs = refs[7:-5]
-    block_ref, inner_ref, outer_ref, table, seen = refs[-5:]
+    state_ref, apay_ref, bpay_ref, ylo_ref, yhi_ref, aedge_ref, bedge_ref = refs[:7]
+    wall_refs = refs[7:-6]
+    block_ref, own_ref, inner_ref, outer_ref, table, seen = refs[-6:]
     _, planes, rows, lanes = state_ref.shape
     deep, stride = block_ref.shape[1:3]
-    span = up_to_tile(FIELDS * HALO * HALO)
+    corners, each_corner = corner_rows()
     each = across + TILE
     blk, sub = lax.axis_index("blk"), lax.axis_index("sub")
-
-    def place(f, x, own, lo, hi):
-        block_ref[f, x + HALO, 0:rows] = own
-        block_ref[f, x + HALO, rows:rows + HALO] = hi
-        block_ref[f, x + HALO, stride - HALO:stride] = lo
 
     for f in range(FIELDS):
         for x in range(planes):
             at = (f * planes + x) * HALO
-            place(
-                f, x, state_ref[f, x],
-                ylo_ref[lo_at + at:lo_at + at + HALO], yhi_ref[hi_at + at:hi_at + at + HALO],
-            )
+            block_ref[f, x + HALO, 0:rows] = state_ref[f, x]
+            block_ref[f, x + HALO, rows:rows + HALO] = yhi_ref[hi_at + at:hi_at + at + HALO]
+            block_ref[f, x + HALO, stride - HALO:stride] = ylo_ref[lo_at + at:lo_at + at + HALO]
     for odd in range(2):
 
         @pl.when(parity() == odd)
         def _():
             for face_ref, edge_ref, above in (
-                (aface_ref, aedge_ref, odd == 0), (bface_ref, bedge_ref, odd == 1),
+                (apay_ref, aedge_ref, odd == 0), (bpay_ref, bedge_ref, odd == 1),
             ):
                 for f in range(FIELDS):
                     for j in range(HALO):
-                        at = (f * HALO + j) * HALO
-                        place(
-                            f, planes + j if above else j - HALO,
-                            face_ref[(f * HALO + j) * rows:(f * HALO + j + 1) * rows],
-                            edge_ref[at:at + HALO], edge_ref[span + at:span + at + HALO],
-                        )
+                        at = (f * HALO + j) * rows
+                        x = planes + HALO + j if above else j
+                        block_ref[f, x, 0:rows] = face_ref[at:at + rows]
+                    for j, first, count in corners:
+                        at = f * each_corner + first
+                        x = planes + HALO + j - 1 if above else HALO - j
+                        block_ref[f, x, stride - count:stride] = edge_ref[at:at + count]
+                        at += FIELDS * each_corner
+                        block_ref[f, x, rows:rows + count] = edge_ref[at:at + count]
 
     if wall_at is None:
         table = wall_refs[0]
     else:
         for ref, (start, flip_blk, flip_sub) in zip(wall_refs, wall_at):
             device = jnp.bitwise_xor(blk, flip_blk) * count_sub + jnp.bitwise_xor(sub, flip_sub)
-            table[pl.ds(pl.multiple_of(device * each, TILE), each)] = ref[start:start + each]
+            table[pl.ds(pl.multiple_of(device * each, TILE), across + 1)] = ref[
+                start:start + across + 1
+            ]
     devices = count_blk * count_sub
     walls = jnp.concatenate(
         [table[d * each:d * each + across] for d in range(devices)], axis=0
@@ -268,20 +257,28 @@
         rho, mx, my, mz, energy = [block_ref[f, x + HALO] for f in range(FIELDS)]
         pressure = (gamma_gas - 1.0) * (energy - 0.5 * (mx * mx + my * my + mz * mz) / rho)
         block_ref[FIELDS, x + HALO] = film_coeff * (pressure / rho - seen[...])
-    pick = iota((TILE, lanes), 0)
-    cell = iota((TILE, lanes), 1)
+    pick = iota((2 * TILE, lanes), 0)
+    cell = iota((2 * TILE, lanes), 1)
     chosen = (
-        ((pick == cell) & (pick < HALO))
-        | ((pick - HALO + lanes - HALO == cell) & (pick >= HALO) & (pick < 2 * HALO))
-    ).astype(jnp.float32)
+        ((pick == cell) & (pick < NEAR))
+        | ((pick - TILE + lanes - NEAR == cell) & (pick >= TILE) & (pick < TILE + NEAR))
+    ).astype(jnp.float32).astype(jnp.bfloat16)
     size = deep * stride
     upper = parity("grp") == 1
     for f in range(FIELDS + 1):
-        ends = dot(chosen, block_ref[f].reshape(size, lanes), 1, 1)
-        low, high = ends[0:HALO], ends[HALO:2 * HALO]
+        ends = sum(
+            lax.dot_general(
+                chosen, piece, (((1,), (1,)), ((), ())), preferred_element_type=jnp.float32
+            )
+            for piece in reversed(pieces_of(block_ref[f].reshape(size, lanes)))
+        )
+        own_ref[f * 2 * TILE:(f + 1) * 2 * TILE, 0:size] = ends
+        low, high = ends[0:HALO], ends[TILE + NEAR - HALO:TILE + NEAR]
         inner_ref[f * HALO:(f + 1) * HALO, 0:size] = jnp.where(upper, low, high)
         outer_ref[f * HALO:(f + 1) * HALO, 0:size] = jnp.where(upper, high, low)
     used = (FIELDS + 1) * HALO
+    if own_ref.shape[1] > size:
+        own_ref[:, size:] = jnp.zeros((own_ref.shape[0], own_ref.shape[1] - size), jnp.float32)
     for ref in (inner_ref, outer_ref):
         if ref.shape[1] > size:
             ref[:, size:] = jnp.zeros((ref.shape[0], ref.shape[1] - size), jnp.float32)
@@ -327,110 +324,91 @@
     return third_part * start + two_thirds * fresh
 
 
-def plane_stage(stage, src, block_ref, ends, put, prim, xface):
-    deep, stride, lanes = src.shape[1:]
-    lane = iota((stride, lanes), 1)
-    low, high = stage + 1, deep - 1 - stage
-    for x in range(low - 1, high + 1):
-        for k, value in enumerate(primitives([src[f, x] for f in range(FIELDS)])):
-            prim[k, x] = value
-
-    def cells(x, d):
-        return [src[f, x] for f in range(FIELDS)] + [
-            prim[d, x], prim[3 + d, x], prim[6, x], prim[7, x]
-        ]
-
-    for x in range(low, high + 1):
-        new = faces(0, cells(x - 1, 0), cells(x, 0))
-        for f in range(FIELDS):
-            xface[x % 2, f] = new[f]
-        if x == low:
-            continue
-        p = x - 1
-        change = [new[f] - xface[p % 2, f] for f in range(FIELDS)]
-        hi = cells(p, 1)
-        lo = [pltpu.roll(v, 1, axis=0) for v in hi]
-        face = faces(1, lo, hi)
-        change = [c + (pltpu.roll(v, stride - 1, axis=0) - v) for c, v in zip(change, face)]
-        hi = cells(p, 2)
-        lo = [pltpu.roll(v, 1, axis=1) for v in hi]
-        face = [jnp.where(lane == 0, 0.0, v) for v in faces(2, lo, hi)]
-        for f in range(FIELDS):
-            total = change[f] + (pltpu.roll(face[f], lanes - 1, axis=1) - face[f])
-            if ends is not None:
-                total = total + ends[f, p]
-            sink = block_ref[FIELDS, p] if f == FIELDS - 1 else None
-            put(f, p, advance(stage, src[f, p], total, block_ref[f, p], sink))
-
-
-def begin_kernel(block_ref, now_ref, prim, xface):
-    def put(f, p, value):
-        now_ref[f, p] = value
-
-    plane_stage(0, block_ref, block_ref, None, put, prim, xface)
-
-
-def fluid_kernel(
-    block_ref, now, inner_own, outer_own, inner_ref, outer_ref, out_ref,
-    prim, xface, ends, slab_base, slab, comb,
+def planes_kernel(block_ref, out_ref, now, prim, xface):
+    deep, _, _ = block_ref.shape[1:]
+    rows = out_ref.shape[2]
+    for stage in range(3):
+        src = block_ref if stage == 0 else now
+        low, high = stage + 1, deep - 1 - stage
+        for x in range(low - 1, high + 1):
+            for k, value in enumerate(primitives([src[f, x] for f in range(FIELDS)])):
+                prim[k, x] = value
+
+        def cells(x, d, src=src):
+            return [src[f, x] for f in range(FIELDS)] + [
+                prim[d, x], prim[3 + d, x], prim[6, x], prim[7, x]
+            ]
+
+        for x in range(low, high + 1):
+            new = faces(0, cells(x - 1, 0), cells(x, 0))
+            for f in range(FIELDS):
+                xface[x % 2, f] = new[f]
+            if x == low:
+                continue
+            p = x - 1
+            change = [new[f] - xface[p % 2, f] for f in range(FIELDS)]
+            for d, axis in ((1, 0), (2, 1)):
+                hi = cells(p, d)
+                lo = [pltpu.roll(v, 1, axis=axis) for v in hi]
+                face = faces(d, lo, hi)
+                last = hi[0].shape[axis] - 1
+                change = [c + (pltpu.roll(v, last, axis=axis) - v) for c, v in zip(change, face)]
+            for f in range(FIELDS):
+                sink = block_ref[FIELDS, p] if f == FIELDS - 1 else None
+                value = advance(stage, src[f, p], change[f], block_ref[f, p], sink)
+                if stage == 2:
+                    out_ref[f, p - HALO] = value[0:rows]
+                else:
+                    now[f, p] = value
+
+
+def ends_kernel(
+    stride, main_ref, own_ref, inner_ref, outer_ref, out_ref, slab_base, slab, comb
 ):
-    _, _, rows, lanes = out_ref.shape
-    deep, stride = block_ref.shape[1:3]
-    size = deep * stride
+    _, planes, rows, lanes = out_ref.shape
     wide = slab.shape[2]
-    group = TILE
+    half = slab.shape[1] // 2
     part = FIELDS * TILE
     source = iota((lanes, FIELDS * lanes), 0)
     target = iota((lanes, FIELDS * lanes), 1)
     field = lax.rem(source, part) // TILE
     end = lax.rem(source, TILE)
-    at_low = (end == 0) & (target == field * lanes) & (source < 3 * part)
-    at_high = (end == 1) & (target == field * lanes + lanes - 1) & (source < 3 * part)
-    spread = (at_high.astype(jnp.float32) - at_low.astype(jnp.float32)).astype(jnp.bfloat16)
+    spread = (
+        ((end < HALO) & (target == field * lanes + end))
+        | (
+            (end >= HALO) & (end < 2 * HALO)
+            & (target == field * lanes + lanes - 2 * HALO + end)
+        )
+    ) & (source < 3 * part)
+    spread = spread.astype(jnp.float32).astype(jnp.bfloat16)
     comb[...] = jnp.zeros(comb.shape, jnp.float32)
     slab_base[...] = jnp.zeros(slab_base.shape, jnp.float32)
     upper = parity("grp") == 1
     for f in range(FIELDS + 1):
-        at = slice(f * HALO, (f + 1) * HALO)
-        inner_z, outer_z, inner, outer = (
-            ref[at] for ref in (inner_own, outer_own, inner_ref, outer_ref)
-        )
+        inner, outer = (ref[f * HALO:(f + 1) * HALO] for ref in (inner_ref, outer_ref))
+        at = f * 2 * TILE
         slab_base[f, 0:HALO] = jnp.where(upper, inner, outer)
-        slab_base[f, HALO:2 * HALO] = jnp.where(upper, inner_z, outer_z)
-        slab_base[f, group:group + HALO] = jnp.where(upper, outer_z, inner_z)
-        slab_base[f, group + HALO:group + 2 * HALO] = jnp.where(upper, outer, inner)
-    for f in range(FIELDS):
-        slab[f] = slab_base[f]
-
-    first_row = lax.rem(iota((2 * TILE, wide), 1), stride) == 0
-    last_row = lax.rem(iota((2 * TILE, wide), 1), stride) == stride - 1
+        slab_base[f, HALO:HALO + NEAR] = own_ref[at:at + NEAR]
+        slab_base[f, half:half + NEAR] = own_ref[at + TILE:at + TILE + NEAR]
+        slab_base[f, half + NEAR:half + NEAR + HALO] = jnp.where(upper, outer, inner)
+
+    first_row = lax.rem(iota((2 * half, wide), 1), stride) == 0
+    last_row = lax.rem(iota((2 * half, wide), 1), stride) == stride - 1
 
     def lane_roll(v, shift):
         return pltpu.roll(v, shift % wide, axis=1)
 
-    def put(f, p, value):
-        if stage == 2:
-            out_ref[f, p - HALO] = value[0:rows]
-        else:
-            now[f, p] = value
-
     for stage in range(3):
-        u = [slab[f] for f in range(FIELDS)]
+        u = [(slab_base if stage == 0 else slab)[f] for f in range(FIELDS)]
         q = primitives(u)
         hi = u + [q[2], q[5], q[6], q[7]]
-        lo = [pltpu.roll(v, 1, axis=0) for v in hi]
-        zface = faces(2, lo, hi)
-        for f in range(FIELDS):
-            comb[f * TILE:f * TILE + 1] = zface[f][HALO:HALO + 1]
-            comb[f * TILE + 1:f * TILE + 2] = zface[f][group + HALO:group + HALO + 1]
-        change = [pltpu.roll(v, 2 * TILE - 1, axis=0) - v for v in zface]
+        face = faces(2, [pltpu.roll(v, 1, axis=0) for v in hi], hi)
+        change = [pltpu.roll(v, 2 * half - 1, axis=0) - v for v in face]
         hi = u + [q[0], q[3], q[6], q[7]]
         face = faces(0, [lane_roll(v, stride) for v in hi], hi)
         change = [c + (lane_roll(v, -stride) - v) for c, v in zip(change, face)]
         hi = u + [q[1], q[4], q[6], q[7]]
-        lo = [
-            jnp.where(first_row, lane_roll(v, 1 - stride), lane_roll(v, 1)) for v in hi
-        ]
+        lo = [jnp.where(first_row, lane_roll(v, 1 - stride), lane_roll(v, 1)) for v in hi]
         face = faces(1, lo, hi)
         change = [
             c + (jnp.where(last_row, lane_roll(v, stride - 1), lane_roll(v, -1)) - v)
@@ -439,25 +417,28 @@
         for f in range(FIELDS):
             sink = slab_base[FIELDS] if f == FIELDS - 1 else None
             slab[f] = advance(stage, u[f], change[f], slab_base[f], sink)
-        whole = comb[0:part]
-        for k in range(2):
-            piece = whole.astype(jnp.bfloat16).astype(jnp.float32)
-            comb[k * part:(k + 1) * part] = piece
-            whole = whole - piece
-        comb[2 * part:3 * part] = whole
-        turned = jnp.transpose(comb[...]).astype(jnp.bfloat16)
-        moved = lax.dot_general(
-            turned, spread, (((1,), (0,)), ((), ())), preferred_element_type=jnp.float32
-        )
-        for f in range(FIELDS):
-            ends[f] = moved[0:size, f * lanes:(f + 1) * lanes].reshape(deep, stride, lanes)
-
-        if stage == 0:
-            for p in range(1, deep - 1):
-                for f in range(FIELDS):
-                    now[f, p] = now[f, p] - (0.5 * time_step) * ends[f, p]
-        else:
-            plane_stage(stage, now, block_ref, ends, put, prim, xface)
+
+    for f in range(FIELDS):
+        comb[f * TILE:f * TILE + HALO] = slab[f, HALO:2 * HALO]
+        first = half + NEAR - HALO
+        comb[f * TILE + HALO:f * TILE + 2 * HALO] = slab[f, first:first + HALO]
+    whole = comb[0:part]
+    for k in range(2):
+        piece = whole.astype(jnp.bfloat16).astype(jnp.float32)
+        comb[k * part:(k + 1) * part] = piece
+        whole = whole - piece
+    comb[2 * part:3 * part] = whole
+    turned = jnp.transpose(comb[...]).astype(jnp.bfloat16)
+    moved = lax.dot_general(
+        turned[HALO * stride:(HALO + planes) * stride], spread, (((1,), (0,)), ((), ())),
+        preferred_element_type=jnp.float32,
+    )
+    lane = iota((rows, lanes), 1)
+    near = (lane < HALO) | (lane >= lanes - HALO)
+    for f in range(FIELDS):
+        for x in range(planes):
+            edge = moved[x * stride:x * stride + rows, f * lanes:(f + 1) * lanes]
+            out_ref[f, x] = jnp.where(near, edge, main_ref[f, x])
 
 
 def metal_kernel(dims, rows, where, order, *refs):
@@ -616,15 +597,15 @@
     count_blk, count_sub = lax.axis_size("blk"), lax.axis_size("sub")
     devices = count_blk * count_sub
     cells = along * across
-    edge = up_to_tile(FIELDS * planes * HALO)
-    each = across + TILE
+    edge = FIELDS * planes * HALO
+    each = across + 1
     record = 5 * cells + rows + TILE
 
     face = FIELDS * HALO * rows
     state, yedge, apay, bpay, metal, wall = call(
         pack_kernel,
         [
-            f32(FIELDS, planes, rows, lanes), f32(2, edge, lanes),
+            f32(FIELDS, planes, rows, lanes), f32(2 * edge, lanes),
             f32(face + record, lanes), f32(face, lanes),
             f32(record, lanes), f32(each, lanes),
         ],
@@ -642,17 +623,17 @@
         ],
     )
     paired = count_blk == 4 and count_sub == 2
-    span = up_to_tile(FIELDS * HALO * HALO)
+    span = FIELDS * corner_rows()[1]
     bpay = outer(bpay)
     if paired:
         wall_a = swap(wall, "blk", 1)
-        ypay = jnp.concatenate([yedge.reshape(2 * edge, lanes), wall, wall_a], axis=0)
+        ypay = jnp.concatenate([yedge, wall, wall_a], axis=0)
         yrecv = swap(ypay, "sub", 1)
         ylo, yhi, lo_at, hi_at = yrecv, yrecv, edge, 0
         parts = [wall, wall_a, yrecv]
         starts = [(0, each), (0, each), (2 * edge, 2 * each)]
     else:
-        ylo, yhi, lo_at, hi_at = ring(yedge[1], "sub", 1), ring(yedge[0], "sub", -1), 0, 0
+        ylo, yhi, lo_at, hi_at = ring(yedge[edge:], "sub", 1), ring(yedge[:edge], "sub", -1), 0, 0
         parts, starts = [], []
     apay = swap(apay, "blk", 1)
     aedge, bedge = call(
@@ -667,41 +648,44 @@
         wall_at = [(0, 0, 0), (0, 1, 0), (2 * edge, 0, 1), (2 * edge + each, 1, 1)]
         wall_at += [(2 * span + k * each, 3 ^ (k & 1), k >> 1) for k in range(4)]
     else:
+        wall = jnp.pad(wall, ((0, across + TILE - each), (0, 0)))
         walls = [lax.all_gather(wall, ("blk", "sub"), axis=0, tiled=True)]
         wall_at = None
     deep, stride = planes + 2 * HALO, rows + TILE
     ends_rows = up_to_tile((FIELDS + 1) * HALO)
     wide_lanes = -(-deep * stride // lanes) * lanes
-    block, inner_z, outer_z = call(
+    block, own_z, inner_z, outer_z = call(
         functools.partial(
             assemble_kernel, ((count_blk, count_sub), across), lo_at, hi_at, wall_at
         ),
         [
             f32(FIELDS + 1, deep, stride, lanes),
+            f32((FIELDS + 1) * 2 * TILE, wide_lanes),
             f32(ends_rows, wide_lanes),
             f32(ends_rows, wide_lanes),
         ],
         [state, apay, bpay, ylo, yhi, aedge, bedge, *walls],
-        scratch=[(devices * each, lanes), (stride, lanes)],
+        scratch=[(devices * (across + TILE), lanes), (stride, lanes)],
     )
     inner_got = swap(inner_z, "grp", 1)
     outer_got = outer(outer_z, "grp")
-    whole = (FIELDS, deep, stride, lanes)
-    work = [(8, deep, stride, lanes), (2, FIELDS, stride, lanes)]
-    first = call(begin_kernel, f32(*whole), [block], scratch=work)
+    planes_next = call(
+        planes_kernel,
+        f32(FIELDS, planes, rows, lanes),
+        [block],
+        scratch=[
+            (FIELDS, deep, stride, lanes), (8, deep, stride, lanes), (2, FIELDS, stride, lanes)
+        ],
+    )
 
     if paired:
         near_y = swap(metal, "sub", 1)
         far = swap(metal, "blk", 2)
-        pairs = [
-            (b * count_sub + s, (b ^ 2) * count_sub + (s ^ 1))
-            for b in range(count_blk) for s in range(count_sub)
-        ]
-        far_y = lax.ppermute(metal, ("blk", "sub"), pairs)
-        mates = swap(jnp.concatenate([near_y, far_y, far], axis=0), "blk", 1)
-        pieces = [metal, apay, far, near_y, far_y, mates]
+        far_y = swap(near_y, "blk", 2)
+        mates = swap(jnp.concatenate([near_y, far, far_y], axis=0), "blk", 1)
+        pieces = [metal, apay, near_y, far, far_y, mates]
         where = [(0, 0), (1, face), (2, 0), (3, 0), (4, 0)] + [(5, k * record) for k in range(3)]
-        order = [(0, 0), (1, 0), (2, 0), (0, 1), (2, 1), (1, 1), (3, 1), (3, 0)]
+        order = [(0, 0), (1, 0), (0, 1), (2, 0), (2, 1), (1, 1), (3, 0), (3, 1)]
     else:
         held, order = metal, [(0, 0)]
         steps = [("blk", flip) for flip in flips(count_blk)]
@@ -727,13 +711,13 @@
             field, field, field, field, (devices * across, lanes), (TILE, devices * rows), (devices * rows, lanes),
         ],
     )
+    slab = 2 * -(-(NEAR + HALO) // (TILE // 2)) * (TILE // 2)
     fluid_next = call(
-        fluid_kernel,
+        functools.partial(ends_kernel, stride),
         f32(FIELDS, planes, rows, lanes),
-        [block, first, inner_z, outer_z, inner_got, outer_got],
+        [planes_next, own_z, inner_got, outer_got],
         scratch=[
-            *work, whole, (FIELDS + 1, 2 * TILE, wide_lanes), (FIELDS, 2 * TILE, wide_lanes),
-            (lanes, wide_lanes),
+            (FIELDS + 1, slab, wide_lanes), (FIELDS, slab, wide_lanes), (lanes, wide_lanes)
         ],
     )
     return (fluid_next, metal_next)

time: 42.7 us -> 40.9 us (0.958)
  waiting for transfers between devices: 17 us -> 14 us
  starting transfers between devices: 14 us -> 15.2 us
    ppermute x8 -> x9, starting transfers between devices: 5.53 us -> 11.6 us  [swap(): return lax.ppermute(value, axis, [(i, i ^ flip) for i in range(count)])]
    ppermute x1 -> x0, waiting for transfers between devices: 4.84 us -> none  [shards(): far_y = lax.ppermute(metal, ('blk', 'sub'), pairs)]
    ppermute x8 -> x9, waiting for transfers between devices: 7.81 us -> 11.9 us  [swap(): return lax.ppermute(value, axis, [(i, i ^ flip) for i in range(count)])]
    ppermute x1 -> x0, starting transfers between devices: 3.99 us -> none  [shards(): far_y = lax.ppermute(metal, ('blk', 'sub'), pairs)]
    ppermute x3, waiting for transfers between devices: 4.31 us -> 2.04 us  [outer(): return lax.ppermute(value, axis, pairs)]
    ppermute x3, starting transfers between devices: 4.44 us -> 3.68 us  [outer(): return lax.ppermute(value, axis, pairs)]
  transfers between devices with their start and end apart: 12 -> 12, of which waited for: 7 -> 7; matrix products, arithmetic and copies ran while one was open for 0% -> 0% of each run, Pallas kernels for 17% -> 18%
where the time goes in v5:
time: 40.9 us; the launch traced here: 40.7 us
  starting transfers between devices  15.2 us (37%)
  waiting for transfers between devices  14 us (34%)
  Pallas kernels  10.8 us (26%)
  between operations  0.7 us (2%)
    ppermute x9, waiting for transfers between devices, swap(): return lax.ppermute(value, axis, [(i, i ^ flip) for i in range(count)])  11.9 us
    ppermute x9, starting transfers between devices, swap(): return lax.ppermute(value, axis, [(i, i ^ flip) for i in range(count)])  11.6 us
    pallas_call x6, Pallas kernels, call(): pl.pallas_call(body, out_shape=out, in_specs=[pl.BlockSpec(memory_space=p...  10.8 us
    ppermute x3, starting transfers between devices, outer(): return lax.ppermute(value, axis, pairs)  3.68 us
    ppermute x3, waiting for transfers between devices, outer(): return lax.ppermute(value, axis, pairs)  2.04 us
  transfers between devices with their start and end apart: 12, of which 7 were waited for; matrix products, arithmetic and copies ran while one was open for 0% of the time, Pallas kernels for 18%

profile of v5, /device:TPU:0, one launch (start us, length us, event | category | flops | bytes accessed | tf_op | source)
XLA Modules:
  0.0 40.7 jit_solution(2342653958736862210)
XLA Ops:
  0.6 1.2 %shard_map.95 = (f32[5,4,32,128]{3,2,1,0:T(8,128)S(1)}, f32[120,128]{1,0:T(8,128)S(1)}, f32[840,128]{1,0:T(8,128)S(1)}, f32[480,128]{1,0:T(8,128)S(1)}, f32[360,128]{1,0:T(8,128)S(1)}, /*index=5*/f32[9,128]{1,0:T(8,128)S(1)}) custom-call(f32[4,32,128]{2,1,0:T(8,128)} %rho_hbm.1, f32[3,4,32,128]{3,2,1,0:T(8,128)} %vel_hbm.1, f32[4,32,128]{2,1,0:T(8,128)} %pre_hbm.1, ...), custom_call_target="tpu_custom_call" | custom-call | flops 100000 | bytes 100000 | tf_op jit(solution)/shard_map/pallas_call | solution.py:47
  1.8 3.1 %collective-permute-start.8 = (f32[360,128]{1,0:T(8,128)S(1)}, f32[360,128]{1,0:T(8,128)S(1)}, u32[]{:S(2)}, u32[]{:S(2)}) collective-permute-start(f32[360,128]{1,0:T(8,128)S(1)} %get-tuple-element.25.refs_0_), channel_id=1, source_target_pairs={{0,1},{1,0},{2,3},{3,2},{4,5},{5,4},{6,7},{7,6},{8,9},{9,8},{10,11... | collective-permute-start | bytes 552968 | tf_op jit(solution)/shard_map/ppermute | solution.py:567
  4.9 1.5 %collective-permute-start.9 = (f32[360,128]{1,0:T(8,128)S(1)}, f32[360,128]{1,0:T(8,128)S(1)}, u32[]{:S(2)}, u32[]{:S(2)}) collective-permute-start(f32[360,128]{1,0:T(8,128)S(1)} %get-tuple-element.25.refs_0_), channel_id=1, source_target_pairs={{0,4},{2,6},{4,0},{6,2},{1,5},{3,7},{5,1},{7,3},{8,12},{10,14},{12... | collective-permute-start | bytes 552968 | tf_op jit(solution)/shard_map/ppermute | solution.py:567
  6.4 3.1 %collective-permute-done.8.refs_2_ = f32[360,128]{1,0:T(8,128)S(1)} collective-permute-done((f32[360,128]{1,0:T(8,128)S(1)}, f32[360,128]{1,0:T(8,128)S(1)}, u32[]{:S(2)}, u32[]{:S(2)}) %collective-permute-start.8) | collective-permute-done | bytes 184352 | tf_op jit(solution)/shard_map/ppermute | solution.py:567
  9.5 1.7 %collective-permute-start.10 = (f32[360,128]{1,0:T(8,128)S(1)}, f32[360,128]{1,0:T(8,128)S(1)}, u32[]{:S(2)}, u32[]{:S(2)}) collective-permute-start(f32[360,128]{1,0:T(8,128)S(1)} %collective-permute-done.8.refs_2_), channel_id=1, source_target_pairs={{0,4},{2,6},{4,0},{6,2},{1,5},{3,7},{5,1},{7,3},{8,12},{10,14},{12... | collective-permute-start | bytes 552968 | tf_op jit(solution)/shard_map/ppermute | solution.py:567
  11.2 0.0 collective-permute-done.9.refs_3_
  11.2 4.1 %collective-permute-done.10.refs_4_ = f32[360,128]{1,0:T(8,128)S(1)} collective-permute-done((f32[360,128]{1,0:T(8,128)S(1)}, f32[360,128]{1,0:T(8,128)S(1)}, u32[]{:S(2)}, u32[]{:S(2)}) %collective-permute-start.10) | collective-permute-done | bytes 184352 | tf_op jit(solution)/shard_map/ppermute | solution.py:567
  15.4 0.1 collective-permute-start.11
  15.4 0.5 %collective-permute-start = (f32[840,128]{1,0:T(8,128)S(1)}, f32[840,128]{1,0:T(8,128)S(1)}, u32[]{:S(2)}, u32[]{:S(2)}) collective-permute-start(f32[840,128]{1,0:T(8,128)S(1)} %get-tuple-element.15), channel_id=1, source_target_pairs={{0,2},{2,0},{4,6},{6,4},{1,3},{3,1},{5,7},{7,5},{8,10},{10,8},{12,... | collective-permute-start | bytes 1290248 | tf_op jit(solution)/shard_map/ppermute | solution.py:567
  15.9 1.1 %collective-permute-start.1 = (f32[480,128]{1,0:T(8,128)S(1)}, f32[480,128]{1,0:T(8,128)S(1)}, u32[]{:S(2)}, u32[]{:S(2)}) collective-permute-start(f32[480,128]{1,0:T(8,128)S(1)} %get-tuple-element.16), channel_id=1, source_target_pairs={{0,6},{2,4},{4,2},{6,0},{1,7},{3,5},{5,3},{7,1},{8,14},{10,12},{12... | collective-permute-start | bytes 737288 | tf_op jit(solution)/shard_map/ppermute | solution.py:573
  17.1 0.4 %collective-permute-start.2 = (f32[9,128]{1,0:T(8,128)S(1)}, f32[9,128]{1,0:T(8,128)S(1)}, u32[]{:S(2)}, u32[]{:S(2)}) collective-permute-start(f32[9,128]{1,0:T(8,128)S(1)} %get-tuple-element.18.refs_2_.refs_7_), channel_id=1, source_target_pairs={{0,2},{2,0},{4,6},{6,4},{1,3},{3,1},{5,7},{7,5},{8,10},{10,8},{12,... | collective-permute-start | bytes 13832 | tf_op jit(solution)/shard_map/ppermute | solution.py:567
  17.5 0.8 %collective-permute-done.2.refs_3_.refs_8_ = f32[9,128]{1,0:T(8,128)S(1)} collective-permute-done((f32[9,128]{1,0:T(8,128)S(1)}, f32[9,128]{1,0:T(8,128)S(1)}, u32[]{:S(2)}, u32[]{:S(2)}) %collective-permute-start.2) | collective-permute-done | bytes 4640 | tf_op jit(solution)/shard_map/ppermute | solution.py:567
  18.4 1.6 %collective-permute-start.3 = (f32[138,128]{1,0:T(8,128)S(1)}, f32[138,128]{1,0:T(8,128)S(1)}, u32[]{:S(2)}, u32[]{:S(2)}) collective-permute-start(f32[138,128]{1,0:T(8,128)S(1)} %pad_maximum_fusion.1), channel_id=1, source_target_pairs={{0,1},{1,0},{2,3},{3,2},{4,5},{5,4},{6,7},{7,6},{8,9},{9,8},{10,11... | collective-permute-start | bytes 211976 | tf_op jit(solution)/shard_map/ppermute | solution.py:567
  19.9 3.0 %collective-permute-done.3.refs_0_.refs_1_.refs_4_.refs_3_.refs_9_.refs_10_ = f32[138,128]{1,0:T(8,128)S(1)} collective-permute-done((f32[138,128]{1,0:T(8,128)S(1)}, f32[138,128]{1,0:T(8,128)S(1)}, u32[]{:S(2)}, u32[]{:S(2)}) %collective-permute-start.3) | collective-permute-done | bytes 70688 | tf_op jit(solution)/shard_map/ppermute | solution.py:567
  23.0 0.1 collective-permute-start.5
  23.0 1.1 %collective-permute-start.4 = (f32[30,128]{1,0:T(8,128)S(1)}, f32[30,128]{1,0:T(8,128)S(1)}, u32[]{:S(2)}, u32[]{:S(2)}) collective-permute-start(f32[30,128]{1,0:T(8,128)S(1)} %get-tuple-element.19), channel_id=1, source_target_pairs={{0,2},{2,0},{4,6},{6,4},{1,3},{3,1},{5,7},{7,5},{8,10},{10,8},{12,... | collective-permute-start | bytes 46088 | tf_op jit(solution)/shard_map/ppermute | solution.py:567
  24.1 0.8 %collective-permute-done.4.refs_5_ = f32[30,128]{1,0:T(8,128)S(1)} collective-permute-done((f32[30,128]{1,0:T(8,128)S(1)}, f32[30,128]{1,0:T(8,128)S(1)}, u32[]{:S(2)}, u32[]{:S(2)}) %collective-permute-start.4) | collective-permute-done | bytes 15392 | tf_op jit(solution)/shard_map/ppermute | solution.py:567
  24.9 1.5 %collective-permute-done.5.refs_6_.refs_11_.refs_12_.refs_13_.refs_14_ = f32[66,128]{1,0:T(8,128)S(1)} collective-permute-done((f32[66,128]{1,0:T(8,128)S(1)}, f32[66,128]{1,0:T(8,128)S(1)}, u32[]{:S(2)}, u32[]{:S(2)}) %collective-permute-start.5) | collective-permute-done | bytes 33824 | tf_op jit(solution)/shard_map/ppermute | solution.py:573
  26.5 0.0 collective-permute-done.1.refs_2_
  26.5 0.0 collective-permute-done.refs_1_
  26.5 1.0 %shard_map.97 = (f32[6,10,40,128]{3,2,1,0:T(8,128)S(1)}, f32[96,512]{1,0:T(8,128)S(1)}, f32[24,512]{1,0:T(8,128)S(1)}, f32[24,512]{1,0:T(8,128)S(1)}) custom-call(f32[5,4,32,128]{3,2,1,0:T(8,128)S(1)} %get-tuple-element.14.refs_0_, f32[840,128]{1,0:T(8,128)S(1)} %collective-permute-done.refs_1_, f32[480,128]{1,0:T(8,128)S(1)} %collective-permute-done.1.refs_2_, ...), custom_call_target="tpu_custom_call" | custom-call | flops 100000 | bytes 100000 | tf_op jit(solution)/shard_map/pallas_call | solution.py:47
  27.5 1.6 %collective-permute-start.6 = (f32[24,512]{1,0:T(8,128)S(1)}, f32[24,512]{1,0:T(8,128)S(1)}, u32[]{:S(2)}, u32[]{:S(2)}) collective-permute-start(f32[24,512]{1,0:T(8,128)S(1)} %get-tuple-element.23), channel_id=1, source_target_pairs={{0,8},{8,0},{16,24},{24,16},{1,9},{9,1},{17,25},{25,17},{2,10},{10... | collective-permute-start | bytes 147464 | tf_op jit(solution)/shard_map/ppermute | solution.py:567
  29.1 2.5 %collective-permute-start.7 = (f32[24,512]{1,0:T(8,128)S(1)}, f32[24,512]{1,0:T(8,128)S(1)}, u32[]{:S(2)}, u32[]{:S(2)}) collective-permute-start(f32[24,512]{1,0:T(8,128)S(1)} %get-tuple-element.24), channel_id=1, source_target_pairs={{0,24},{8,16},{16,8},{24,0},{1,25},{9,17},{17,9},{25,1},{2,26},{10... | collective-permute-start | bytes 147464 | tf_op jit(solution)/shard_map/ppermute | solution.py:573
  31.6 2.9 %shard_map.98.main_ref = f32[5,4,32,128]{3,2,1,0:T(8,128)S(1)} custom-call(f32[6,10,40,128]{3,2,1,0:T(8,128)S(1)} %get-tuple-element.21.block_ref), custom_call_target="tpu_custom_call" | custom-call | flops 100000 | bytes 100000 | tf_op jit(solution)/shard_map/pallas_call | solution.py:47
  34.5 0.0 collective-permute-done.6.inner_ref
  34.5 0.5 %collective-permute-done.7.outer_ref = f32[24,512]{1,0:T(8,128)S(1)} collective-permute-done((f32[24,512]{1,0:T(8,128)S(1)}, f32[24,512]{1,0:T(8,128)S(1)}, u32[]{:S(2)}, u32[]{:S(2)}) %collective-permute-start.7) | collective-permute-done | bytes 49184 | tf_op jit(solution)/shard_map/ppermute | solution.py:573
  35.0 3.2 %shard_map.99 = f32[5,4,32,128]{3,2,1,0:T(8,128)} custom-call(f32[5,4,32,128]{3,2,1,0:T(8,128)S(1)} %shard_map.98.main_ref, f32[96,512]{1,0:T(8,128)S(1)} %get-tuple-element.22.own_ref, f32[24,512]{1,0:T(8,128)S(1)} %collective-permute-done.6.inner_ref, f32[24,512]{1,0:T(8,128)S(1)} %collective-permute-done.7.outer_ref), custom_call_target="tpu_custom_call" | custom-call | flops 100000 | bytes 100000 | tf_op jit(solution)/shard_map/pallas_call | solution.py:47
  38.2 0.0 collective-permute-done.11.refs_5_
  38.2 2.5 %shard_map.100 = f32[8,8,128]{2,1,0:T(8,128)} custom-call(f32[360,128]{1,0:T(8,128)S(1)} %get-tuple-element.25.refs_0_, f32[840,128]{1,0:T(8,128)S(1)} %collective-permute-done.refs_1_, f32[360,128]{1,0:T(8,128)S(1)} %collective-permute-done.8.refs_2_, f32[360,128]{1,0:T(8,128)S(1)} %collective-permute-done.9.refs_3_, ...), custom_call_target="tpu_custom_call" | custom-call | flops 100000 | bytes 100000 | tf_op jit(solution)/shard_map/pallas_call | solution.py:47
  (3 shorter events, 0.1 us)
Async XLA Ops:
  1.8 7.7 %collective-permute-start.8 = (f32[360,128]{1,0:T(8,128)S(1)}, f32[360,128]{1,0:T(8,128)S(1)}, u32[]{:S(2)}, u32[]{:S(2)}) collective-permute-start(f32[360,128]{1,0:T(8,128)S(1)} %get-tuple-element.25.refs_0_), channel_id=1, source_target_pairs={{0,1},{1,0},{2,3},{3,2},{4,5},{5,4},{6,7},{7,6},{8,9},{9,8},{10,11... | collective-permute-start | bytes 552968 | tf_op jit(solution)/shard_map/ppermute | solution.py:567
  4.9 6.4 %collective-permute-start.9 = (f32[360,128]{1,0:T(8,128)S(1)}, f32[360,128]{1,0:T(8,128)S(1)}, u32[]{:S(2)}, u32[]{:S(2)}) collective-permute-start(f32[360,128]{1,0:T(8,128)S(1)} %get-tuple-element.25.refs_0_), channel_id=1, source_target_pairs={{0,4},{2,6},{4,0},{6,2},{1,5},{3,7},{5,1},{7,3},{8,12},{10,14},{12... | collective-permute-start | bytes 552968 | tf_op jit(solution)/shard_map/ppermute | solution.py:567
  9.5 5.8 %collective-permute-start.10 = (f32[360,128]{1,0:T(8,128)S(1)}, f32[360,128]{1,0:T(8,128)S(1)}, u32[]{:S(2)}, u32[]{:S(2)}) collective-permute-start(f32[360,128]{1,0:T(8,128)S(1)} %collective-permute-done.8.refs_2_), channel_id=1, source_target_pairs={{0,4},{2,6},{4,0},{6,2},{1,5},{3,7},{5,1},{7,3},{8,12},{10,14},{12... | collective-permute-start | bytes 552968 | tf_op jit(solution)/shard_map/ppermute | solution.py:567
  15.4 22.9 %collective-permute-start.11 = (f32[1080,128]{1,0:T(8,128)S(1)}, f32[1080,128]{1,0:T(8,128)S(1)}, u32[]{:S(2)}, u32[]{:S(2)}) collective-permute-start(f32[1080,128]{1,0:T(8,128)S(1)} %pad_maximum_fusion), channel_id=1, source_target_pairs={{0,2},{2,0},{4,6},{6,4},{1,3},{3,1},{5,7},{7,5},{8,10},{10,8},{12,... | collective-permute-start | bytes 1658888 | tf_op jit(solution)/shard_map/ppermute | solution.py:567
  15.4 11.0 %collective-permute-start = (f32[840,128]{1,0:T(8,128)S(1)}, f32[840,128]{1,0:T(8,128)S(1)}, u32[]{:S(2)}, u32[]{:S(2)}) collective-permute-start(f32[840,128]{1,0:T(8,128)S(1)} %get-tuple-element.15), channel_id=1, source_target_pairs={{0,2},{2,0},{4,6},{6,4},{1,3},{3,1},{5,7},{7,5},{8,10},{10,8},{12,... | collective-permute-start | bytes 1290248 | tf_op jit(solution)/shard_map/ppermute | solution.py:567
  15.9 10.5 %collective-permute-start.1 = (f32[480,128]{1,0:T(8,128)S(1)}, f32[480,128]{1,0:T(8,128)S(1)}, u32[]{:S(2)}, u32[]{:S(2)}) collective-permute-start(f32[480,128]{1,0:T(8,128)S(1)} %get-tuple-element.16), channel_id=1, source_target_pairs={{0,6},{2,4},{4,2},{6,0},{1,7},{3,5},{5,3},{7,1},{8,14},{10,12},{12... | collective-permute-start | bytes 737288 | tf_op jit(solution)/shard_map/ppermute | solution.py:573
  17.1 1.3 %collective-permute-start.2 = (f32[9,128]{1,0:T(8,128)S(1)}, f32[9,128]{1,0:T(8,128)S(1)}, u32[]{:S(2)}, u32[]{:S(2)}) collective-permute-start(f32[9,128]{1,0:T(8,128)S(1)} %get-tuple-element.18.refs_2_.refs_7_), channel_id=1, source_target_pairs={{0,2},{2,0},{4,6},{6,4},{1,3},{3,1},{5,7},{7,5},{8,10},{10,8},{12,... | collective-permute-start | bytes 13832 | tf_op jit(solution)/shard_map/ppermute | solution.py:567
  18.4 4.6 %collective-permute-start.3 = (f32[138,128]{1,0:T(8,128)S(1)}, f32[138,128]{1,0:T(8,128)S(1)}, u32[]{:S(2)}, u32[]{:S(2)}) collective-permute-start(f32[138,128]{1,0:T(8,128)S(1)} %pad_maximum_fusion.1), channel_id=1, source_target_pairs={{0,1},{1,0},{2,3},{3,2},{4,5},{5,4},{6,7},{7,6},{8,9},{9,8},{10,11... | collective-permute-start | bytes 211976 | tf_op jit(solution)/shard_map/ppermute | solution.py:567
  23.0 3.5 %collective-permute-start.5 = (f32[66,128]{1,0:T(8,128)S(1)}, f32[66,128]{1,0:T(8,128)S(1)}, u32[]{:S(2)}, u32[]{:S(2)}) collective-permute-start(f32[66,128]{1,0:T(8,128)S(1)} %get-tuple-element.20), channel_id=1, source_target_pairs={{0,6},{2,4},{4,2},{6,0},{1,7},{3,5},{5,3},{7,1},{8,14},{10,12},{12... | collective-permute-start | bytes 101384 | tf_op jit(solution)/shard_map/ppermute | solution.py:573
  23.0 1.9 %collective-permute-start.4 = (f32[30,128]{1,0:T(8,128)S(1)}, f32[30,128]{1,0:T(8,128)S(1)}, u32[]{:S(2)}, u32[]{:S(2)}) collective-permute-start(f32[30,128]{1,0:T(8,128)S(1)} %get-tuple-element.19), channel_id=1, source_target_pairs={{0,2},{2,0},{4,6},{6,4},{1,3},{3,1},{5,7},{7,5},{8,10},{10,8},{12,... | collective-permute-start | bytes 46088 | tf_op jit(solution)/shard_map/ppermute | solution.py:567
  27.5 7.0 %collective-permute-start.6 = (f32[24,512]{1,0:T(8,128)S(1)}, f32[24,512]{1,0:T(8,128)S(1)}, u32[]{:S(2)}, u32[]{:S(2)}) collective-permute-start(f32[24,512]{1,0:T(8,128)S(1)} %get-tuple-element.23), channel_id=1, source_target_pairs={{0,8},{8,0},{16,24},{24,16},{1,9},{9,1},{17,25},{25,17},{2,10},{10... | collective-permute-start | bytes 147464 | tf_op jit(solution)/shard_map/ppermute | solution.py:567
  29.1 5.9 %collective-permute-start.7 = (f32[24,512]{1,0:T(8,128)S(1)}, f32[24,512]{1,0:T(8,128)S(1)}, u32[]{:S(2)}, u32[]{:S(2)}) collective-permute-start(f32[24,512]{1,0:T(8,128)S(1)} %get-tuple-element.24), channel_id=1, source_target_pairs={{0,24},{8,16},{16,8},{24,0},{1,25},{9,17},{17,9},{25,1},{2,26},{10... | collective-permute-start | bytes 147464 | tf_op jit(solution)/shard_map/ppermute | solution.py:573

commit v6 on v5

--- a/solution.py
+++ b/solution.py
@@ -34,7 +34,7 @@
     return total
 
 
-def call(body, out, inputs, hbm=(), cost=100_000, scratch=()):
+def call(body, out, inputs, hbm=(), hbm_out=(), cost=100_000, scratch=()):
     inputs = [
         pltpu.with_memory_space_constraint(x, pltpu.HBM) if i in hbm else x
         for i, x in enumerate(inputs)
@@ -51,7 +51,13 @@
             pl.BlockSpec(memory_space=pltpu.HBM if i in hbm else pltpu.VMEM)
             for i in range(len(inputs))
         ],
-        out_specs=jax.tree.map(lambda _: pl.BlockSpec(memory_space=pltpu.VMEM), out),
+        out_specs=jax.tree.unflatten(
+            jax.tree.structure(out),
+            [
+                pl.BlockSpec(memory_space=pltpu.HBM if i in hbm_out else pltpu.VMEM)
+                for i in range(len(jax.tree.leaves(out)))
+            ],
+        ),
         scratch_shapes=[
             pltpu.VMEM(x, jnp.float32) if isinstance(x, tuple) else x for x in scratch
         ],
@@ -363,11 +369,12 @@
 
 
 def ends_kernel(
-    stride, main_ref, own_ref, inner_ref, outer_ref, out_ref, slab_base, slab, comb
+    stride, main_ref, own_ref, inner_ref, outer_ref, out_ref, slab_base, base, slab, comb
 ):
     _, planes, rows, lanes = out_ref.shape
-    wide = slab.shape[2]
-    half = slab.shape[1] // 2
+    deep = planes + 2 * HALO
+    wide = slab_base.shape[2]
+    half = slab_base.shape[1] // 2
     part = FIELDS * TILE
     source = iota((lanes, FIELDS * lanes), 0)
     target = iota((lanes, FIELDS * lanes), 1)
@@ -392,18 +399,23 @@
         slab_base[f, half:half + NEAR] = own_ref[at + TILE:at + TILE + NEAR]
         slab_base[f, half + NEAR:half + NEAR + HALO] = jnp.where(upper, outer, inner)
 
-    first_row = lax.rem(iota((2 * half, wide), 1), stride) == 0
-    last_row = lax.rem(iota((2 * half, wide), 1), stride) == stride - 1
-
-    def lane_roll(v, shift):
-        return pltpu.roll(v, shift % wide, axis=1)
-
+    narrow = min(wide, -(-(deep - 1) * stride // lanes) * lanes)
+    kept = NEAR + HALO - 2
+    start = slab_base
     for stage in range(3):
-        u = [(slab_base if stage == 0 else slab)[f] for f in range(FIELDS)]
+        src = slab_base if stage == 0 else slab
+        u = [src[f] for f in range(FIELDS)]
+        tall, width = u[0].shape
+        first_row = lax.rem(iota((tall, width), 1), stride) == 0
+        last_row = lax.rem(iota((tall, width), 1), stride) == stride - 1
+
+        def lane_roll(v, shift, width=width):
+            return pltpu.roll(v, shift % width, axis=1)
+
         q = primitives(u)
         hi = u + [q[2], q[5], q[6], q[7]]
         face = faces(2, [pltpu.roll(v, 1, axis=0) for v in hi], hi)
-        change = [pltpu.roll(v, 2 * half - 1, axis=0) - v for v in face]
+        change = [pltpu.roll(v, tall - 1, axis=0) - v for v in face]
         hi = u + [q[0], q[3], q[6], q[7]]
         face = faces(0, [lane_roll(v, stride) for v in hi], hi)
         change = [c + (lane_roll(v, -stride) - v) for c, v in zip(change, face)]
@@ -415,13 +427,34 @@
             for c, v in zip(change, face)
         ]
         for f in range(FIELDS):
-            sink = slab_base[FIELDS] if f == FIELDS - 1 else None
-            slab[f] = advance(stage, u[f], change[f], slab_base[f], sink)
+            sink = start[FIELDS] if f == FIELDS - 1 else None
+            value = advance(stage, u[f], change[f], start[f], sink)
+            if stage:
+                slab[f] = value
+                continue
+            for group in range(2):
+                slab[f, group * TILE:group * TILE + kept] = value[
+                    group * half + 1:group * half + 1 + kept, 0:narrow
+                ]
+                slab[f, group * TILE + kept:(group + 1) * TILE] = jnp.zeros(
+                    (TILE - kept, narrow), jnp.float32
+                )
+        if stage == 0:
+            for f in range(FIELDS + 1):
+                for group in range(2):
+                    base[f, group * TILE:group * TILE + kept] = slab_base[
+                        f, group * half + 1:group * half + 1 + kept, 0:narrow
+                    ]
+                    base[f, group * TILE + kept:(group + 1) * TILE] = jnp.zeros(
+                        (TILE - kept, narrow), jnp.float32
+                    )
+            start = base
 
     for f in range(FIELDS):
-        comb[f * TILE:f * TILE + HALO] = slab[f, HALO:2 * HALO]
-        first = half + NEAR - HALO
-        comb[f * TILE + HALO:f * TILE + 2 * HALO] = slab[f, first:first + HALO]
+        first = HALO - 1
+        comb[f * TILE:f * TILE + HALO, 0:narrow] = slab[f, first:first + HALO]
+        first = TILE + NEAR - HALO - 1
+        comb[f * TILE + HALO:f * TILE + 2 * HALO, 0:narrow] = slab[f, first:first + HALO]
     whole = comb[0:part]
     for k in range(2):
         piece = whole.astype(jnp.bfloat16).astype(jnp.float32)
@@ -442,6 +475,10 @@
 
 
 def metal_kernel(dims, rows, where, order, *refs):
+    fluid_ref, fluid_hbm, written = refs[-20], refs[-18], refs[-1]
+    refs = (*refs[:-20], refs[-19], *refs[-17:-1])
+    leave = pltpu.make_async_copy(fluid_ref, fluid_hbm, written)
+    leave.start()
     count_blk, count_sub, along, across = dims
     devices = count_blk * count_sub
     pieces = [(refs[k], start) for k, start in where]
@@ -545,6 +582,7 @@
         if step + 1 == ITERS:
             towards = res[pl.ds(mine + 1, along), pl.ds(side, across)] + times(beta, dirn[mine_at])
             out_ref[...] = sol[...] + times(alpha, towards)
+            leave.wait()
             break
 
         def update(x, carry, step=step, alpha=alpha, beta=beta):
@@ -700,24 +738,28 @@
     deep_metal = count_blk * along
     field = (deep_metal, wide, lanes)
     padded = (deep_metal + 2, wide, lanes)
-    metal_next = call(
-        functools.partial(
-            metal_kernel, (count_blk, count_sub, along, across), rows, where, order
-        ),
-        f32(along, across, lanes),
-        pieces,
-        scratch=[
-            (along, across, lanes), padded, padded, field, field, field, field, padded, field,
-            field, field, field, field, (devices * across, lanes), (TILE, devices * rows), (devices * rows, lanes),
-        ],
-    )
     slab = 2 * -(-(NEAR + HALO) // (TILE // 2)) * (TILE // 2)
-    fluid_next = call(
+    narrow = min(wide_lanes, -(-(deep - 1) * stride // lanes) * lanes)
+    fluid = call(
         functools.partial(ends_kernel, stride),
         f32(FIELDS, planes, rows, lanes),
         [planes_next, own_z, inner_got, outer_got],
         scratch=[
-            (FIELDS + 1, slab, wide_lanes), (FIELDS, slab, wide_lanes), (lanes, wide_lanes)
+            (FIELDS + 1, slab, wide_lanes), (FIELDS + 1, 2 * TILE, narrow),
+            (FIELDS, 2 * TILE, narrow), (lanes, wide_lanes),
+        ],
+    )
+    metal_next, fluid_next = call(
+        functools.partial(
+            metal_kernel, (count_blk, count_sub, along, across), rows, where, order
+        ),
+        [f32(along, across, lanes), f32(FIELDS, planes, rows, lanes)],
+        [*pieces, fluid],
+        hbm_out=(1,),
+        scratch=[
+            (along, across, lanes), padded, padded, field, field, field, field, padded, field,
+            field, field, field, field, (devices * across, lanes), (TILE, devices * rows), (devices * rows, lanes),
+            pltpu.SemaphoreType.DMA,
         ],
     )
     return (fluid_next, metal_next)

time: 40.9 us -> 39.6 us (0.968)
  Pallas kernels: 10.8 us -> 9.32 us
    pallas_call x6, Pallas kernels: 10.8 us -> 9.32 us  [call(): pl.pallas_call(body, out_shape=out, in_specs=[pl.BlockSpec(memory_space=p...]
  transfers between devices with their start and end apart: 12 -> 12, of which waited for: 7 -> 7; matrix products, arithmetic and copies ran while one was open for 0% -> 0% of each run, Pallas kernels for 18% -> 14%
where the time goes in v6:
time: 39.6 us; the launch traced here: 39.4 us
  starting transfers between devices  15.2 us (38%)
  waiting for transfers between devices  14.1 us (36%)
  Pallas kernels  9.32 us (24%)
  between operations  0.72 us (2%)
    ppermute x9, waiting for transfers between devices, swap(): return lax.ppermute(value, axis, [(i, i ^ flip) for i in range(count)])  11.9 us
    ppermute x9, starting transfers between devices, swap(): return lax.ppermute(value, axis, [(i, i ^ flip) for i in range(count)])  11.6 us
    pallas_call x6, Pallas kernels, call(): pl.pallas_call(body, out_shape=out, in_specs=[pl.BlockSpec(memory_space=p...  9.32 us
    ppermute x3, starting transfers between devices, outer(): return lax.ppermute(value, axis, pairs)  3.68 us
    ppermute x3, waiting for transfers between devices, outer(): return lax.ppermute(value, axis, pairs)  2.2 us
  transfers between devices with their start and end apart: 12, of which 7 were waited for; matrix products, arithmetic and copies ran while one was open for 0% of the time, Pallas kernels for 14%

profile of v6, /device:TPU:0, one launch (start us, length us, event | category | flops | bytes accessed | tf_op | source)
XLA Modules:
  0.0 39.4 jit_solution(9274662130579219537)
XLA Ops:
  0.6 1.2 %shard_map.95 = (f32[5,4,32,128]{3,2,1,0:T(8,128)S(1)}, f32[120,128]{1,0:T(8,128)S(1)}, f32[840,128]{1,0:T(8,128)S(1)}, f32[480,128]{1,0:T(8,128)S(1)}, f32[360,128]{1,0:T(8,128)S(1)}, /*index=5*/f32[9,128]{1,0:T(8,128)S(1)}) custom-call(f32[4,32,128]{2,1,0:T(8,128)} %rho_hbm.1, f32[3,4,32,128]{3,2,1,0:T(8,128)} %vel_hbm.1, f32[4,32,128]{2,1,0:T(8,128)} %pre_hbm.1, ...), custom_call_target="tpu_custom_call" | custom-call | flops 100000 | bytes 100000 | tf_op jit(solution)/shard_map/pallas_call | solution.py:47
  1.8 3.1 %collective-permute-start.1 = (f32[360,128]{1,0:T(8,128)S(1)}, f32[360,128]{1,0:T(8,128)S(1)}, u32[]{:S(2)}, u32[]{:S(2)}) collective-permute-start(f32[360,128]{1,0:T(8,128)S(1)} %get-tuple-element.16.refs_0_), channel_id=1, source_target_pairs={{0,1},{1,0},{2,3},{3,2},{4,5},{5,4},{6,7},{7,6},{8,9},{9,8},{10,11... | collective-permute-start | bytes 552968 | tf_op jit(solution)/shard_map/ppermute | solution.py:605
  4.9 1.5 %collective-permute-start.2 = (f32[360,128]{1,0:T(8,128)S(1)}, f32[360,128]{1,0:T(8,128)S(1)}, u32[]{:S(2)}, u32[]{:S(2)}) collective-permute-start(f32[360,128]{1,0:T(8,128)S(1)} %get-tuple-element.16.refs_0_), channel_id=1, source_target_pairs={{0,4},{2,6},{4,0},{6,2},{1,5},{3,7},{5,1},{7,3},{8,12},{10,14},{12... | collective-permute-start | bytes 552968 | tf_op jit(solution)/shard_map/ppermute | solution.py:605
  6.4 3.1 %collective-permute-done.1.refs_2_ = f32[360,128]{1,0:T(8,128)S(1)} collective-permute-done((f32[360,128]{1,0:T(8,128)S(1)}, f32[360,128]{1,0:T(8,128)S(1)}, u32[]{:S(2)}, u32[]{:S(2)}) %collective-permute-start.1) | collective-permute-done | bytes 184352 | tf_op jit(solution)/shard_map/ppermute | solution.py:605
  9.5 1.7 %collective-permute-start.3 = (f32[360,128]{1,0:T(8,128)S(1)}, f32[360,128]{1,0:T(8,128)S(1)}, u32[]{:S(2)}, u32[]{:S(2)}) collective-permute-start(f32[360,128]{1,0:T(8,128)S(1)} %collective-permute-done.1.refs_2_), channel_id=1, source_target_pairs={{0,4},{2,6},{4,0},{6,2},{1,5},{3,7},{5,1},{7,3},{8,12},{10,14},{12... | collective-permute-start | bytes 552968 | tf_op jit(solution)/shard_map/ppermute | solution.py:605
  11.2 0.0 collective-permute-done.2.refs_3_
  11.2 4.1 %collective-permute-done.3.refs_4_ = f32[360,128]{1,0:T(8,128)S(1)} collective-permute-done((f32[360,128]{1,0:T(8,128)S(1)}, f32[360,128]{1,0:T(8,128)S(1)}, u32[]{:S(2)}, u32[]{:S(2)}) %collective-permute-start.3) | collective-permute-done | bytes 184352 | tf_op jit(solution)/shard_map/ppermute | solution.py:605
  15.4 0.1 collective-permute-start.4
  15.4 0.5 %collective-permute-start = (f32[840,128]{1,0:T(8,128)S(1)}, f32[840,128]{1,0:T(8,128)S(1)}, u32[]{:S(2)}, u32[]{:S(2)}) collective-permute-start(f32[840,128]{1,0:T(8,128)S(1)} %get-tuple-element.17), channel_id=1, source_target_pairs={{0,2},{2,0},{4,6},{6,4},{1,3},{3,1},{5,7},{7,5},{8,10},{10,8},{12,... | collective-permute-start | bytes 1290248 | tf_op jit(solution)/shard_map/ppermute | solution.py:605
  15.9 1.1 %collective-permute-start.5 = (f32[480,128]{1,0:T(8,128)S(1)}, f32[480,128]{1,0:T(8,128)S(1)}, u32[]{:S(2)}, u32[]{:S(2)}) collective-permute-start(f32[480,128]{1,0:T(8,128)S(1)} %get-tuple-element.19), channel_id=1, source_target_pairs={{0,6},{2,4},{4,2},{6,0},{1,7},{3,5},{5,3},{7,1},{8,14},{10,12},{12... | collective-permute-start | bytes 737288 | tf_op jit(solution)/shard_map/ppermute | solution.py:611
  17.1 0.4 %collective-permute-start.6 = (f32[9,128]{1,0:T(8,128)S(1)}, f32[9,128]{1,0:T(8,128)S(1)}, u32[]{:S(2)}, u32[]{:S(2)}) collective-permute-start(f32[9,128]{1,0:T(8,128)S(1)} %get-tuple-element.21.refs_2_.refs_7_), channel_id=1, source_target_pairs={{0,2},{2,0},{4,6},{6,4},{1,3},{3,1},{5,7},{7,5},{8,10},{10,8},{12,... | collective-permute-start | bytes 13832 | tf_op jit(solution)/shard_map/ppermute | solution.py:605
  17.5 0.8 %collective-permute-done.6.refs_3_.refs_8_ = f32[9,128]{1,0:T(8,128)S(1)} collective-permute-done((f32[9,128]{1,0:T(8,128)S(1)}, f32[9,128]{1,0:T(8,128)S(1)}, u32[]{:S(2)}, u32[]{:S(2)}) %collective-permute-start.6) | collective-permute-done | bytes 4640 | tf_op jit(solution)/shard_map/ppermute | solution.py:605
  18.4 1.6 %collective-permute-start.7 = (f32[138,128]{1,0:T(8,128)S(1)}, f32[138,128]{1,0:T(8,128)S(1)}, u32[]{:S(2)}, u32[]{:S(2)}) collective-permute-start(f32[138,128]{1,0:T(8,128)S(1)} %pad_maximum_fusion.1), channel_id=1, source_target_pairs={{0,1},{1,0},{2,3},{3,2},{4,5},{5,4},{6,7},{7,6},{8,9},{9,8},{10,11... | collective-permute-start | bytes 211976 | tf_op jit(solution)/shard_map/ppermute | solution.py:605
  19.9 3.0 %collective-permute-done.7.refs_0_.refs_1_.refs_4_.refs_3_.refs_9_.refs_10_ = f32[138,128]{1,0:T(8,128)S(1)} collective-permute-done((f32[138,128]{1,0:T(8,128)S(1)}, f32[138,128]{1,0:T(8,128)S(1)}, u32[]{:S(2)}, u32[]{:S(2)}) %collective-permute-start.7) | collective-permute-done | bytes 70688 | tf_op jit(solution)/shard_map/ppermute | solution.py:605
  23.0 0.1 collective-permute-start.9
  23.0 1.1 %collective-permute-start.8 = (f32[30,128]{1,0:T(8,128)S(1)}, f32[30,128]{1,0:T(8,128)S(1)}, u32[]{:S(2)}, u32[]{:S(2)}) collective-permute-start(f32[30,128]{1,0:T(8,128)S(1)} %get-tuple-element.22), channel_id=1, source_target_pairs={{0,2},{2,0},{4,6},{6,4},{1,3},{3,1},{5,7},{7,5},{8,10},{10,8},{12,... | collective-permute-start | bytes 46088 | tf_op jit(solution)/shard_map/ppermute | solution.py:605
  24.1 0.8 %collective-permute-done.8.refs_5_ = f32[30,128]{1,0:T(8,128)S(1)} collective-permute-done((f32[30,128]{1,0:T(8,128)S(1)}, f32[30,128]{1,0:T(8,128)S(1)}, u32[]{:S(2)}, u32[]{:S(2)}) %collective-permute-start.8) | collective-permute-done | bytes 15392 | tf_op jit(solution)/shard_map/ppermute | solution.py:605
  24.9 1.5 %collective-permute-done.9.refs_6_.refs_11_.refs_12_.refs_13_.refs_14_ = f32[66,128]{1,0:T(8,128)S(1)} collective-permute-done((f32[66,128]{1,0:T(8,128)S(1)}, f32[66,128]{1,0:T(8,128)S(1)}, u32[]{:S(2)}, u32[]{:S(2)}) %collective-permute-start.9) | collective-permute-done | bytes 33824 | tf_op jit(solution)/shard_map/ppermute | solution.py:611
  26.5 0.0 collective-permute-done.5.refs_2_
  26.5 0.0 collective-permute-done.refs_1_
  26.5 1.0 %shard_map.97 = (f32[6,10,40,128]{3,2,1,0:T(8,128)S(1)}, f32[96,512]{1,0:T(8,128)S(1)}, f32[24,512]{1,0:T(8,128)S(1)}, f32[24,512]{1,0:T(8,128)S(1)}) custom-call(f32[5,4,32,128]{3,2,1,0:T(8,128)S(1)} %get-tuple-element.18.refs_0_, f32[840,128]{1,0:T(8,128)S(1)} %collective-permute-done.refs_1_, f32[480,128]{1,0:T(8,128)S(1)} %collective-permute-done.5.refs_2_, ...), custom_call_target="tpu_custom_call" | custom-call | flops 100000 | bytes 100000 | tf_op jit(solution)/shard_map/pallas_call | solution.py:47
  27.5 1.6 %collective-permute-start.10 = (f32[24,512]{1,0:T(8,128)S(1)}, f32[24,512]{1,0:T(8,128)S(1)}, u32[]{:S(2)}, u32[]{:S(2)}) collective-permute-start(f32[24,512]{1,0:T(8,128)S(1)} %get-tuple-element.26), channel_id=1, source_target_pairs={{0,8},{8,0},{16,24},{24,16},{1,9},{9,1},{17,25},{25,17},{2,10},{10... | collective-permute-start | bytes 147464 | tf_op jit(solution)/shard_map/ppermute | solution.py:605
  29.1 2.5 %collective-permute-start.11 = (f32[24,512]{1,0:T(8,128)S(1)}, f32[24,512]{1,0:T(8,128)S(1)}, u32[]{:S(2)}, u32[]{:S(2)}) collective-permute-start(f32[24,512]{1,0:T(8,128)S(1)} %get-tuple-element.27), channel_id=1, source_target_pairs={{0,24},{8,16},{16,8},{24,0},{1,25},{9,17},{17,9},{25,1},{2,26},{10... | collective-permute-start | bytes 147464 | tf_op jit(solution)/shard_map/ppermute | solution.py:611
  31.6 2.7 %shard_map.98.main_ref = f32[5,4,32,128]{3,2,1,0:T(8,128)S(1)} custom-call(f32[6,10,40,128]{3,2,1,0:T(8,128)S(1)} %get-tuple-element.24.block_ref), custom_call_target="tpu_custom_call" | custom-call | flops 100000 | bytes 100000 | tf_op jit(solution)/shard_map/pallas_call | solution.py:47
  34.3 0.0 collective-permute-done.10.inner_ref
  34.3 0.7 %collective-permute-done.11.outer_ref = f32[24,512]{1,0:T(8,128)S(1)} collective-permute-done((f32[24,512]{1,0:T(8,128)S(1)}, f32[24,512]{1,0:T(8,128)S(1)}, u32[]{:S(2)}, u32[]{:S(2)}) %collective-permute-start.11) | collective-permute-done | bytes 49184 | tf_op jit(solution)/shard_map/ppermute | solution.py:611
  35.0 1.9 %shard_map.99.refs_6_ = f32[5,4,32,128]{3,2,1,0:T(8,128)S(1)} custom-call(f32[5,4,32,128]{3,2,1,0:T(8,128)S(1)} %shard_map.98.main_ref, f32[96,512]{1,0:T(8,128)S(1)} %get-tuple-element.25.own_ref, f32[24,512]{1,0:T(8,128)S(1)} %collective-permute-done.10.inner_ref, f32[24,512]{1,0:T(8,128)S(1)} %collective-permute-done.11.outer_ref), custom_call_target="tpu_custom_call" | custom-call | flops 100000 | bytes 100000 | tf_op jit(solution)/shard_map/pallas_call | solution.py:47
  36.9 0.0 collective-permute-done.4.refs_5_
  36.9 2.5 %shard_map.100 = (f32[8,8,128]{2,1,0:T(8,128)}, f32[5,4,32,128]{3,2,1,0:T(8,128)}) custom-call(f32[360,128]{1,0:T(8,128)S(1)} %get-tuple-element.16.refs_0_, f32[840,128]{1,0:T(8,128)S(1)} %collective-permute-done.refs_1_, f32[360,128]{1,0:T(8,128)S(1)} %collective-permute-done.1.refs_2_, f32[360,128]{1,0:T(8,128)S(1)} %collective-permute-done.2.refs_3_, ...), custom_call_target="tpu_custom_call" | custom-call | flops 100000 | bytes 100000 | tf_op jit(solution)/shard_map/pallas_call | solution.py:47
  (3 shorter events, 0.1 us)
Async XLA Ops:
  1.8 7.7 %collective-permute-start.1 = (f32[360,128]{1,0:T(8,128)S(1)}, f32[360,128]{1,0:T(8,128)S(1)}, u32[]{:S(2)}, u32[]{:S(2)}) collective-permute-start(f32[360,128]{1,0:T(8,128)S(1)} %get-tuple-element.16.refs_0_), channel_id=1, source_target_pairs={{0,1},{1,0},{2,3},{3,2},{4,5},{5,4},{6,7},{7,6},{8,9},{9,8},{10,11... | collective-permute-start | bytes 552968 | tf_op jit(solution)/shard_map/ppermute | solution.py:605
  4.9 6.4 %collective-permute-start.2 = (f32[360,128]{1,0:T(8,128)S(1)}, f32[360,128]{1,0:T(8,128)S(1)}, u32[]{:S(2)}, u32[]{:S(2)}) collective-permute-start(f32[360,128]{1,0:T(8,128)S(1)} %get-tuple-element.16.refs_0_), channel_id=1, source_target_pairs={{0,4},{2,6},{4,0},{6,2},{1,5},{3,7},{5,1},{7,3},{8,12},{10,14},{12... | collective-permute-start | bytes 552968 | tf_op jit(solution)/shard_map/ppermute | solution.py:605
  9.5 5.8 %collective-permute-start.3 = (f32[360,128]{1,0:T(8,128)S(1)}, f32[360,128]{1,0:T(8,128)S(1)}, u32[]{:S(2)}, u32[]{:S(2)}) collective-permute-start(f32[360,128]{1,0:T(8,128)S(1)} %collective-permute-done.1.refs_2_), channel_id=1, source_target_pairs={{0,4},{2,6},{4,0},{6,2},{1,5},{3,7},{5,1},{7,3},{8,12},{10,14},{12... | collective-permute-start | bytes 552968 | tf_op jit(solution)/shard_map/ppermute | solution.py:605
  15.4 21.6 %collective-permute-start.4 = (f32[1080,128]{1,0:T(8,128)S(1)}, f32[1080,128]{1,0:T(8,128)S(1)}, u32[]{:S(2)}, u32[]{:S(2)}) collective-permute-start(f32[1080,128]{1,0:T(8,128)S(1)} %pad_maximum_fusion), channel_id=1, source_target_pairs={{0,2},{2,0},{4,6},{6,4},{1,3},{3,1},{5,7},{7,5},{8,10},{10,8},{12,... | collective-permute-start | bytes 1658888 | tf_op jit(solution)/shard_map/ppermute | solution.py:605
  15.4 11.0 %collective-permute-start = (f32[840,128]{1,0:T(8,128)S(1)}, f32[840,128]{1,0:T(8,128)S(1)}, u32[]{:S(2)}, u32[]{:S(2)}) collective-permute-start(f32[840,128]{1,0:T(8,128)S(1)} %get-tuple-element.17), channel_id=1, source_target_pairs={{0,2},{2,0},{4,6},{6,4},{1,3},{3,1},{5,7},{7,5},{8,10},{10,8},{12,... | collective-permute-start | bytes 1290248 | tf_op jit(solution)/shard_map/ppermute | solution.py:605
  15.9 10.5 %collective-permute-start.5 = (f32[480,128]{1,0:T(8,128)S(1)}, f32[480,128]{1,0:T(8,128)S(1)}, u32[]{:S(2)}, u32[]{:S(2)}) collective-permute-start(f32[480,128]{1,0:T(8,128)S(1)} %get-tuple-element.19), channel_id=1, source_target_pairs={{0,6},{2,4},{4,2},{6,0},{1,7},{3,5},{5,3},{7,1},{8,14},{10,12},{12... | collective-permute-start | bytes 737288 | tf_op jit(solution)/shard_map/ppermute | solution.py:611
  17.1 1.3 %collective-permute-start.6 = (f32[9,128]{1,0:T(8,128)S(1)}, f32[9,128]{1,0:T(8,128)S(1)}, u32[]{:S(2)}, u32[]{:S(2)}) collective-permute-start(f32[9,128]{1,0:T(8,128)S(1)} %get-tuple-element.21.refs_2_.refs_7_), channel_id=1, source_target_pairs={{0,2},{2,0},{4,6},{6,4},{1,3},{3,1},{5,7},{7,5},{8,10},{10,8},{12,... | collective-permute-start | bytes 13832 | tf_op jit(solution)/shard_map/ppermute | solution.py:605
  18.4 4.6 %collective-permute-start.7 = (f32[138,128]{1,0:T(8,128)S(1)}, f32[138,128]{1,0:T(8,128)S(1)}, u32[]{:S(2)}, u32[]{:S(2)}) collective-permute-start(f32[138,128]{1,0:T(8,128)S(1)} %pad_maximum_fusion.1), channel_id=1, source_target_pairs={{0,1},{1,0},{2,3},{3,2},{4,5},{5,4},{6,7},{7,6},{8,9},{9,8},{10,11... | collective-permute-start | bytes 211976 | tf_op jit(solution)/shard_map/ppermute | solution.py:605
  23.0 3.5 %collective-permute-start.9 = (f32[66,128]{1,0:T(8,128)S(1)}, f32[66,128]{1,0:T(8,128)S(1)}, u32[]{:S(2)}, u32[]{:S(2)}) collective-permute-start(f32[66,128]{1,0:T(8,128)S(1)} %get-tuple-element.23), channel_id=1, source_target_pairs={{0,6},{2,4},{4,2},{6,0},{1,7},{3,5},{5,3},{7,1},{8,14},{10,12},{12... | collective-permute-start | bytes 101384 | tf_op jit(solution)/shard_map/ppermute | solution.py:611
  23.0 1.9 %collective-permute-start.8 = (f32[30,128]{1,0:T(8,128)S(1)}, f32[30,128]{1,0:T(8,128)S(1)}, u32[]{:S(2)}, u32[]{:S(2)}) collective-permute-start(f32[30,128]{1,0:T(8,128)S(1)} %get-tuple-element.22), channel_id=1, source_target_pairs={{0,2},{2,0},{4,6},{6,4},{1,3},{3,1},{5,7},{7,5},{8,10},{10,8},{12,... | collective-permute-start | bytes 46088 | tf_op jit(solution)/shard_map/ppermute | solution.py:605
  27.5 6.8 %collective-permute-start.10 = (f32[24,512]{1,0:T(8,128)S(1)}, f32[24,512]{1,0:T(8,128)S(1)}, u32[]{:S(2)}, u32[]{:S(2)}) collective-permute-start(f32[24,512]{1,0:T(8,128)S(1)} %get-tuple-element.26), channel_id=1, source_target_pairs={{0,8},{8,0},{16,24},{24,16},{1,9},{9,1},{17,25},{25,17},{2,10},{10... | collective-permute-start | bytes 147464 | tf_op jit(solution)/shard_map/ppermute | solution.py:605
  29.1 5.9 %collective-permute-start.11 = (f32[24,512]{1,0:T(8,128)S(1)}, f32[24,512]{1,0:T(8,128)S(1)}, u32[]{:S(2)}, u32[]{:S(2)}) collective-permute-start(f32[24,512]{1,0:T(8,128)S(1)} %get-tuple-element.27), channel_id=1, source_target_pairs={{0,24},{8,16},{16,8},{24,0},{1,25},{9,17},{17,9},{25,1},{2,26},{10... | collective-permute-start | bytes 147464 | tf_op jit(solution)/shard_map/ppermute | solution.py:611

commit v7 on v6

--- a/solution.py
+++ b/solution.py
@@ -196,6 +196,12 @@
         at += count
 
 
+def far_row(f, planes, stride):
+    first = HALO * stride
+    row = (FIELDS + 1) * (HALO - 1) + min(f, FIELDS - 2)
+    return row, first, first + planes * stride if f == FIELDS - 1 else first
+
+
 def assemble_kernel(dims, lo_at, hi_at, wall_at, *refs):
     axes, across = dims
     count_blk, count_sub = axes
@@ -280,16 +286,19 @@
         )
         own_ref[f * 2 * TILE:(f + 1) * 2 * TILE, 0:size] = ends
         low, high = ends[0:HALO], ends[TILE + NEAR - HALO:TILE + NEAR]
-        inner_ref[f * HALO:(f + 1) * HALO, 0:size] = jnp.where(upper, low, high)
-        outer_ref[f * HALO:(f + 1) * HALO, 0:size] = jnp.where(upper, high, low)
-    used = (FIELDS + 1) * HALO
+        at = slice(f * (HALO - 1), (f + 1) * (HALO - 1))
+        inner_ref[at, 0:size] = jnp.where(upper, low[:-1], high[1:])
+        outer_ref[at, 0:size] = jnp.where(upper, high[1:], low[:-1])
+        if f == FIELDS:
+            continue
+        inner, outer = jnp.where(upper, low[-1:], high[:1]), jnp.where(upper, high[:1], low[-1:])
+        for ref, value in ((inner_ref, inner), (outer_ref, outer)):
+            row, first, there = far_row(f, planes, stride)
+            ref[row:row + 1, there:there + planes * stride] = value[
+                :, first:first + planes * stride
+            ]
     if own_ref.shape[1] > size:
         own_ref[:, size:] = jnp.zeros((own_ref.shape[0], own_ref.shape[1] - size), jnp.float32)
-    for ref in (inner_ref, outer_ref):
-        if ref.shape[1] > size:
-            ref[:, size:] = jnp.zeros((ref.shape[0], ref.shape[1] - size), jnp.float32)
-        if ref.shape[0] > used:
-            ref[used:] = jnp.zeros((ref.shape[0] - used, ref.shape[1]), jnp.float32)
 
 
 def primitives(u):
@@ -392,12 +401,22 @@
     slab_base[...] = jnp.zeros(slab_base.shape, jnp.float32)
     upper = parity("grp") == 1
     for f in range(FIELDS + 1):
-        inner, outer = (ref[f * HALO:(f + 1) * HALO] for ref in (inner_ref, outer_ref))
+        at = slice(f * (HALO - 1), (f + 1) * (HALO - 1))
+        inner, outer = inner_ref[at], outer_ref[at]
+        slab_base[f, 1:HALO] = jnp.where(upper, inner, outer)
+        slab_base[f, half + NEAR:half + NEAR + HALO - 1] = jnp.where(upper, outer, inner)
         at = f * 2 * TILE
-        slab_base[f, 0:HALO] = jnp.where(upper, inner, outer)
         slab_base[f, HALO:HALO + NEAR] = own_ref[at:at + NEAR]
         slab_base[f, half:half + NEAR] = own_ref[at + TILE:at + TILE + NEAR]
-        slab_base[f, half + NEAR:half + NEAR + HALO] = jnp.where(upper, outer, inner)
+        if f == FIELDS:
+            continue
+        row, first, there = far_row(f, planes, stride)
+        inner, outer = inner_ref[row:row + 1], outer_ref[row:row + 1]
+        if there != first:
+            inner, outer = (pltpu.roll(v, wide + first - there, axis=1) for v in (inner, outer))
+        slab_base[f, 0:1] = jnp.where(upper, inner, outer)
+        last = half + NEAR + HALO - 1
+        slab_base[f, last:last + 1] = jnp.where(upper, outer, inner)
 
     narrow = min(wide, -(-(deep - 1) * stride // lanes) * lanes)
     kept = NEAR + HALO - 2
@@ -690,7 +709,7 @@
         walls = [lax.all_gather(wall, ("blk", "sub"), axis=0, tiled=True)]
         wall_at = None
     deep, stride = planes + 2 * HALO, rows + TILE
-    ends_rows = up_to_tile((FIELDS + 1) * HALO)
+    ends_rows = up_to_tile((FIELDS + 1) * (HALO - 1) + FIELDS - 1)
     wide_lanes = -(-deep * stride // lanes) * lanes
     block, own_z, inner_z, outer_z = call(
         functools.partial(

time: 39.6 us -> 39.4 us (level)
  transfers between devices with their start and end apart: 12 -> 12, of which waited for: 7 -> 7; matrix products, arithmetic and copies ran while one was open for 0% -> 0% of each run, Pallas kernels for 14% -> 15%
where the time goes in v7:
time: 39.4 us; the launch traced here: 39.3 us
  starting transfers between devices  15.2 us (39%)
  waiting for transfers between devices  13.9 us (35%)
  Pallas kernels  9.4 us (24%)
  between operations  0.71 us (2%)
    ppermute x9, waiting for transfers between devices, swap(): return lax.ppermute(value, axis, [(i, i ^ flip) for i in range(count)])  11.9 us
    ppermute x9, starting transfers between devices, swap(): return lax.ppermute(value, axis, [(i, i ^ flip) for i in range(count)])  11.5 us
    pallas_call x6, Pallas kernels, call(): pl.pallas_call(body, out_shape=out, in_specs=[pl.BlockSpec(memory_space=p...  9.4 us
    ppermute x3, starting transfers between devices, outer(): return lax.ppermute(value, axis, pairs)  3.68 us
    ppermute x3, waiting for transfers between devices, outer(): return lax.ppermute(value, axis, pairs)  2.03 us
  transfers between devices with their start and end apart: 12, of which 7 were waited for; matrix products, arithmetic and copies ran while one was open for 0% of the time, Pallas kernels for 15%

profile of v7, /device:TPU:0, one launch (start us, length us, event | category | flops | bytes accessed | tf_op | source)
XLA Modules:
  0.0 39.3 jit_solution(3631081224941536616)
XLA Ops:
  0.6 1.2 %shard_map.95 = (f32[5,4,32,128]{3,2,1,0:T(8,128)S(1)}, f32[120,128]{1,0:T(8,128)S(1)}, f32[840,128]{1,0:T(8,128)S(1)}, f32[480,128]{1,0:T(8,128)S(1)}, f32[360,128]{1,0:T(8,128)S(1)}, /*index=5*/f32[9,128]{1,0:T(8,128)S(1)}) custom-call(f32[4,32,128]{2,1,0:T(8,128)} %rho_hbm.1, f32[3,4,32,128]{3,2,1,0:T(8,128)} %vel_hbm.1, f32[4,32,128]{2,1,0:T(8,128)} %pre_hbm.1, ...), custom_call_target="tpu_custom_call" | custom-call | flops 100000 | bytes 100000 | tf_op jit(solution)/shard_map/pallas_call | solution.py:47
  1.8 3.1 %collective-permute-start.1 = (f32[360,128]{1,0:T(8,128)S(1)}, f32[360,128]{1,0:T(8,128)S(1)}, u32[]{:S(2)}, u32[]{:S(2)}) collective-permute-start(f32[360,128]{1,0:T(8,128)S(1)} %get-tuple-element.16.refs_0_), channel_id=1, source_target_pairs={{0,1},{1,0},{2,3},{3,2},{4,5},{5,4},{6,7},{7,6},{8,9},{9,8},{10,11... | collective-permute-start | bytes 552968 | tf_op jit(solution)/shard_map/ppermute | solution.py:624
  4.9 1.5 %collective-permute-start.2 = (f32[360,128]{1,0:T(8,128)S(1)}, f32[360,128]{1,0:T(8,128)S(1)}, u32[]{:S(2)}, u32[]{:S(2)}) collective-permute-start(f32[360,128]{1,0:T(8,128)S(1)} %get-tuple-element.16.refs_0_), channel_id=1, source_target_pairs={{0,4},{2,6},{4,0},{6,2},{1,5},{3,7},{5,1},{7,3},{8,12},{10,14},{12... | collective-permute-start | bytes 552968 | tf_op jit(solution)/shard_map/ppermute | solution.py:624
  6.4 3.1 %collective-permute-done.1.refs_2_ = f32[360,128]{1,0:T(8,128)S(1)} collective-permute-done((f32[360,128]{1,0:T(8,128)S(1)}, f32[360,128]{1,0:T(8,128)S(1)}, u32[]{:S(2)}, u32[]{:S(2)}) %collective-permute-start.1) | collective-permute-done | bytes 184352 | tf_op jit(solution)/shard_map/ppermute | solution.py:624
  9.5 1.7 %collective-permute-start.3 = (f32[360,128]{1,0:T(8,128)S(1)}, f32[360,128]{1,0:T(8,128)S(1)}, u32[]{:S(2)}, u32[]{:S(2)}) collective-permute-start(f32[360,128]{1,0:T(8,128)S(1)} %collective-permute-done.1.refs_2_), channel_id=1, source_target_pairs={{0,4},{2,6},{4,0},{6,2},{1,5},{3,7},{5,1},{7,3},{8,12},{10,14},{12... | collective-permute-start | bytes 552968 | tf_op jit(solution)/shard_map/ppermute | solution.py:624
  11.2 0.0 collective-permute-done.2.refs_3_
  11.2 4.1 %collective-permute-done.3.refs_4_ = f32[360,128]{1,0:T(8,128)S(1)} collective-permute-done((f32[360,128]{1,0:T(8,128)S(1)}, f32[360,128]{1,0:T(8,128)S(1)}, u32[]{:S(2)}, u32[]{:S(2)}) %collective-permute-start.3) | collective-permute-done | bytes 184352 | tf_op jit(solution)/shard_map/ppermute | solution.py:624
  15.4 0.1 collective-permute-start.4
  15.4 0.5 %collective-permute-start = (f32[840,128]{1,0:T(8,128)S(1)}, f32[840,128]{1,0:T(8,128)S(1)}, u32[]{:S(2)}, u32[]{:S(2)}) collective-permute-start(f32[840,128]{1,0:T(8,128)S(1)} %get-tuple-element.17), channel_id=1, source_target_pairs={{0,2},{2,0},{4,6},{6,4},{1,3},{3,1},{5,7},{7,5},{8,10},{10,8},{12,... | collective-permute-start | bytes 1290248 | tf_op jit(solution)/shard_map/ppermute | solution.py:624
  15.9 1.1 %collective-permute-start.5 = (f32[480,128]{1,0:T(8,128)S(1)}, f32[480,128]{1,0:T(8,128)S(1)}, u32[]{:S(2)}, u32[]{:S(2)}) collective-permute-start(f32[480,128]{1,0:T(8,128)S(1)} %get-tuple-element.19), channel_id=1, source_target_pairs={{0,6},{2,4},{4,2},{6,0},{1,7},{3,5},{5,3},{7,1},{8,14},{10,12},{12... | collective-permute-start | bytes 737288 | tf_op jit(solution)/shard_map/ppermute | solution.py:630
  17.1 0.4 %collective-permute-start.6 = (f32[9,128]{1,0:T(8,128)S(1)}, f32[9,128]{1,0:T(8,128)S(1)}, u32[]{:S(2)}, u32[]{:S(2)}) collective-permute-start(f32[9,128]{1,0:T(8,128)S(1)} %get-tuple-element.21.refs_2_.refs_7_), channel_id=1, source_target_pairs={{0,2},{2,0},{4,6},{6,4},{1,3},{3,1},{5,7},{7,5},{8,10},{10,8},{12,... | collective-permute-start | bytes 13832 | tf_op jit(solution)/shard_map/ppermute | solution.py:624
  17.5 0.8 %collective-permute-done.6.refs_3_.refs_8_ = f32[9,128]{1,0:T(8,128)S(1)} collective-permute-done((f32[9,128]{1,0:T(8,128)S(1)}, f32[9,128]{1,0:T(8,128)S(1)}, u32[]{:S(2)}, u32[]{:S(2)}) %collective-permute-start.6) | collective-permute-done | bytes 4640 | tf_op jit(solution)/shard_map/ppermute | solution.py:624
  18.4 1.6 %collective-permute-start.7 = (f32[138,128]{1,0:T(8,128)S(1)}, f32[138,128]{1,0:T(8,128)S(1)}, u32[]{:S(2)}, u32[]{:S(2)}) collective-permute-start(f32[138,128]{1,0:T(8,128)S(1)} %pad_maximum_fusion.1), channel_id=1, source_target_pairs={{0,1},{1,0},{2,3},{3,2},{4,5},{5,4},{6,7},{7,6},{8,9},{9,8},{10,11... | collective-permute-start | bytes 211976 | tf_op jit(solution)/shard_map/ppermute | solution.py:624
  19.9 3.0 %collective-permute-done.7.refs_0_.refs_1_.refs_4_.refs_3_.refs_9_.refs_10_ = f32[138,128]{1,0:T(8,128)S(1)} collective-permute-done((f32[138,128]{1,0:T(8,128)S(1)}, f32[138,128]{1,0:T(8,128)S(1)}, u32[]{:S(2)}, u32[]{:S(2)}) %collective-permute-start.7) | collective-permute-done | bytes 70688 | tf_op jit(solution)/shard_map/ppermute | solution.py:624
  23.0 0.1 collective-permute-start.9
  23.0 1.1 %collective-permute-start.8 = (f32[30,128]{1,0:T(8,128)S(1)}, f32[30,128]{1,0:T(8,128)S(1)}, u32[]{:S(2)}, u32[]{:S(2)}) collective-permute-start(f32[30,128]{1,0:T(8,128)S(1)} %get-tuple-element.22), channel_id=1, source_target_pairs={{0,2},{2,0},{4,6},{6,4},{1,3},{3,1},{5,7},{7,5},{8,10},{10,8},{12,... | collective-permute-start | bytes 46088 | tf_op jit(solution)/shard_map/ppermute | solution.py:624
  24.1 0.8 %collective-permute-done.8.refs_5_ = f32[30,128]{1,0:T(8,128)S(1)} collective-permute-done((f32[30,128]{1,0:T(8,128)S(1)}, f32[30,128]{1,0:T(8,128)S(1)}, u32[]{:S(2)}, u32[]{:S(2)}) %collective-permute-start.8) | collective-permute-done | bytes 15392 | tf_op jit(solution)/shard_map/ppermute | solution.py:624
  24.9 1.5 %collective-permute-done.9.refs_6_.refs_11_.refs_12_.refs_13_.refs_14_ = f32[66,128]{1,0:T(8,128)S(1)} collective-permute-done((f32[66,128]{1,0:T(8,128)S(1)}, f32[66,128]{1,0:T(8,128)S(1)}, u32[]{:S(2)}, u32[]{:S(2)}) %collective-permute-start.9) | collective-permute-done | bytes 33824 | tf_op jit(solution)/shard_map/ppermute | solution.py:630
  26.5 0.0 collective-permute-done.5.refs_2_
  26.5 0.0 collective-permute-done.refs_1_
  26.5 1.0 %shard_map.97 = (f32[6,10,40,128]{3,2,1,0:T(8,128)S(1)}, f32[96,512]{1,0:T(8,128)S(1)}, f32[16,512]{1,0:T(8,128)S(1)}, f32[16,512]{1,0:T(8,128)S(1)}) custom-call(f32[5,4,32,128]{3,2,1,0:T(8,128)S(1)} %get-tuple-element.18.refs_0_, f32[840,128]{1,0:T(8,128)S(1)} %collective-permute-done.refs_1_, f32[480,128]{1,0:T(8,128)S(1)} %collective-permute-done.5.refs_2_, ...), custom_call_target="tpu_custom_call" | custom-call | flops 100000 | bytes 100000 | tf_op jit(solution)/shard_map/pallas_call | solution.py:47
  27.5 1.6 %collective-permute-start.10 = (f32[16,512]{1,0:T(8,128)S(1)}, f32[16,512]{1,0:T(8,128)S(1)}, u32[]{:S(2)}, u32[]{:S(2)}) collective-permute-start(f32[16,512]{1,0:T(8,128)S(1)} %get-tuple-element.26), channel_id=1, source_target_pairs={{0,8},{8,0},{16,24},{24,16},{1,9},{9,1},{17,25},{25,17},{2,10},{10... | collective-permute-start | bytes 98312 | tf_op jit(solution)/shard_map/ppermute | solution.py:624
  29.1 2.5 %collective-permute-start.11 = (f32[16,512]{1,0:T(8,128)S(1)}, f32[16,512]{1,0:T(8,128)S(1)}, u32[]{:S(2)}, u32[]{:S(2)}) collective-permute-start(f32[16,512]{1,0:T(8,128)S(1)} %get-tuple-element.27), channel_id=1, source_target_pairs={{0,24},{8,16},{16,8},{24,0},{1,25},{9,17},{17,9},{25,1},{2,26},{10... | collective-permute-start | bytes 98312 | tf_op jit(solution)/shard_map/ppermute | solution.py:630
  31.6 2.7 %shard_map.98.main_ref = f32[5,4,32,128]{3,2,1,0:T(8,128)S(1)} custom-call(f32[6,10,40,128]{3,2,1,0:T(8,128)S(1)} %get-tuple-element.24.block_ref), custom_call_target="tpu_custom_call" | custom-call | flops 100000 | bytes 100000 | tf_op jit(solution)/shard_map/pallas_call | solution.py:47
  34.3 0.0 collective-permute-done.10.inner_ref
  34.3 0.5 %collective-permute-done.11.outer_ref = f32[16,512]{1,0:T(8,128)S(1)} collective-permute-done((f32[16,512]{1,0:T(8,128)S(1)}, f32[16,512]{1,0:T(8,128)S(1)}, u32[]{:S(2)}, u32[]{:S(2)}) %collective-permute-start.11) | collective-permute-done | bytes 32800 | tf_op jit(solution)/shard_map/ppermute | solution.py:630
  34.8 1.9 %shard_map.99.refs_6_ = f32[5,4,32,128]{3,2,1,0:T(8,128)S(1)} custom-call(f32[5,4,32,128]{3,2,1,0:T(8,128)S(1)} %shard_map.98.main_ref, f32[96,512]{1,0:T(8,128)S(1)} %get-tuple-element.25.own_ref, f32[16,512]{1,0:T(8,128)S(1)} %collective-permute-done.10.inner_ref, f32[16,512]{1,0:T(8,128)S(1)} %collective-permute-done.11.outer_ref), custom_call_target="tpu_custom_call" | custom-call | flops 100000 | bytes 100000 | tf_op jit(solution)/shard_map/pallas_call | solution.py:47
  36.8 0.0 collective-permute-done.4.refs_5_
  36.8 2.5 %shard_map.100 = (f32[8,8,128]{2,1,0:T(8,128)}, f32[5,4,32,128]{3,2,1,0:T(8,128)}) custom-call(f32[360,128]{1,0:T(8,128)S(1)} %get-tuple-element.16.refs_0_, f32[840,128]{1,0:T(8,128)S(1)} %collective-permute-done.refs_1_, f32[360,128]{1,0:T(8,128)S(1)} %collective-permute-done.1.refs_2_, f32[360,128]{1,0:T(8,128)S(1)} %collective-permute-done.2.refs_3_, ...), custom_call_target="tpu_custom_call" | custom-call | flops 100000 | bytes 100000 | tf_op jit(solution)/shard_map/pallas_call | solution.py:47
  (3 shorter events, 0.1 us)
Async XLA Ops:
  1.8 7.7 %collective-permute-start.1 = (f32[360,128]{1,0:T(8,128)S(1)}, f32[360,128]{1,0:T(8,128)S(1)}, u32[]{:S(2)}, u32[]{:S(2)}) collective-permute-start(f32[360,128]{1,0:T(8,128)S(1)} %get-tuple-element.16.refs_0_), channel_id=1, source_target_pairs={{0,1},{1,0},{2,3},{3,2},{4,5},{5,4},{6,7},{7,6},{8,9},{9,8},{10,11... | collective-permute-start | bytes 552968 | tf_op jit(solution)/shard_map/ppermute | solution.py:624
  4.9 6.4 %collective-permute-start.2 = (f32[360,128]{1,0:T(8,128)S(1)}, f32[360,128]{1,0:T(8,128)S(1)}, u32[]{:S(2)}, u32[]{:S(2)}) collective-permute-start(f32[360,128]{1,0:T(8,128)S(1)} %get-tuple-element.16.refs_0_), channel_id=1, source_target_pairs={{0,4},{2,6},{4,0},{6,2},{1,5},{3,7},{5,1},{7,3},{8,12},{10,14},{12... | collective-permute-start | bytes 552968 | tf_op jit(solution)/shard_map/ppermute | solution.py:624
  9.5 5.8 %collective-permute-start.3 = (f32[360,128]{1,0:T(8,128)S(1)}, f32[360,128]{1,0:T(8,128)S(1)}, u32[]{:S(2)}, u32[]{:S(2)}) collective-permute-start(f32[360,128]{1,0:T(8,128)S(1)} %collective-permute-done.1.refs_2_), channel_id=1, source_target_pairs={{0,4},{2,6},{4,0},{6,2},{1,5},{3,7},{5,1},{7,3},{8,12},{10,14},{12... | collective-permute-start | bytes 552968 | tf_op jit(solution)/shard_map/ppermute | solution.py:624
  15.4 21.4 %collective-permute-start.4 = (f32[1080,128]{1,0:T(8,128)S(1)}, f32[1080,128]{1,0:T(8,128)S(1)}, u32[]{:S(2)}, u32[]{:S(2)}) collective-permute-start(f32[1080,128]{1,0:T(8,128)S(1)} %pad_maximum_fusion), channel_id=1, source_target_pairs={{0,2},{2,0},{4,6},{6,4},{1,3},{3,1},{5,7},{7,5},{8,10},{10,8},{12,... | collective-permute-start | bytes 1658888 | tf_op jit(solution)/shard_map/ppermute | solution.py:624
  15.4 11.0 %collective-permute-start = (f32[840,128]{1,0:T(8,128)S(1)}, f32[840,128]{1,0:T(8,128)S(1)}, u32[]{:S(2)}, u32[]{:S(2)}) collective-permute-start(f32[840,128]{1,0:T(8,128)S(1)} %get-tuple-element.17), channel_id=1, source_target_pairs={{0,2},{2,0},{4,6},{6,4},{1,3},{3,1},{5,7},{7,5},{8,10},{10,8},{12,... | collective-permute-start | bytes 1290248 | tf_op jit(solution)/shard_map/ppermute | solution.py:624
  15.9 10.5 %collective-permute-start.5 = (f32[480,128]{1,0:T(8,128)S(1)}, f32[480,128]{1,0:T(8,128)S(1)}, u32[]{:S(2)}, u32[]{:S(2)}) collective-permute-start(f32[480,128]{1,0:T(8,128)S(1)} %get-tuple-element.19), channel_id=1, source_target_pairs={{0,6},{2,4},{4,2},{6,0},{1,7},{3,5},{5,3},{7,1},{8,14},{10,12},{12... | collective-permute-start | bytes 737288 | tf_op jit(solution)/shard_map/ppermute | solution.py:630
  17.1 1.3 %collective-permute-start.6 = (f32[9,128]{1,0:T(8,128)S(1)}, f32[9,128]{1,0:T(8,128)S(1)}, u32[]{:S(2)}, u32[]{:S(2)}) collective-permute-start(f32[9,128]{1,0:T(8,128)S(1)} %get-tuple-element.21.refs_2_.refs_7_), channel_id=1, source_target_pairs={{0,2},{2,0},{4,6},{6,4},{1,3},{3,1},{5,7},{7,5},{8,10},{10,8},{12,... | collective-permute-start | bytes 13832 | tf_op jit(solution)/shard_map/ppermute | solution.py:624
  18.4 4.6 %collective-permute-start.7 = (f32[138,128]{1,0:T(8,128)S(1)}, f32[138,128]{1,0:T(8,128)S(1)}, u32[]{:S(2)}, u32[]{:S(2)}) collective-permute-start(f32[138,128]{1,0:T(8,128)S(1)} %pad_maximum_fusion.1), channel_id=1, source_target_pairs={{0,1},{1,0},{2,3},{3,2},{4,5},{5,4},{6,7},{7,6},{8,9},{9,8},{10,11... | collective-permute-start | bytes 211976 | tf_op jit(solution)/shard_map/ppermute | solution.py:624
  23.0 3.5 %collective-permute-start.9 = (f32[66,128]{1,0:T(8,128)S(1)}, f32[66,128]{1,0:T(8,128)S(1)}, u32[]{:S(2)}, u32[]{:S(2)}) collective-permute-start(f32[66,128]{1,0:T(8,128)S(1)} %get-tuple-element.23), channel_id=1, source_target_pairs={{0,6},{2,4},{4,2},{6,0},{1,7},{3,5},{5,3},{7,1},{8,14},{10,12},{12... | collective-permute-start | bytes 101384 | tf_op jit(solution)/shard_map/ppermute | solution.py:630
  23.0 1.9 %collective-permute-start.8 = (f32[30,128]{1,0:T(8,128)S(1)}, f32[30,128]{1,0:T(8,128)S(1)}, u32[]{:S(2)}, u32[]{:S(2)}) collective-permute-start(f32[30,128]{1,0:T(8,128)S(1)} %get-tuple-element.22), channel_id=1, source_target_pairs={{0,2},{2,0},{4,6},{6,4},{1,3},{3,1},{5,7},{7,5},{8,10},{10,8},{12,... | collective-permute-start | bytes 46088 | tf_op jit(solution)/shard_map/ppermute | solution.py:624
  27.5 6.8 %collective-permute-start.10 = (f32[16,512]{1,0:T(8,128)S(1)}, f32[16,512]{1,0:T(8,128)S(1)}, u32[]{:S(2)}, u32[]{:S(2)}) collective-permute-start(f32[16,512]{1,0:T(8,128)S(1)} %get-tuple-element.26), channel_id=1, source_target_pairs={{0,8},{8,0},{16,24},{24,16},{1,9},{9,1},{17,25},{25,17},{2,10},{10... | collective-permute-start | bytes 98312 | tf_op jit(solution)/shard_map/ppermute | solution.py:624
  29.1 5.7 %collective-permute-start.11 = (f32[16,512]{1,0:T(8,128)S(1)}, f32[16,512]{1,0:T(8,128)S(1)}, u32[]{:S(2)}, u32[]{:S(2)}) collective-permute-start(f32[16,512]{1,0:T(8,128)S(1)} %get-tuple-element.27), channel_id=1, source_target_pairs={{0,24},{8,16},{16,8},{24,0},{1,25},{9,17},{17,9},{25,1},{2,26},{10... | collective-permute-start | bytes 98312 | tf_op jit(solution)/shard_map/ppermute | solution.py:630

commit v8 on v7

--- a/solution.py
+++ b/solution.py
@@ -340,7 +340,7 @@
 
 
 def planes_kernel(block_ref, out_ref, now, prim, xface):
-    deep, _, _ = block_ref.shape[1:]
+    deep, stride, lanes = block_ref.shape[1:]
     rows = out_ref.shape[2]
     for stage in range(3):
         src = block_ref if stage == 0 else now
@@ -349,30 +349,38 @@
             for k, value in enumerate(primitives([src[f, x] for f in range(FIELDS)])):
                 prim[k, x] = value
 
-        def cells(x, d, src=src):
-            return [src[f, x] for f in range(FIELDS)] + [
-                prim[d, x], prim[3 + d, x], prim[6, x], prim[7, x]
+        tall = rows if stage == 2 else stride
+
+        def cells(x, d, tall=tall, src=src):
+            return [src[f, x, 0:tall] for f in range(FIELDS)] + [
+                prim[k, x, 0:tall] for k in (d, 3 + d, 6, 7)
             ]
 
         for x in range(low, high + 1):
             new = faces(0, cells(x - 1, 0), cells(x, 0))
             for f in range(FIELDS):
-                xface[x % 2, f] = new[f]
+                xface[x % 2, f, 0:tall] = new[f]
             if x == low:
                 continue
             p = x - 1
-            change = [new[f] - xface[p % 2, f] for f in range(FIELDS)]
-            for d, axis in ((1, 0), (2, 1)):
-                hi = cells(p, d)
-                lo = [pltpu.roll(v, 1, axis=axis) for v in hi]
-                face = faces(d, lo, hi)
-                last = hi[0].shape[axis] - 1
-                change = [c + (pltpu.roll(v, last, axis=axis) - v) for c, v in zip(change, face)]
+            change = [new[f] - xface[p % 2, f, 0:tall] for f in range(FIELDS)]
+            hi = cells(p, 1, stride)
+            face = faces(1, [pltpu.roll(v, 1, axis=0) for v in hi], hi)
+            change = [
+                c + (pltpu.roll(v, stride - 1, axis=0) - v)[0:tall] for c, v in zip(change, face)
+            ]
+            hi = cells(p, 2)
+            face = faces(2, [pltpu.roll(v, 1, axis=1) for v in hi], hi)
+            change = [
+                c + (pltpu.roll(v, lanes - 1, axis=1) - v) for c, v in zip(change, face)
+            ]
             for f in range(FIELDS):
-                sink = block_ref[FIELDS, p] if f == FIELDS - 1 else None
-                value = advance(stage, src[f, p], change[f], block_ref[f, p], sink)
+                sink = block_ref[FIELDS, p, 0:tall] if f == FIELDS - 1 else None
+                value = advance(
+                    stage, src[f, p, 0:tall], change[f], block_ref[f, p, 0:tall], sink
+                )
                 if stage == 2:
-                    out_ref[f, p - HALO] = value[0:rows]
+                    out_ref[f, p - HALO] = value
                 else:
                     now[f, p] = value
 

time: 39.4 us -> 39.4 us (level)
  no operation moved by 1% of the time
where the time goes in v8:
time: 39.4 us; the launch traced here: 39.3 us
  starting transfers between devices  15.2 us (39%)
  waiting for transfers between devices  13.9 us (35%)
  Pallas kernels  9.4 us (24%)
  between operations  0.71 us (2%)
    ppermute x9, waiting for transfers between devices, swap(): return lax.ppermute(value, axis, [(i, i ^ flip) for i in range(count)])  11.9 us
    ppermute x9, starting transfers between devices, swap(): return lax.ppermute(value, axis, [(i, i ^ flip) for i in range(count)])  11.5 us
    pallas_call x6, Pallas kernels, call(): pl.pallas_call(body, out_shape=out, in_specs=[pl.BlockSpec(memory_space=p...  9.4 us
    ppermute x3, starting transfers between devices, outer(): return lax.ppermute(value, axis, pairs)  3.68 us
    ppermute x3, waiting for transfers between devices, outer(): return lax.ppermute(value, axis, pairs)  2.03 us
  transfers between devices with their start and end apart: 12, of which 7 were waited for; matrix products, arithmetic and copies ran while one was open for 0% of the time, Pallas kernels for 15%

profile of v8, /device:TPU:0, one launch (start us, length us, event | category | flops | bytes accessed | tf_op | source)
XLA Modules:
  0.0 39.3 jit_solution(3631081224941536616)
XLA Ops:
  0.6 1.2 %shard_map.95 = (f32[5,4,32,128]{3,2,1,0:T(8,128)S(1)}, f32[120,128]{1,0:T(8,128)S(1)}, f32[840,128]{1,0:T(8,128)S(1)}, f32[480,128]{1,0:T(8,128)S(1)}, f32[360,128]{1,0:T(8,128)S(1)}, /*index=5*/f32[9,128]{1,0:T(8,128)S(1)}) custom-call(f32[4,32,128]{2,1,0:T(8,128)} %rho_hbm.1, f32[3,4,32,128]{3,2,1,0:T(8,128)} %vel_hbm.1, f32[4,32,128]{2,1,0:T(8,128)} %pre_hbm.1, ...), custom_call_target="tpu_custom_call" | custom-call | flops 100000 | bytes 100000 | tf_op jit(solution)/shard_map/pallas_call | solution.py:47
  1.8 3.1 %collective-permute-start.1 = (f32[360,128]{1,0:T(8,128)S(1)}, f32[360,128]{1,0:T(8,128)S(1)}, u32[]{:S(2)}, u32[]{:S(2)}) collective-permute-start(f32[360,128]{1,0:T(8,128)S(1)} %get-tuple-element.16.refs_0_), channel_id=1, source_target_pairs={{0,1},{1,0},{2,3},{3,2},{4,5},{5,4},{6,7},{7,6},{8,9},{9,8},{10,11... | collective-permute-start | bytes 552968 | tf_op jit(solution)/shard_map/ppermute | solution.py:632
  4.9 1.5 %collective-permute-start.2 = (f32[360,128]{1,0:T(8,128)S(1)}, f32[360,128]{1,0:T(8,128)S(1)}, u32[]{:S(2)}, u32[]{:S(2)}) collective-permute-start(f32[360,128]{1,0:T(8,128)S(1)} %get-tuple-element.16.refs_0_), channel_id=1, source_target_pairs={{0,4},{2,6},{4,0},{6,2},{1,5},{3,7},{5,1},{7,3},{8,12},{10,14},{12... | collective-permute-start | bytes 552968 | tf_op jit(solution)/shard_map/ppermute | solution.py:632
  6.4 3.1 %collective-permute-done.1.refs_2_ = f32[360,128]{1,0:T(8,128)S(1)} collective-permute-done((f32[360,128]{1,0:T(8,128)S(1)}, f32[360,128]{1,0:T(8,128)S(1)}, u32[]{:S(2)}, u32[]{:S(2)}) %collective-permute-start.1) | collective-permute-done | bytes 184352 | tf_op jit(solution)/shard_map/ppermute | solution.py:632
  9.5 1.7 %collective-permute-start.3 = (f32[360,128]{1,0:T(8,128)S(1)}, f32[360,128]{1,0:T(8,128)S(1)}, u32[]{:S(2)}, u32[]{:S(2)}) collective-permute-start(f32[360,128]{1,0:T(8,128)S(1)} %collective-permute-done.1.refs_2_), channel_id=1, source_target_pairs={{0,4},{2,6},{4,0},{6,2},{1,5},{3,7},{5,1},{7,3},{8,12},{10,14},{12... | collective-permute-start | bytes 552968 | tf_op jit(solution)/shard_map/ppermute | solution.py:632
  11.2 0.0 collective-permute-done.2.refs_3_
  11.2 4.1 %collective-permute-done.3.refs_4_ = f32[360,128]{1,0:T(8,128)S(1)} collective-permute-done((f32[360,128]{1,0:T(8,128)S(1)}, f32[360,128]{1,0:T(8,128)S(1)}, u32[]{:S(2)}, u32[]{:S(2)}) %collective-permute-start.3) | collective-permute-done | bytes 184352 | tf_op jit(solution)/shard_map/ppermute | solution.py:632
  15.4 0.1 collective-permute-start.4
  15.4 0.5 %collective-permute-start = (f32[840,128]{1,0:T(8,128)S(1)}, f32[840,128]{1,0:T(8,128)S(1)}, u32[]{:S(2)}, u32[]{:S(2)}) collective-permute-start(f32[840,128]{1,0:T(8,128)S(1)} %get-tuple-element.17), channel_id=1, source_target_pairs={{0,2},{2,0},{4,6},{6,4},{1,3},{3,1},{5,7},{7,5},{8,10},{10,8},{12,... | collective-permute-start | bytes 1290248 | tf_op jit(solution)/shard_map/ppermute | solution.py:632
  15.9 1.1 %collective-permute-start.5 = (f32[480,128]{1,0:T(8,128)S(1)}, f32[480,128]{1,0:T(8,128)S(1)}, u32[]{:S(2)}, u32[]{:S(2)}) collective-permute-start(f32[480,128]{1,0:T(8,128)S(1)} %get-tuple-element.19), channel_id=1, source_target_pairs={{0,6},{2,4},{4,2},{6,0},{1,7},{3,5},{5,3},{7,1},{8,14},{10,12},{12... | collective-permute-start | bytes 737288 | tf_op jit(solution)/shard_map/ppermute | solution.py:638
  17.1 0.4 %collective-permute-start.6 = (f32[9,128]{1,0:T(8,128)S(1)}, f32[9,128]{1,0:T(8,128)S(1)}, u32[]{:S(2)}, u32[]{:S(2)}) collective-permute-start(f32[9,128]{1,0:T(8,128)S(1)} %get-tuple-element.21.refs_2_.refs_7_), channel_id=1, source_target_pairs={{0,2},{2,0},{4,6},{6,4},{1,3},{3,1},{5,7},{7,5},{8,10},{10,8},{12,... | collective-permute-start | bytes 13832 | tf_op jit(solution)/shard_map/ppermute | solution.py:632
  17.5 0.8 %collective-permute-done.6.refs_3_.refs_8_ = f32[9,128]{1,0:T(8,128)S(1)} collective-permute-done((f32[9,128]{1,0:T(8,128)S(1)}, f32[9,128]{1,0:T(8,128)S(1)}, u32[]{:S(2)}, u32[]{:S(2)}) %collective-permute-start.6) | collective-permute-done | bytes 4640 | tf_op jit(solution)/shard_map/ppermute | solution.py:632
  18.4 1.6 %collective-permute-start.7 = (f32[138,128]{1,0:T(8,128)S(1)}, f32[138,128]{1,0:T(8,128)S(1)}, u32[]{:S(2)}, u32[]{:S(2)}) collective-permute-start(f32[138,128]{1,0:T(8,128)S(1)} %pad_maximum_fusion.1), channel_id=1, source_target_pairs={{0,1},{1,0},{2,3},{3,2},{4,5},{5,4},{6,7},{7,6},{8,9},{9,8},{10,11... | collective-permute-start | bytes 211976 | tf_op jit(solution)/shard_map/ppermute | solution.py:632
  19.9 3.0 %collective-permute-done.7.refs_0_.refs_1_.refs_4_.refs_3_.refs_9_.refs_10_ = f32[138,128]{1,0:T(8,128)S(1)} collective-permute-done((f32[138,128]{1,0:T(8,128)S(1)}, f32[138,128]{1,0:T(8,128)S(1)}, u32[]{:S(2)}, u32[]{:S(2)}) %collective-permute-start.7) | collective-permute-done | bytes 70688 | tf_op jit(solution)/shard_map/ppermute | solution.py:632
  23.0 0.1 collective-permute-start.9
  23.0 1.1 %collective-permute-start.8 = (f32[30,128]{1,0:T(8,128)S(1)}, f32[30,128]{1,0:T(8,128)S(1)}, u32[]{:S(2)}, u32[]{:S(2)}) collective-permute-start(f32[30,128]{1,0:T(8,128)S(1)} %get-tuple-element.22), channel_id=1, source_target_pairs={{0,2},{2,0},{4,6},{6,4},{1,3},{3,1},{5,7},{7,5},{8,10},{10,8},{12,... | collective-permute-start | bytes 46088 | tf_op jit(solution)/shard_map/ppermute | solution.py:632
  24.1 0.8 %collective-permute-done.8.refs_5_ = f32[30,128]{1,0:T(8,128)S(1)} collective-permute-done((f32[30,128]{1,0:T(8,128)S(1)}, f32[30,128]{1,0:T(8,128)S(1)}, u32[]{:S(2)}, u32[]{:S(2)}) %collective-permute-start.8) | collective-permute-done | bytes 15392 | tf_op jit(solution)/shard_map/ppermute | solution.py:632
  24.9 1.5 %collective-permute-done.9.refs_6_.refs_11_.refs_12_.refs_13_.refs_14_ = f32[66,128]{1,0:T(8,128)S(1)} collective-permute-done((f32[66,128]{1,0:T(8,128)S(1)}, f32[66,128]{1,0:T(8,128)S(1)}, u32[]{:S(2)}, u32[]{:S(2)}) %collective-permute-start.9) | collective-permute-done | bytes 33824 | tf_op jit(solution)/shard_map/ppermute | solution.py:638
  26.5 0.0 collective-permute-done.5.refs_2_
  26.5 0.0 collective-permute-done.refs_1_
  26.5 1.0 %shard_map.97 = (f32[6,10,40,128]{3,2,1,0:T(8,128)S(1)}, f32[96,512]{1,0:T(8,128)S(1)}, f32[16,512]{1,0:T(8,128)S(1)}, f32[16,512]{1,0:T(8,128)S(1)}) custom-call(f32[5,4,32,128]{3,2,1,0:T(8,128)S(1)} %get-tuple-element.18.refs_0_, f32[840,128]{1,0:T(8,128)S(1)} %collective-permute-done.refs_1_, f32[480,128]{1,0:T(8,128)S(1)} %collective-permute-done.5.refs_2_, ...), custom_call_target="tpu_custom_call" | custom-call | flops 100000 | bytes 100000 | tf_op jit(solution)/shard_map/pallas_call | solution.py:47
  27.5 1.6 %collective-permute-start.10 = (f32[16,512]{1,0:T(8,128)S(1)}, f32[16,512]{1,0:T(8,128)S(1)}, u32[]{:S(2)}, u32[]{:S(2)}) collective-permute-start(f32[16,512]{1,0:T(8,128)S(1)} %get-tuple-element.26), channel_id=1, source_target_pairs={{0,8},{8,0},{16,24},{24,16},{1,9},{9,1},{17,25},{25,17},{2,10},{10... | collective-permute-start | bytes 98312 | tf_op jit(solution)/shard_map/ppermute | solution.py:632
  29.1 2.5 %collective-permute-start.11 = (f32[16,512]{1,0:T(8,128)S(1)}, f32[16,512]{1,0:T(8,128)S(1)}, u32[]{:S(2)}, u32[]{:S(2)}) collective-permute-start(f32[16,512]{1,0:T(8,128)S(1)} %get-tuple-element.27), channel_id=1, source_target_pairs={{0,24},{8,16},{16,8},{24,0},{1,25},{9,17},{17,9},{25,1},{2,26},{10... | collective-permute-start | bytes 98312 | tf_op jit(solution)/shard_map/ppermute | solution.py:638
  31.6 2.7 %shard_map.98.main_ref = f32[5,4,32,128]{3,2,1,0:T(8,128)S(1)} custom-call(f32[6,10,40,128]{3,2,1,0:T(8,128)S(1)} %get-tuple-element.24.block_ref), custom_call_target="tpu_custom_call" | custom-call | flops 100000 | bytes 100000 | tf_op jit(solution)/shard_map/pallas_call | solution.py:47
  34.3 0.0 collective-permute-done.10.inner_ref
  34.3 0.5 %collective-permute-done.11.outer_ref = f32[16,512]{1,0:T(8,128)S(1)} collective-permute-done((f32[16,512]{1,0:T(8,128)S(1)}, f32[16,512]{1,0:T(8,128)S(1)}, u32[]{:S(2)}, u32[]{:S(2)}) %collective-permute-start.11) | collective-permute-done | bytes 32800 | tf_op jit(solution)/shard_map/ppermute | solution.py:638
  34.8 1.9 %shard_map.99.refs_6_ = f32[5,4,32,128]{3,2,1,0:T(8,128)S(1)} custom-call(f32[5,4,32,128]{3,2,1,0:T(8,128)S(1)} %shard_map.98.main_ref, f32[96,512]{1,0:T(8,128)S(1)} %get-tuple-element.25.own_ref, f32[16,512]{1,0:T(8,128)S(1)} %collective-permute-done.10.inner_ref, f32[16,512]{1,0:T(8,128)S(1)} %collective-permute-done.11.outer_ref), custom_call_target="tpu_custom_call" | custom-call | flops 100000 | bytes 100000 | tf_op jit(solution)/shard_map/pallas_call | solution.py:47
  36.8 0.0 collective-permute-done.4.refs_5_
  36.8 2.5 %shard_map.100 = (f32[8,8,128]{2,1,0:T(8,128)}, f32[5,4,32,128]{3,2,1,0:T(8,128)}) custom-call(f32[360,128]{1,0:T(8,128)S(1)} %get-tuple-element.16.refs_0_, f32[840,128]{1,0:T(8,128)S(1)} %collective-permute-done.refs_1_, f32[360,128]{1,0:T(8,128)S(1)} %collective-permute-done.1.refs_2_, f32[360,128]{1,0:T(8,128)S(1)} %collective-permute-done.2.refs_3_, ...), custom_call_target="tpu_custom_call" | custom-call | flops 100000 | bytes 100000 | tf_op jit(solution)/shard_map/pallas_call | solution.py:47
  (3 shorter events, 0.1 us)
Async XLA Ops:
  1.8 7.7 %collective-permute-start.1 = (f32[360,128]{1,0:T(8,128)S(1)}, f32[360,128]{1,0:T(8,128)S(1)}, u32[]{:S(2)}, u32[]{:S(2)}) collective-permute-start(f32[360,128]{1,0:T(8,128)S(1)} %get-tuple-element.16.refs_0_), channel_id=1, source_target_pairs={{0,1},{1,0},{2,3},{3,2},{4,5},{5,4},{6,7},{7,6},{8,9},{9,8},{10,11... | collective-permute-start | bytes 552968 | tf_op jit(solution)/shard_map/ppermute | solution.py:632
  4.9 6.4 %collective-permute-start.2 = (f32[360,128]{1,0:T(8,128)S(1)}, f32[360,128]{1,0:T(8,128)S(1)}, u32[]{:S(2)}, u32[]{:S(2)}) collective-permute-start(f32[360,128]{1,0:T(8,128)S(1)} %get-tuple-element.16.refs_0_), channel_id=1, source_target_pairs={{0,4},{2,6},{4,0},{6,2},{1,5},{3,7},{5,1},{7,3},{8,12},{10,14},{12... | collective-permute-start | bytes 552968 | tf_op jit(solution)/shard_map/ppermute | solution.py:632
  9.5 5.8 %collective-permute-start.3 = (f32[360,128]{1,0:T(8,128)S(1)}, f32[360,128]{1,0:T(8,128)S(1)}, u32[]{:S(2)}, u32[]{:S(2)}) collective-permute-start(f32[360,128]{1,0:T(8,128)S(1)} %collective-permute-done.1.refs_2_), channel_id=1, source_target_pairs={{0,4},{2,6},{4,0},{6,2},{1,5},{3,7},{5,1},{7,3},{8,12},{10,14},{12... | collective-permute-start | bytes 552968 | tf_op jit(solution)/shard_map/ppermute | solution.py:632
  15.4 21.4 %collective-permute-start.4 = (f32[1080,128]{1,0:T(8,128)S(1)}, f32[1080,128]{1,0:T(8,128)S(1)}, u32[]{:S(2)}, u32[]{:S(2)}) collective-permute-start(f32[1080,128]{1,0:T(8,128)S(1)} %pad_maximum_fusion), channel_id=1, source_target_pairs={{0,2},{2,0},{4,6},{6,4},{1,3},{3,1},{5,7},{7,5},{8,10},{10,8},{12,... | collective-permute-start | bytes 1658888 | tf_op jit(solution)/shard_map/ppermute | solution.py:632
  15.4 11.0 %collective-permute-start = (f32[840,128]{1,0:T(8,128)S(1)}, f32[840,128]{1,0:T(8,128)S(1)}, u32[]{:S(2)}, u32[]{:S(2)}) collective-permute-start(f32[840,128]{1,0:T(8,128)S(1)} %get-tuple-element.17), channel_id=1, source_target_pairs={{0,2},{2,0},{4,6},{6,4},{1,3},{3,1},{5,7},{7,5},{8,10},{10,8},{12,... | collective-permute-start | bytes 1290248 | tf_op jit(solution)/shard_map/ppermute | solution.py:632
  15.9 10.5 %collective-permute-start.5 = (f32[480,128]{1,0:T(8,128)S(1)}, f32[480,128]{1,0:T(8,128)S(1)}, u32[]{:S(2)}, u32[]{:S(2)}) collective-permute-start(f32[480,128]{1,0:T(8,128)S(1)} %get-tuple-element.19), channel_id=1, source_target_pairs={{0,6},{2,4},{4,2},{6,0},{1,7},{3,5},{5,3},{7,1},{8,14},{10,12},{12... | collective-permute-start | bytes 737288 | tf_op jit(solution)/shard_map/ppermute | solution.py:638
  17.1 1.3 %collective-permute-start.6 = (f32[9,128]{1,0:T(8,128)S(1)}, f32[9,128]{1,0:T(8,128)S(1)}, u32[]{:S(2)}, u32[]{:S(2)}) collective-permute-start(f32[9,128]{1,0:T(8,128)S(1)} %get-tuple-element.21.refs_2_.refs_7_), channel_id=1, source_target_pairs={{0,2},{2,0},{4,6},{6,4},{1,3},{3,1},{5,7},{7,5},{8,10},{10,8},{12,... | collective-permute-start | bytes 13832 | tf_op jit(solution)/shard_map/ppermute | solution.py:632
  18.4 4.6 %collective-permute-start.7 = (f32[138,128]{1,0:T(8,128)S(1)}, f32[138,128]{1,0:T(8,128)S(1)}, u32[]{:S(2)}, u32[]{:S(2)}) collective-permute-start(f32[138,128]{1,0:T(8,128)S(1)} %pad_maximum_fusion.1), channel_id=1, source_target_pairs={{0,1},{1,0},{2,3},{3,2},{4,5},{5,4},{6,7},{7,6},{8,9},{9,8},{10,11... | collective-permute-start | bytes 211976 | tf_op jit(solution)/shard_map/ppermute | solution.py:632
  23.0 3.5 %collective-permute-start.9 = (f32[66,128]{1,0:T(8,128)S(1)}, f32[66,128]{1,0:T(8,128)S(1)}, u32[]{:S(2)}, u32[]{:S(2)}) collective-permute-start(f32[66,128]{1,0:T(8,128)S(1)} %get-tuple-element.23), channel_id=1, source_target_pairs={{0,6},{2,4},{4,2},{6,0},{1,7},{3,5},{5,3},{7,1},{8,14},{10,12},{12... | collective-permute-start | bytes 101384 | tf_op jit(solution)/shard_map/ppermute | solution.py:638
  23.0 1.9 %collective-permute-start.8 = (f32[30,128]{1,0:T(8,128)S(1)}, f32[30,128]{1,0:T(8,128)S(1)}, u32[]{:S(2)}, u32[]{:S(2)}) collective-permute-start(f32[30,128]{1,0:T(8,128)S(1)} %get-tuple-element.22), channel_id=1, source_target_pairs={{0,2},{2,0},{4,6},{6,4},{1,3},{3,1},{5,7},{7,5},{8,10},{10,8},{12,... | collective-permute-start | bytes 46088 | tf_op jit(solution)/shard_map/ppermute | solution.py:632
  27.5 6.8 %collective-permute-start.10 = (f32[16,512]{1,0:T(8,128)S(1)}, f32[16,512]{1,0:T(8,128)S(1)}, u32[]{:S(2)}, u32[]{:S(2)}) collective-permute-start(f32[16,512]{1,0:T(8,128)S(1)} %get-tuple-element.26), channel_id=1, source_target_pairs={{0,8},{8,0},{16,24},{24,16},{1,9},{9,1},{17,25},{25,17},{2,10},{10... | collective-permute-start | bytes 98312 | tf_op jit(solution)/shard_map/ppermute | solution.py:632
  29.1 5.7 %collective-permute-start.11 = (f32[16,512]{1,0:T(8,128)S(1)}, f32[16,512]{1,0:T(8,128)S(1)}, u32[]{:S(2)}, u32[]{:S(2)}) collective-permute-start(f32[16,512]{1,0:T(8,128)S(1)} %get-tuple-element.27), channel_id=1, source_target_pairs={{0,24},{8,16},{16,8},{24,0},{1,25},{9,17},{17,9},{25,1},{2,26},{10... | collective-permute-start | bytes 98312 | tf_op jit(solution)/shard_map/ppermute | solution.py:638
